TPU v7x, 256 devices: a whole 4x4x8 slice. The times are simulated.
256 devices in a mesh: gx: 64 (over z, x, core), gy: 4 (over y).
Axes of the slice: x: 4, y: 4, z: 8, core: 2. Of those that a mesh axis runs over, the one named last changes fastest.
Arguments:
- particles: float32 [4, 7, 393216], P('gy', None, 'gx'), may hold values from -4 to 1024, as said below
- routing: int32 [4, 2, 393216], P('gy', None, 'gx'), may hold values from 0 to 32767, as said below
- tile_list: int32 [4, 2, 409600], P('gy', None, 'gx'), may hold values from 0 to 400, as said below
Outputs:
- particle_rates: float32 [4, 4, 393216], P('gy', None, 'gx')
Inputs may be any that keep to these rules, and one draw needn't show every extreme that they name: `routing`: row 0 is the new owner's gx index (the gy index does not change), row 1 the slot there. Each device's columns are grouped by new owner in increasing order. At most 192 of one device's particles go to one owner, and in every draw some owner receives exactly 192 from every device. No two particles share an owner and a slot. An owner's particles fill whole pencils, each from its first slot, all but one pencil at most. `particles`: positions lie in the cell of the particle's slot: pencil (i, j) covers [i, i + 1) x [j, j + 1) in x and y, cell k of a pencil, k = (slot % 128) // 8, covers [k, k + 1) in z. Masses are positive. `tile_list`: row 0 is a pencil a of the device, index i * 16 + j for local pencil (i, j); row 1 a pencil b, index (i + 2) * 20 + j + 2 for local pencil (i, j) counted from two pencils before the block, or 400 for an unused entry. The used entries come first in no fixed order, and are exactly the pairs in which both a and b hold particles and b is at most two pencils from a along x and along y. Unused entries have a = 0.
All inputs are finite; a program needn't handle non-finite values.
Results may differ from a plain program's by a relative error of at most 0.0003.
Values sent between devices are 32-bit elements; how exact they have to be, the bound alone decides.
A program may use at most 128 MiB of HBM per device.

v0:
```python
import math

import jax
import jax.numpy as jnp
from jax import lax
from jax.sharding import PartitionSpec as P

CX = 16
CY = 16
NZ = 16
CAP = 8


kernel_norm = 21.0 / (16.0 * math.pi)
sound_speed = 2.0
rest_density = 1.0
gravity = 1.0
visc_alpha = 0.5
eta_square = 0.01
pair_block = 64


def extended(block, sides, width):
    for axis, dim in sides:
        count = lax.axis_size(axis)
        forward = [(i, i + 1) for i in range(count - 1)]
        backward = [(target, source) for source, target in forward]
        low = lax.ppermute(
            lax.slice_in_dim(block, block.shape[dim] - width, None, axis=dim), axis, forward
        )
        high = lax.ppermute(lax.slice_in_dim(block, 0, width, axis=dim), axis, backward)
        block = jnp.concatenate([low, block, high], axis=dim)
    return block


def kernel_value(dist_sq):
    radius = jnp.sqrt(dist_sq)
    falloff = jnp.maximum(1.0 - 0.5 * radius, 0.0)
    return kernel_norm * falloff**4 * (1.0 + 2.0 * radius)


def pressure_term(density):
    pressure = (
        sound_speed * sound_speed * rest_density / 7.0 * ((density / rest_density) ** 7 - 1.0)
    )
    return pressure / (density * density)


def selector(left_ids, row_total):
    row_ids = jnp.arange(row_total, dtype=jnp.int32)
    return (row_ids[:, None] == left_ids[None, :]).astype(jnp.float32)


def density_blocks(first_ids, second_ids, pair_count, pos_left, grid_right, density_init):
    row_total = density_init.shape[0]

    def density_advance(block_idx, density):
        start_at = block_idx * pair_block
        left_ids = lax.dynamic_slice_in_dim(first_ids, start_at, pair_block)
        right_ids = lax.dynamic_slice_in_dim(second_ids, start_at, pair_block)
        rows_left = jnp.take(pos_left, left_ids, axis=1)
        rows_right = jnp.take(grid_right, right_ids, axis=1)
        diff_x = rows_left[0][:, :, None] - rows_right[0][:, None, :]
        diff_y = rows_left[1][:, :, None] - rows_right[1][:, None, :]
        diff_z = rows_left[2][:, :, None] - rows_right[2][:, None, :]
        dist_sq = diff_x * diff_x + diff_y * diff_y + diff_z * diff_z
        weight = kernel_value(dist_sq) * rows_right[3][:, None, :]
        block_sums = jnp.sum(weight, axis=2)
        return density + jnp.dot(
            selector(left_ids, row_total),
            block_sums,
            precision=lax.Precision.HIGHEST,
            preferred_element_type=jnp.float32,
        )

    blocks = (pair_count + pair_block - 1) // pair_block
    return lax.fori_loop(0, blocks, density_advance, density_init)


def force_blocks(first_ids, second_ids, pair_count, rows_a, rows_b):
    pencil_total = rows_a.shape[1]

    def force_advance(block_idx, accel):
        start_at = block_idx * pair_block
        left_ids = lax.dynamic_slice_in_dim(first_ids, start_at, pair_block)
        right_ids = lax.dynamic_slice_in_dim(second_ids, start_at, pair_block)
        rows_left = jnp.take(rows_a, left_ids, axis=1)
        rows_right = jnp.take(rows_b, right_ids, axis=1)
        diff_x = rows_left[0][:, :, None] - rows_right[0][:, None, :]
        diff_y = rows_left[1][:, :, None] - rows_right[1][:, None, :]
        diff_z = rows_left[2][:, :, None] - rows_right[2][:, None, :]
        dist_sq = diff_x * diff_x + diff_y * diff_y + diff_z * diff_z
        radius = jnp.sqrt(dist_sq)
        falloff = jnp.maximum(1.0 - 0.5 * radius, 0.0)
        slope_coef = 5.0 * kernel_norm * falloff**3
        vel_dot = (
            (rows_left[3][:, :, None] - rows_right[3][:, None, :]) * diff_x
            + (rows_left[4][:, :, None] - rows_right[4][:, None, :]) * diff_y
            + (rows_left[5][:, :, None] - rows_right[5][:, None, :]) * diff_z
        )
        approach = jnp.minimum(vel_dot, 0.0) / (dist_sq + eta_square)
        viscous = (
            -visc_alpha
            * sound_speed
            * approach
            / (0.5 * (rows_left[6][:, :, None] + rows_right[7][:, None, :]))
        )
        pair_coef = (
            rows_right[6][:, None, :]
            * (rows_left[7][:, :, None] + rows_right[8][:, None, :] + viscous)
            * slope_coef
        )
        pair_sums = jnp.stack(
            [
                jnp.sum(pair_coef * diff_x, axis=2),
                jnp.sum(pair_coef * diff_y, axis=2),
                jnp.sum(pair_coef * diff_z, axis=2),
            ]
        )
        added = jnp.einsum(
            "pb,cbs->cps",
            selector(left_ids, pencil_total),
            pair_sums,
            precision=lax.Precision.HIGHEST,
            preferred_element_type=jnp.float32,
        )
        return accel + added

    blocks = (pair_count + pair_block - 1) // pair_block
    accel_init = jnp.zeros((3, pencil_total, rows_a.shape[2]), jnp.float32)
    return lax.fori_loop(0, blocks, force_advance, accel_init)


def select_pairs(first_ids, second_ids, keep_mask, dummy_id):
    total_len = first_ids.shape[0]
    padded_len = (total_len + pair_block - 1) // pair_block * pair_block
    keep_int = keep_mask.astype(jnp.int32)
    target = jnp.where(keep_mask, jnp.cumsum(keep_int) - 1, padded_len)
    left_ids = jnp.zeros((padded_len,), jnp.int32).at[target].set(first_ids, mode="drop")
    right_ids = jnp.full((padded_len,), dummy_id, jnp.int32).at[target].set(second_ids, mode="drop")
    return (left_ids, right_ids, jnp.sum(keep_int))


def with_dummy(values_in):
    return jnp.concatenate(
        [values_in, jnp.zeros((values_in.shape[0], 1, values_in.shape[2]), values_in.dtype)], axis=1
    )


def guarded(density, masses):
    return jnp.where(masses > 0.0, density, rest_density)


def local(particles, routing, tile_list):
    lanes_total = lax.axis_size("gx")
    row_count = particles.shape[2]
    capacity = 2 * row_count // lanes_total
    pencil_slots = NZ * CAP
    pencils = CX * CY
    slots_all = pencils * pencil_slots
    ext_count = (CX + 4) * (CY + 4)
    fields = particles[0]
    owner_of = routing[0, 0]
    slot_ids = routing[0, 1]
    owner_ids = jnp.arange(lanes_total, dtype=jnp.int32)
    match_owner = owner_of[None, :] == owner_ids[:, None]
    counts = jnp.sum(match_owner.astype(jnp.int32), axis=1)
    starts = jnp.cumsum(counts) - counts
    within = jnp.arange(capacity, dtype=jnp.int32)
    is_valid = within[None, :] < counts[:, None]
    picked = jnp.where(is_valid, starts[:, None] + within[None, :], 0).reshape(-1)
    packed = jnp.concatenate([fields, slot_ids.astype(jnp.float32)[None, :]], axis=0)
    outgoing = jnp.take(packed, picked, axis=1).reshape(8, lanes_total, capacity)
    marker = jnp.where(is_valid, outgoing[7], float(slots_all))
    outgoing = jnp.concatenate([outgoing[:7], marker[None]], axis=0)
    arrived = lax.all_to_all(outgoing, "gx", split_axis=1, concat_axis=1, tiled=True)
    arrived_slot = arrived[7].reshape(-1).astype(jnp.int32)
    own_grid = (
        jnp.zeros((7, slots_all), jnp.float32)
        .at[:, arrived_slot]
        .set(arrived[:7].reshape(7, -1), mode="drop")
    )
    own_grid = own_grid.reshape(7, CX, CY, pencil_slots)
    own_flat = own_grid.reshape(7, pencils, pencil_slots)
    mass_own = own_flat[6]
    pos_own = own_flat[0:3]
    first_list = tile_list[0, 0]
    second_list = tile_list[0, 1]
    is_live = second_list < ext_count
    base_left, base_right, base_count = select_pairs(first_list, second_list, is_live, ext_count)
    local_fields = jnp.concatenate([own_grid[0:3], own_grid[6:7]], axis=0)
    zero_density = jnp.zeros((pencils, pencil_slots), jnp.float32)
    near_first = extended(local_fields, (("gx", 1), ("gy", 2)), 2)
    near_right = with_dummy(near_first.reshape(4, ext_count, pencil_slots))
    density_own = guarded(
        density_blocks(base_left, base_right, base_count, pos_own, near_right, zero_density),
        mass_own,
    )
    second_fields = jnp.concatenate(
        [own_grid[3:6], density_own.reshape(1, CX, CY, pencil_slots)], axis=0
    )
    near_second = extended(second_fields, (("gx", 1), ("gy", 2)), 2)
    pos_near = near_first[0:3]
    mass_near = near_first[3]
    vel_near = near_second[0:3]
    density_near = guarded(near_second[3], mass_near)
    pterm_near = pressure_term(density_near)
    rows_b = jnp.concatenate(
        [pos_near, vel_near, mass_near[None], density_near[None], pterm_near[None]], axis=0
    )
    rows_b = with_dummy(rows_b.reshape(9, ext_count, pencil_slots))
    rows_a = jnp.concatenate(
        [own_flat[0:6], density_own[None], pressure_term(density_own)[None]], axis=0
    )
    accel = force_blocks(base_left, base_right, base_count, rows_a, rows_b)
    accel = accel.at[2].add(-gravity)
    results = jnp.concatenate([accel, density_own[None]], axis=0).reshape(4, slots_all)
    reply = jnp.take(results, jnp.minimum(arrived_slot, slots_all - 1), axis=1).reshape(
        4, lanes_total, capacity
    )
    home_rows = lax.all_to_all(reply, "gx", split_axis=1, concat_axis=1, tiled=True)
    start_of = jnp.sum(jnp.where(match_owner, starts[:, None], 0), axis=0)
    row_index = owner_of * capacity + jnp.arange(row_count, dtype=jnp.int32) - start_of
    answer = jnp.take(home_rows.reshape(4, -1), row_index, axis=1)
    return answer[None]


def solution(mesh):
    in_specs = (P("gy", None, "gx"), P("gy", None, "gx"), P("gy", None, "gx"))
    out_specs = P("gy", None, "gx")
    return jax.shard_map(local, mesh=mesh, in_specs=in_specs, out_specs=out_specs, check_vma=False)
```

profile of v0, /device:TPU:25, one launch (start us, length us, event | category | flops | bytes accessed | tf_op | source)
XLA Modules:
  0.0 854.2 jit_solution(11146458619620292247)
XLA Ops:
  4.0 41.0 %gather_fusion.4 = f32[12288,8]{1,0:T(8,128)} fusion(f32[8,6144]{0,1:T(8,128)S(1)} %copy.71, s32[12288]{0:T(1024)S(1)} %broadcast_clamp_fusion.1), kind=kCustom, calls=%fused_computation.4 | custom fusion | bytes 835584 | tf_op jit(solution)/shard_map/jit(_take)/gather | solution.py:173
  45.0 8.6 %select_bitcast_fusion.4 = f32[8,12288]{0,1:T(8,128)S(1)} fusion(f32[12288,8]{1,0:T(8,128)} %gather_fusion.4, pred[12288]{0:T(1024)(128)(4,1)S(1)} %compare_and_fusion.5), kind=kLoop, calls=%fused_computation.74 | loop fusion | flops 98304 | bytes 798720 | tf_op jit(solution)/shard_map/jit(_take)/select_n | solution.py:173
  56.2 3.4 slice_reduce_fusion.1
  59.9 5.0 copy.72
  65.8 12.2 %all-to-all-start = ((f32[8,64,192]{2,0,1:T(8,128)}), f32[8,64,192]{2,0,1:T(8,128)S(1)}, u32[]{:S(2)}, u32[]{:S(2)}) async-start(f32[8,64,192]{2,0,1:T(8,128)} %pad_maximum_fusion.3), calls=%async_computation | async-start | bytes 1048576 | tf_op jit(solution)/shard_map/all_to_all | solution.py:176
  80.6 24.5 %scatter_custom_fusion.2 = s32[6400]{0:T(1024)} fusion(s32[6400]{0:T(1024)S(1)} %fusion.35, s32[6400]{0:T(1024)S(1)} %get-tuple-element.133, s32[]{:T(128)} %constant.210.clone.1), kind=kCustom, calls=%fused_computation.140 | custom fusion | bytes 25604 | tf_op jit(solution)/shard_map/scatter | solution.py:139
  105.1 24.5 %scatter_custom_fusion = s32[6400]{0:T(1024)} fusion(s32[6400]{0:T(1024)S(1)} %fusion.35, s32[6400]{0:T(1024)S(1)} %get-tuple-element.135, s32[]{:T(128)} %constant.220.clone.1), kind=kCustom, calls=%fused_computation.142 | custom fusion | bytes 25604 | tf_op jit(solution)/shard_map/scatter | solution.py:140
  130.3 4.0 copy.76
  134.4 37.5 %scatter_custom_fusion.1 = f32[7,32768]{0,1:T(8,128)} fusion(s32[12288]{0:T(1024)S(1)} %bitcast.254, f32[12288,7]{1,0:T(8,128)} %copy.76, f32[]{:T(128)} %constant.219.clone.1), kind=kCustom, calls=%fused_computation.71 | custom fusion | bytes 918016 | tf_op jit(solution)/shard_map/scatter | solution.py:181
  171.8 25.8 %fusion.46 = (f32[3,32768]{0,1:T(8,128)}, f32[3,32768]{0,1:T(8,128)}) fusion(f32[7,32768]{0,1:T(8,128)} %scatter_custom_fusion.1), kind=kLoop, calls=%fused_computation.150 | loop fusion | bytes 1572864 | tf_op jit(solution)/shard_map/slice | solution.py:200
  198.2 9.0 %slice_reduce_fusion = f32[32768]{0:T(1024)S(1)} fusion(f32[7,32768]{0,1:T(8,128)S(1)} %copy-done), kind=kLoop, calls=%fused_computation.70 | loop fusion | bytes 262144 | tf_op jit(solution)/shard_map/slice | solution.py:185
  207.2 10.0 %copy.77 = f32[3,16,16,128]{3,0,2,1:T(4,128)S(1)} copy(f32[3,16,16,128]{0,3,2,1:T(8,128)} %bitcast.192) | data formatting | bytes 786432 | tf_op jit(solution)/shard_map/slice | solution.py:191
  222.9 11.2 %compare_reduce_fusion = pred[32768]{0:T(1024)(128)(4,1)S(1)} fusion(f32[7,32768]{0,1:T(8,128)} %scatter_custom_fusion.1), kind=kLoop, calls=%fused_computation.69 | loop fusion | flops 32768 | bytes 163840 | tf_op jit(solution)/shard_map/gt | solution.py:151
  237.9 9.4 %copy.79 = f32[3,256,128]{2,0,1:T(4,128)S(1)} copy(f32[3,256,128]{0,2,1:T(8,128)} %bitcast.193) | data formatting | bytes 786432 | tf_op jit(solution)/shard_map/while | solution.py:77
  247.3 10.0 %copy.80 = f32[3,16,16,128]{3,0,2,1:T(4,128)S(1)} copy(f32[3,16,16,128]{0,3,2,1:T(8,128)} %bitcast.194) | data formatting | bytes 786432 | tf_op jit(solution)/shard_map/slice | solution.py:200
  257.8 8.3 while.21
  260.5 5.4 multiply_reduce_fusion.2
  268.2 3.6 collective-permute-start.4
  271.9 9.4 %copy.82 = f32[6,256,128]{2,0,1:T(8,128)S(1)} copy(f32[6,256,128]{0,2,1:T(8,128)} %bitcast.191) | data formatting | bytes 1572864 | tf_op jit(solution)/shard_map/slice | solution.py:213
  281.4 93.3 %collective-permute-start.7 = (f32[4,20,2,128]{3,0,2,1:T(4,128)S(1)}, f32[4,20,2,128]{3,0,2,1:T(4,128)S(1)}, u32[]{:S(2)}, u32[]{:S(2)}) collective-permute-start(f32[4,20,2,128]{3,0,2,1:T(4,128)S(1)} %get-tuple-element.208), channel_id=1, source_target_pairs={{1,0},{2,1},{3,2},{5,4},{6,5},{7,6},{9,8},{10,9},{11,10},{13,12},{... | collective-permute-start | bytes 245768 | tf_op jit(solution)/shard_map/ppermute | solution.py:31
  377.6 3.6 collective-permute-done.6
  384.2 8.5 concatenate.71
  394.6 21.1 %while.22 = (s32[]{:T(128)}, f32[3,256,128]{1,2,0:T(8,128)S(1)}, s32[]{:T(128)}, s32[6400]{0:T(1024)}, f32[9,401,128]{2,0,1:T(8,128)}, /*index=5*/s32[6400]{0:T(...) while((s32[]{:T(128)}, f32[3,256,128]{1,2,0:T(8,128)S(1)}, ...), condition=%wide.region_16.17_spmd, body=%wide.region_12.16_spmd.sunk | while | flops 116673472 | bytes 4893863 | solution.py:131
  400.5 14.7 %fusion.65 = (f32[64,128]{1,0:T(8,128)S(1)}, f32[64,128]{1,0:T(8,128)S(1)}, f32[64,128]{1,0:T(8,128)S(1)}) fusion(f32[64,128]{1,0:T(8,128)S(1)} %bitcast.220, f32[64,128]{1,0:T(8,128)S(1)} %bitcast.229, f32[64,128]{1,0:T(8,128)S(1)} %bitcast.215, f32[64,128]{1,0:T(8,128)S(1)} %bitcast.224, f32[64,128]{1,0:T(8,128)S(1)} %bitcast.216, ...), kind=kLoop, calls=%fused_computation.42.clone.1 | loop fusion | flops 40869888 | bytes 655360 | tf_op jit(solution)/shard_map/while/body/reduce_sum | solution.py:115
  416.4 8.6 %copy.86 = f32[4,32768]{0,1:T(8,128)} copy(f32[4,32768]{1,0:T(4,128)S(1)} %pad_maximum_fusion.4) | data formatting | bytes 1048576 | tf_op jit(solution)/shard_map/concatenate | solution.py:217
  425.0 46.8 %gather_fusion.5 = f32[12288,4]{1,0:T(8,128)} fusion(f32[4,32768]{0,1:T(8,128)} %copy.86, s32[12288]{0:T(1024)S(1)} %broadcast_clamp_fusion), kind=kCustom, calls=%fused_computation.5 | custom fusion | bytes 442368 | tf_op jit(solution)/shard_map/jit(_take)/gather | solution.py:218
  471.8 4.9 copy.87
  477.5 329.4 %all-to-all-start.1 = ((f32[4,64,192]{2,0,1:T(4,128)}), f32[4,64,192]{2,0,1:T(4,128)S(1)}, u32[]{:S(2)}, u32[]{:S(2)}) async-start(f32[4,64,192]{2,0,1:T(4,128)} %broadcast_select_fusion), calls=%async_computation.1 | async-start | bytes 524288 | tf_op jit(solution)/shard_map/all_to_all | solution.py:221
  806.9 13.0 %all-to-all-done.1 = f32[4,64,192]{2,0,1:T(4,128)S(1)} async-done(((f32[4,64,192]{2,0,1:T(4,128)}), f32[4,64,192]{2,0,1:T(4,128)S(1)}, u32[]{:S(2)}, u32[]{:S(2)}) %all-to-all-start.1) | async-done | bytes 196640 | tf_op jit(solution)/shard_map/all_to_all | solution.py:221
  820.0 4.1 copy.88
  824.0 23.7 %gather_fusion.6 = f32[6144,4]{1,0:T(8,128)} fusion(f32[4,12288]{0,1:T(8,128)} %bitcast.198, s32[6144]{0:T(1024)S(1)} %broadcast_clamp_fusion.2), kind=kCustom, calls=%fused_computation.6 | custom fusion | bytes 221184 | tf_op jit(solution)/shard_map/jit(_take)/gather | solution.py:224
  847.7 4.7 bitcast_select_fusion
  (106 shorter events, 42.9 us)
Async XLA Ops:
  53.6 2.7 copy-start.1
  59.9 18.1 %copy-start.3 = (s32[1,2,6400]{2,1,0:T(2,128)S(1)}, s32[1,2,6400]{2,1,0:T(2,128)}, u32[]{:S(2)}) copy-start(s32[1,2,6400]{2,1,0:T(2,128)} %param.11) | copy-start | bytes 153604
  59.9 69.7 %copy-start.4 = (s32[1,2,6144]{2,1,0:T(2,128)S(1)}, s32[1,2,6144]{2,1,0:T(2,128)}, u32[]{:S(2)}) copy-start(s32[1,2,6144]{2,1,0:T(2,128)} %param.10) | copy-start | bytes 147460
  65.8 63.8 %all-to-all-start = ((f32[8,64,192]{2,0,1:T(8,128)}), f32[8,64,192]{2,0,1:T(8,128)S(1)}, u32[]{:S(2)}, u32[]{:S(2)}) async-start(f32[8,64,192]{2,0,1:T(8,128)} %pad_maximum_fusion.3), calls=%async_computation | async-start | bytes 1048576 | tf_op jit(solution)/shard_map/all_to_all | solution.py:176
  171.8 26.4 %copy-start = (f32[7,32768]{0,1:T(8,128)S(1)}, f32[7,32768]{0,1:T(8,128)}, u32[]{:S(2)}) copy-start(f32[7,32768]{0,1:T(8,128)} %scatter_custom_fusion.1) | copy-start | bytes 2752516
  217.3 16.8 %collective-permute-start.1 = (f32[4,2,16,128]{3,0,2,1:T(4,128)S(1)}, f32[4,2,16,128]{3,0,2,1:T(4,128)S(1)}, u32[]{:S(2)}, u32[]{:S(2)}) collective-permute-start(f32[4,2,16,128]{3,0,2,1:T(4,128)S(1)} %get-tuple-element.214), channel_id=1, source_target_pairs={{4,0},{8,4},{12,8},{16,12},{20,16},{24,20},{28,24},{32,28},{36,32}... | collective-permute-start | bytes 196616 | tf_op jit(solution)/shard_map/ppermute | solution.py:31
  219.7 14.5 %collective-permute-start = (f32[4,2,16,128]{3,0,2,1:T(4,128)S(1)}, f32[4,2,16,128]{3,0,2,1:T(4,128)S(1)}, u32[]{:S(2)}, u32[]{:S(2)}) collective-permute-start(f32[4,2,16,128]{3,0,2,1:T(4,128)S(1)} %get-tuple-element.213), channel_id=1, source_target_pairs={{0,4},{4,8},{8,12},{12,16},{16,20},{20,24},{24,28},{28,32},{32,36}... | collective-permute-start | bytes 196616 | tf_op jit(solution)/shard_map/ppermute | solution.py:28
  234.2 23.1 %collective-permute-start.3 = (f32[4,20,2,128]{3,0,2,1:T(4,128)S(1)}, f32[4,20,2,128]{3,0,2,1:T(4,128)S(1)}, u32[]{:S(2)}, u32[]{:S(2)}) collective-permute-start(f32[4,20,2,128]{3,0,2,1:T(4,128)S(1)} %get-tuple-element.210), channel_id=1, source_target_pairs={{1,0},{2,1},{3,2},{5,4},{6,5},{7,6},{9,8},{10,9},{11,10},{13,12},{... | collective-permute-start | bytes 245768 | tf_op jit(solution)/shard_map/ppermute | solution.py:31
  236.6 20.7 %collective-permute-start.2 = (f32[4,20,2,128]{3,0,2,1:T(4,128)S(1)}, f32[4,20,2,128]{3,0,2,1:T(4,128)S(1)}, u32[]{:S(2)}, u32[]{:S(2)}) collective-permute-start(f32[4,20,2,128]{3,0,2,1:T(4,128)S(1)} %get-tuple-element.209), channel_id=1, source_target_pairs={{0,1},{1,2},{2,3},{4,5},{5,6},{6,7},{8,9},{9,10},{10,11},{12,13},{... | collective-permute-start | bytes 245768 | tf_op jit(solution)/shard_map/ppermute | solution.py:28
  247.3 10.5 %copy-start.5 = (s32[6400]{0:T(1024)S(1)}, s32[6400]{0:T(1024)}, u32[]{:S(2)}) copy-start(s32[6400]{0:T(1024)} %scatter_custom_fusion.2) | copy-start | bytes 76804
  257.7 124.8 %copy-start.2 = (f32[4,20,20,128]{3,0,2,1:T(4,128)}, f32[4,20,20,128]{3,0,2,1:T(4,128)S(1)}, u32[]{:S(2)}) copy-start(f32[4,20,20,128]{3,0,2,1:T(4,128)S(1)} %pad_maximum_fusion.1) | copy-start | bytes 2457604
  266.3 15.0 %collective-permute-start.5 = (f32[4,2,16,128]{3,0,2,1:T(4,128)S(1)}, f32[4,2,16,128]{3,0,2,1:T(4,128)S(1)}, u32[]{:S(2)}, u32[]{:S(2)}) collective-permute-start(f32[4,2,16,128]{3,0,2,1:T(4,128)S(1)} %get-tuple-element.212), channel_id=1, source_target_pairs={{4,0},{8,4},{12,8},{16,12},{20,16},{24,20},{28,24},{32,28},{36,32}... | collective-permute-start | bytes 196616 | tf_op jit(solution)/shard_map/ppermute | solution.py:31
  268.2 13.1 %collective-permute-start.4 = (f32[4,2,16,128]{3,0,2,1:T(4,128)S(1)}, f32[4,2,16,128]{3,0,2,1:T(4,128)S(1)}, u32[]{:S(2)}, u32[]{:S(2)}) collective-permute-start(f32[4,2,16,128]{3,0,2,1:T(4,128)S(1)} %get-tuple-element.211), channel_id=1, source_target_pairs={{0,4},{4,8},{8,12},{12,16},{16,20},{20,24},{24,28},{28,32},{32,36}... | collective-permute-start | bytes 196616 | tf_op jit(solution)/shard_map/ppermute | solution.py:28
  281.4 96.2 %collective-permute-start.7 = (f32[4,20,2,128]{3,0,2,1:T(4,128)S(1)}, f32[4,20,2,128]{3,0,2,1:T(4,128)S(1)}, u32[]{:S(2)}, u32[]{:S(2)}) collective-permute-start(f32[4,20,2,128]{3,0,2,1:T(4,128)S(1)} %get-tuple-element.208), channel_id=1, source_target_pairs={{1,0},{2,1},{3,2},{5,4},{6,5},{7,6},{9,8},{10,9},{11,10},{13,12},{... | collective-permute-start | bytes 245768 | tf_op jit(solution)/shard_map/ppermute | solution.py:31
  374.8 6.5 collective-permute-start.6
  477.5 342.5 %all-to-all-start.1 = ((f32[4,64,192]{2,0,1:T(4,128)}), f32[4,64,192]{2,0,1:T(4,128)S(1)}, u32[]{:S(2)}, u32[]{:S(2)}) async-start(f32[4,64,192]{2,0,1:T(4,128)} %broadcast_select_fusion), calls=%async_computation.1 | async-start | bytes 524288 | tf_op jit(solution)/shard_map/all_to_all | solution.py:221
where the time goes:
time: 858 us; the launch traced here: 854 us
  starting transfers between devices  451 us (53%)
  local copies, waits for them, and re-layouts  327 us (38%)
  other arithmetic  57.3 us (7%)
  waiting for transfers between devices  16.7 us (2%)
    all_to_all x1, starting transfers between devices, local(): lax.all_to_all(reply, 'gx', split_axis=1, concat_axis=1, tiled=True)  329 us
    ppermute x4, starting transfers between devices, extended(): lax.ppermute(lax.slice_in_dim(block, 0, width, axis=dim), axis, backward)  100 us
    gather x2, local copies, waits for them, and re-layouts, local(): jnp.take(results, jnp.minimum(arrived_slot, slots_all - 1), axis=1)  51.7 us
    gather x1, local copies, waits for them, and re-layouts, local(): jnp.take(packed, picked, axis=1).reshape(8, lanes_total, capacity)  41 us
    scatter x1, local copies, waits for them, and re-layouts, local(): own_grid = jnp.zeros((7, slots_all), jnp.float32).at[:, arrived_slot].set...  37.5 us
    slice x2, local copies, waits for them, and re-layouts, local(): own_grid[3:6]  35.8 us
    scatter x1, local copies, waits for them, and re-layouts, select_pairs(): jnp.zeros((padded_len,), jnp.int32).at[target].set(first_ids, mode='drop')  24.5 us
    scatter x1, local copies, waits for them, and re-layouts, select_pairs(): jnp.full((padded_len,), dummy_id, jnp.int32).at[target]  24.5 us
  transfers between devices with their start and end apart: 10, of which 2 were waited for; matrix products, arithmetic and copies ran while one was open for 11% of the time, Pallas kernels for 0%

commit v1 on v0

v1 whole, which is shorter than its diff:
```python
import math

import jax
import jax.numpy as jnp
from jax import lax
from jax.experimental import pallas as pl
from jax.experimental.pallas import tpu as pltpu
from jax.sharding import PartitionSpec as P

CX = 16
CY = 16
NZ = 16
CAP = 8


kernel_norm = 21.0 / (16.0 * math.pi)
sound_speed = 2.0
rest_density = 1.0
gravity = 1.0
visc_alpha = 0.5
eta_square = 0.01
pair_block = 64


def extended(block, sides, width):
    for axis, dim in sides:
        count = lax.axis_size(axis)
        forward = [(i, i + 1) for i in range(count - 1)]
        backward = [(target, source) for source, target in forward]
        low = lax.ppermute(
            lax.slice_in_dim(block, block.shape[dim] - width, None, axis=dim), axis, forward
        )
        high = lax.ppermute(lax.slice_in_dim(block, 0, width, axis=dim), axis, backward)
        block = jnp.concatenate([low, block, high], axis=dim)
    return block


def kernel_value(dist_sq):
    radius = jnp.sqrt(dist_sq)
    falloff = jnp.maximum(1.0 - 0.5 * radius, 0.0)
    return kernel_norm * falloff**4 * (1.0 + 2.0 * radius)


def pressure_term(density):
    pressure = (
        sound_speed * sound_speed * rest_density / 7.0 * ((density / rest_density) ** 7 - 1.0)
    )
    return pressure / (density * density)


def expand_cells(fields, pencil_count):
    depth = fields.shape[0]
    cells = fields.reshape(depth, pencil_count, NZ, CAP).transpose(1, 0, 3, 2)
    wide = jnp.broadcast_to(cells[..., None], cells.shape + (CAP,))
    wide = wide.reshape(pencil_count, depth, CAP, NZ * CAP)
    dummy = jnp.zeros((1, depth, CAP, NZ * CAP), jnp.float32)
    return jnp.concatenate([wide, dummy], axis=0)


def shifted(rows, step):
    shift = (-CAP * step) % (NZ * CAP)
    if shift == 0:
        return rows
    return pltpu.roll(rows, shift, 1)


def density_kernel(first_ref, second_ref, count_ref, own_ref, near_ref, out_ref):
    out_ref[...] = jnp.zeros(out_ref.shape, jnp.float32)

    def body(p, carry):
        a = first_ref[p]
        b = second_ref[p]
        xi = own_ref[a, 0:1, :]
        yi = own_ref[a, 1:2, :]
        zi = own_ref[a, 2:3, :]
        xj = near_ref[b, 0]
        yj = near_ref[b, 1]
        zj = near_ref[b, 2]
        mj = near_ref[b, 3]
        total = jnp.zeros((CAP, NZ * CAP), jnp.float32)
        for step in range(-2, 3):
            dx = xi - shifted(xj, step)
            dy = yi - shifted(yj, step)
            dz = zi - shifted(zj, step)
            dist_sq = dx * dx + dy * dy + dz * dz
            radius = jnp.sqrt(dist_sq)
            falloff = jnp.maximum(1.0 - 0.5 * radius, 0.0)
            sq = falloff * falloff
            weight = kernel_norm * (sq * sq) * (1.0 + 2.0 * radius)
            total = total + weight * shifted(mj, step)
        out_ref[a] = out_ref[a] + total
        return carry

    lax.fori_loop(0, count_ref[0], body, 0)


def force_kernel(first_ref, second_ref, count_ref, own_ref, near_ref, out_ref):
    out_ref[...] = jnp.zeros(out_ref.shape, jnp.float32)

    def body(p, carry):
        a = first_ref[p]
        b = second_ref[p]
        left = [own_ref[a, k : k + 1, :] for k in range(8)]
        right = [near_ref[b, k] for k in range(9)]
        acc_x = jnp.zeros((CAP, NZ * CAP), jnp.float32)
        acc_y = acc_x
        acc_z = acc_x
        for step in range(-2, 3):
            xj, yj, zj, uj, vj, wj, mj, rj, pj = [shifted(r, step) for r in right]
            dx = left[0] - xj
            dy = left[1] - yj
            dz = left[2] - zj
            dist_sq = dx * dx + dy * dy + dz * dz
            radius = jnp.sqrt(dist_sq)
            falloff = jnp.maximum(1.0 - 0.5 * radius, 0.0)
            slope_coef = 5.0 * kernel_norm * (falloff * falloff * falloff)
            vel_dot = (left[3] - uj) * dx + (left[4] - vj) * dy + (left[5] - wj) * dz
            viscous = (-visc_alpha * sound_speed) * jnp.minimum(vel_dot, 0.0) / (
                (dist_sq + eta_square) * (0.5 * (left[6] + rj))
            )
            pair_coef = mj * (left[7] + pj + viscous) * slope_coef
            acc_x = acc_x + pair_coef * dx
            acc_y = acc_y + pair_coef * dy
            acc_z = acc_z + pair_coef * dz
        out_ref[a, 0] = out_ref[a, 0] + acc_x
        out_ref[a, 1] = out_ref[a, 1] + acc_y
        out_ref[a, 2] = out_ref[a, 2] + acc_z
        return carry

    lax.fori_loop(0, count_ref[0], body, 0)


def pair_pass(kernel, first_ids, second_ids, pair_count, own_rows, near_rows, out_depth):
    pencils = own_rows.shape[0]
    if out_depth == 1:
        out_shape = (pencils, CAP, NZ * CAP)
    else:
        out_shape = (pencils, out_depth, CAP, NZ * CAP)
    vmem = pl.BlockSpec(memory_space=pltpu.VMEM)
    return pl.pallas_call(
        kernel,
        out_shape=jax.ShapeDtypeStruct(out_shape, jnp.float32),
        grid_spec=pltpu.PrefetchScalarGridSpec(
            num_scalar_prefetch=3,
            grid=(1,),
            in_specs=[vmem, vmem],
            out_specs=vmem,
        ),
    )(first_ids, second_ids, pair_count.reshape(1), own_rows, near_rows)


def with_dummy(values_in):
    return jnp.concatenate(
        [values_in, jnp.zeros((values_in.shape[0], 1, values_in.shape[2]), values_in.dtype)], axis=1
    )


def guarded(density, masses):
    return jnp.where(masses > 0.0, density, rest_density)


def local(particles, routing, tile_list):
    lanes_total = lax.axis_size("gx")
    row_count = particles.shape[2]
    capacity = 2 * row_count // lanes_total
    pencil_slots = NZ * CAP
    pencils = CX * CY
    slots_all = pencils * pencil_slots
    ext_count = (CX + 4) * (CY + 4)
    fields = particles[0]
    owner_of = routing[0, 0]
    slot_ids = routing[0, 1]
    owner_ids = jnp.arange(lanes_total, dtype=jnp.int32)
    match_owner = owner_of[None, :] == owner_ids[:, None]
    counts = jnp.sum(match_owner.astype(jnp.int32), axis=1)
    starts = jnp.cumsum(counts) - counts
    within = jnp.arange(capacity, dtype=jnp.int32)
    is_valid = within[None, :] < counts[:, None]
    picked = jnp.where(is_valid, starts[:, None] + within[None, :], 0).reshape(-1)
    packed = jnp.concatenate([fields, slot_ids.astype(jnp.float32)[None, :]], axis=0)
    outgoing = jnp.take(packed, picked, axis=1).reshape(8, lanes_total, capacity)
    marker = jnp.where(is_valid, outgoing[7], float(slots_all))
    outgoing = jnp.concatenate([outgoing[:7], marker[None]], axis=0)
    arrived = lax.all_to_all(outgoing, "gx", split_axis=1, concat_axis=1, tiled=True)
    arrived_slot = arrived[7].reshape(-1).astype(jnp.int32)
    own_grid = (
        jnp.zeros((7, slots_all), jnp.float32)
        .at[:, arrived_slot]
        .set(arrived[:7].reshape(7, -1), mode="drop")
    )
    own_grid = own_grid.reshape(7, CX, CY, pencil_slots)
    own_flat = own_grid.reshape(7, pencils, pencil_slots)
    mass_own = own_flat[6]
    pos_own = own_flat[0:3]
    first_list = tile_list[0, 0]
    second_list = tile_list[0, 1]
    pair_count = jnp.sum((second_list < ext_count).astype(jnp.int32))
    local_fields = jnp.concatenate([own_grid[0:3], own_grid[6:7]], axis=0)
    near_first = extended(local_fields, (("gx", 1), ("gy", 2)), 2)
    own_pos = jnp.concatenate(
        [pos_own, jnp.zeros((5, pencils, pencil_slots), jnp.float32)], axis=0
    ).transpose(1, 0, 2)
    near_rows = expand_cells(near_first.reshape(4, ext_count, pencil_slots), ext_count)
    density_sums = pair_pass(
        density_kernel, first_list, second_list, pair_count, own_pos, near_rows, 1
    )
    density_own = guarded(jnp.sum(density_sums, axis=1), mass_own)
    second_fields = jnp.concatenate(
        [own_grid[3:6], density_own.reshape(1, CX, CY, pencil_slots)], axis=0
    )
    near_second = extended(second_fields, (("gx", 1), ("gy", 2)), 2)
    pos_near = near_first[0:3]
    mass_near = near_first[3]
    vel_near = near_second[0:3]
    density_near = guarded(near_second[3], mass_near)
    pterm_near = pressure_term(density_near)
    rows_b = jnp.concatenate(
        [pos_near, vel_near, mass_near[None], density_near[None], pterm_near[None]], axis=0
    )
    rows_b = expand_cells(rows_b.reshape(9, ext_count, pencil_slots), ext_count)
    rows_a = jnp.concatenate(
        [own_flat[0:6], density_own[None], pressure_term(density_own)[None]], axis=0
    ).transpose(1, 0, 2)
    accel = pair_pass(force_kernel, first_list, second_list, pair_count, rows_a, rows_b, 3)
    accel = jnp.sum(accel, axis=2).transpose(1, 0, 2)
    accel = accel.at[2].add(-gravity)
    results = jnp.concatenate([accel, density_own[None]], axis=0).reshape(4, slots_all)
    reply = jnp.take(results, jnp.minimum(arrived_slot, slots_all - 1), axis=1).reshape(
        4, lanes_total, capacity
    )
    home_rows = lax.all_to_all(reply, "gx", split_axis=1, concat_axis=1, tiled=True)
    start_of = jnp.sum(jnp.where(match_owner, starts[:, None], 0), axis=0)
    row_index = owner_of * capacity + jnp.arange(row_count, dtype=jnp.int32) - start_of
    answer = jnp.take(home_rows.reshape(4, -1), row_index, axis=1)
    return answer[None]


def solution(mesh):
    in_specs = (P("gy", None, "gx"), P("gy", None, "gx"), P("gy", None, "gx"))
    out_specs = P("gy", None, "gx")
    return jax.shard_map(local, mesh=mesh, in_specs=in_specs, out_specs=out_specs, check_vma=False)
```

time: 858 us -> 706 us (0.82)
  the two profiles are of different devices: /device:TPU:25 before, /device:TPU:1 now
where the time goes in v1:
time: 706 us; the launch traced here: 696 us
  local copies, waits for them, and re-layouts  357 us (51%)
  Pallas kernels  165 us (23%)
  starting transfers between devices  78.8 us (11%)
  other arithmetic  64.8 us (9%)
  waiting for transfers between devices  29.9 us (4%)
    pallas_call x2, Pallas kernels, pair_pass(): pl.pallas_call(kernel, out_shape=jax.ShapeDtypeStruct(out_shape, jnp.floa...  165 us
    gather x2, local copies, waits for them, and re-layouts, local(): jnp.take(results, jnp.minimum(arrived_slot, slots_all - 1), axis=1)  51.7 us
    all_to_all x1, starting transfers between devices, local(): lax.all_to_all(reply, 'gx', split_axis=1, concat_axis=1, tiled=True)  42.7 us
    gather x1, local copies, waits for them, and re-layouts, local(): jnp.take(packed, picked, axis=1).reshape(8, lanes_total, capacity)  41 us
    reshape x4, local copies, waits for them, and re-layouts, expand_cells(): wide = wide.reshape(pencil_count, depth, CAP, NZ * CAP)  41 us
    scatter x1, local copies, waits for them, and re-layouts, local(): own_grid = jnp.zeros((7, slots_all), jnp.float32).at[:, arrived_slot].set...  37.9 us
    gather x1, local copies, waits for them, and re-layouts, local(): answer = jnp.take(home_rows.reshape(4, -1), row_index, axis=1)  23.7 us
    slice x2, local copies, waits for them, and re-layouts, local(): own_grid[3:6]  22.2 us
  transfers between devices with their start and end apart: 10, of which 4 were waited for; matrix products, arithmetic and copies ran while one was open for 9% of the time, Pallas kernels for 0%

profile of v1, /device:TPU:1, one launch (start us, length us, event | category | flops | bytes accessed | tf_op | source)
XLA Modules:
  0.0 696.1 jit_solution(2954893319601488009)
XLA Ops:
  4.0 41.0 %gather_fusion = f32[12288,8]{1,0:T(8,128)} fusion(f32[8,6144]{0,1:T(8,128)S(1)} %copy.213, s32[12288]{0:T(1024)S(1)} %broadcast_clamp_fusion.1), kind=kCustom, calls=%fused_computation | custom fusion | bytes 835584 | tf_op jit(solution)/shard_map/jit(_take)/gather | solution.py:181
  45.0 8.6 %select_bitcast_fusion = f32[8,12288]{0,1:T(8,128)S(1)} fusion(f32[12288,8]{1,0:T(8,128)} %gather_fusion, pred[12288]{0:T(1024)(128)(4,1)S(1)} %compare_and_fusion.1), kind=kLoop, calls=%fused_computation.12 | loop fusion | flops 98304 | bytes 798720 | tf_op jit(solution)/shard_map/jit(_take)/select_n | solution.py:181
  59.9 5.0 copy.214
  65.8 13.0 %all-to-all-start = ((f32[8,64,192]{2,0,1:T(8,128)}), f32[8,64,192]{2,0,1:T(8,128)S(1)}, u32[]{:S(2)}, u32[]{:S(2)}) async-start(f32[8,64,192]{2,0,1:T(8,128)} %pad_maximum_fusion.3), calls=%async_computation | async-start | bytes 1048576 | tf_op jit(solution)/shard_map/all_to_all | solution.py:184
  81.2 15.3 %all-to-all-done = f32[8,64,192]{2,0,1:T(8,128)S(1)} async-done(((f32[8,64,192]{2,0,1:T(8,128)}), f32[8,64,192]{2,0,1:T(8,128)S(1)}, u32[]{:S(2)}, u32[]{:S(2)}) %all-to-all-start) | async-done | bytes 393248 | tf_op jit(solution)/shard_map/all_to_all | solution.py:184
  101.2 37.9 %scatter_custom_fusion = f32[7,32768]{0,1:T(8,128)} fusion(s32[12288]{0:T(1024)S(1)} %bitcast.103, f32[12288,7]{1,0:T(8,128)} %copy.218, f32[]{:T(128)} %constant.99.clone.1), kind=kCustom, calls=%fused_computation.9 | custom fusion | bytes 918016 | tf_op jit(solution)/shard_map/scatter | solution.py:189
  139.1 12.7 %slice_reduce_fusion = f32[32768]{0:T(1024)S(1)} fusion(f32[7,32768]{0,1:T(8,128)} %scatter_custom_fusion), kind=kLoop, calls=%fused_computation.5 | loop fusion | bytes 262144 | tf_op jit(solution)/shard_map/slice | solution.py:193
  151.8 10.0 %fusion.8 = (pred[32768]{0:T(1024)(128)(4,1)S(1)}, pred[1,32768]{0,1:T(8,128)(4,1)}) fusion(f32[7,32768]{0,1:T(8,128)S(1)} %copy-done), kind=kLoop, calls=%fused_computation.80 | loop fusion | flops 32768 | bytes 196608 | tf_op jit(solution)/shard_map/gt | solution.py:159
  161.8 12.2 %fusion.9 = (f32[3,32768]{0,1:T(8,128)}, f32[3,32768]{0,1:T(8,128)}) fusion(f32[7,32768]{0,1:T(8,128)S(1)} %copy-done), kind=kLoop, calls=%fused_computation.81 | loop fusion | bytes 1572864 | tf_op jit(solution)/shard_map/slice | solution.py:209
  174.0 10.0 %copy.222 = f32[3,16,16,128]{3,2,1,0:T(8,128)S(1)} copy(f32[3,16,16,128]{0,3,2,1:T(8,128)} %bitcast.76) | data formatting | bytes 786432 | tf_op jit(solution)/shard_map/slice | solution.py:198
  189.3 9.4 %copy.231 = f32[6,256,128]{2,0,1:T(8,128)S(1)} copy(f32[6,256,128]{0,2,1:T(8,128)} %bitcast.75) | data formatting | bytes 1572864 | tf_op jit(solution)/shard_map/slice | solution.py:222
  198.8 10.0 %copy.233 = f32[3,16,16,128]{3,2,1,0:T(8,128)S(1)} copy(f32[3,16,16,128]{0,3,2,1:T(8,128)} %bitcast.79) | data formatting | bytes 786432 | tf_op jit(solution)/shard_map/slice | solution.py:209
  208.8 9.4 %copy.221 = f32[3,256,128]{2,0,1:T(4,128)S(1)} copy(f32[3,256,128]{0,2,1:T(8,128)} %bitcast.77) | data formatting | bytes 786432 | tf_op jit(solution)/shard_map/slice | solution.py:194
  229.6 5.1 reshape_reshape.2
  240.8 9.9 %copy.229 = f32[400,4,8,128]{3,2,1,0:T(8,128)} copy(f32[400,4,8,128]{0,3,2,1:T(8,128)} %broadcast_bitcast_fusion.1) | data formatting | bytes 13107200 | tf_op jit(solution)/shard_map/reshape | solution.py:55
  250.8 6.4 concatenate.64.near_ref
  257.1 77.3 %shard_map.37 = f32[256,8,128]{2,1,0:T(8,128)} custom-call(s32[6400]{0:T(1024)} %get-tuple-element.18.first_ref, s32[6400]{0:T(1024)} %copy-done.2, s32[1]{0:T(128)} %bitcast.7.count_ref, f32[256,8,128]{2,1,0:T(8,128)} %pad_bitcast_fusion.own_ref, f32[401,4,8,128]{3,2,1,0:T(8,128)} %concatenate.64.near_ref), custom_call_target="tpu_custom_call" | custom-call | tf_op jit(solution)/shard_map/pallas_call | solution.py:140
  341.5 8.2 %copy.246 = f32[1,32768]{0,1:T(8,128)} copy(f32[1,32768]{1,0:T(1,128)S(1)} %bitcast.92) | data formatting | bytes 262144 | tf_op jit(solution)/shard_map/reduce_sum | solution.py:207
  350.1 12.4 %broadcast_select_fusion = f32[1,32768]{0,1:T(8,128)} fusion(pred[1,32768]{0,1:T(8,128)(4,1)} %get-tuple-element.24, f32[1,32768]{0,1:T(8,128)} %copy.246), kind=kLoop, calls=%fused_computation.8 | loop fusion | flops 32768 | bytes 294912 | tf_op jit(solution)/shard_map/jit(_where)/select_n | solution.py:159
  372.1 5.7 collective-permute-start.6
  396.3 8.9 %broadcast_bitcast_fusion = f32[400,9,8,128]{0,3,2,1:T(8,128)} fusion(f32[400,9,8,16]{0,3,2,1:T(8,128)S(1)} %copy.242), kind=kLoop, calls=%fused_computation.7 | loop fusion | bytes 16588800 | tf_op jit(solution)/shard_map/reshape | solution.py:55
  405.2 17.9 %copy.243 = f32[400,9,8,128]{3,2,1,0:T(8,128)} copy(f32[400,9,8,128]{0,3,2,1:T(8,128)} %broadcast_bitcast_fusion) | data formatting | bytes 29491200 | tf_op jit(solution)/shard_map/reshape | solution.py:55
  423.1 11.4 %concatenate.75.near_ref = f32[401,9,8,128]{3,2,1,0:T(8,128)} pad(f32[400,9,8,128]{3,2,1,0:T(8,128)} %copy.243, f32[]{:T(128)} %constant.99.clone.1), padding=0_1x0_0x0_0x0_0 | pad | bytes 29528068 | tf_op jit(solution)/shard_map/concatenate | solution.py:57
  434.5 87.5 %shard_map.38 = f32[256,3,8,128]{3,2,1,0:T(8,128)} custom-call(s32[6400]{0:T(1024)} %get-tuple-element.18.first_ref, s32[6400]{0:T(1024)} %copy-done.2, s32[1]{0:T(128)} %bitcast.7.count_ref, f32[256,8,128]{2,1,0:T(8,128)} %maximum_bitcast_fusion.own_ref, f32[401,9,8,128]{3,2,1,0:T(8,128)} %concatenate.75.near_ref), custom_call_target="tpu_custom_call" | custom-call | tf_op jit(solution)/shard_map/pallas_call | solution.py:140
  527.9 8.3 %copy.245 = f32[3,256,128]{0,2,1:T(8,128)} copy(f32[3,256,128]{2,0,1:T(4,128)S(1)} %scatter-add.4) | data formatting | bytes 786432 | tf_op jit(solution)/shard_map/scatter-add | solution.py:226
  536.1 17.3 %pad_maximum_fusion = f32[4,32768]{0,1:T(8,128)} fusion(f32[1,32768]{0,1:T(8,128)} %broadcast_select_fusion, f32[3,32768]{0,1:T(8,128)} %bitcast.78), kind=kLoop, calls=%fused_computation.4 | loop fusion | flops 131072 | bytes 1048576 | tf_op jit(solution)/shard_map/concatenate | solution.py:227
  553.4 46.8 %gather_fusion.1 = f32[12288,4]{1,0:T(8,128)} fusion(f32[4,32768]{0,1:T(8,128)} %pad_maximum_fusion, s32[12288]{0:T(1024)S(1)} %broadcast_clamp_fusion), kind=kCustom, calls=%fused_computation.1 | custom fusion | bytes 442368 | tf_op jit(solution)/shard_map/jit(_take)/gather | solution.py:228
  600.2 4.9 copy.247
  606.0 42.7 %all-to-all-start.1 = ((f32[4,64,192]{2,0,1:T(4,128)}), f32[4,64,192]{2,0,1:T(4,128)S(1)}, u32[]{:S(2)}, u32[]{:S(2)}) async-start(f32[4,64,192]{2,0,1:T(4,128)} %broadcast_select_fusion.1), calls=%async_computation.1 | async-start | bytes 524288 | tf_op jit(solution)/shard_map/all_to_all | solution.py:231
  648.7 13.0 %all-to-all-done.1 = f32[4,64,192]{2,0,1:T(4,128)S(1)} async-done(((f32[4,64,192]{2,0,1:T(4,128)}), f32[4,64,192]{2,0,1:T(4,128)S(1)}, u32[]{:S(2)}, u32[]{:S(2)}) %all-to-all-start.1) | async-done | bytes 196640 | tf_op jit(solution)/shard_map/all_to_all | solution.py:231
  665.8 23.7 %gather_fusion.2 = f32[6144,4]{1,0:T(8,128)} fusion(f32[4,12288]{0,1:T(8,128)} %bitcast.81, s32[6144]{0:T(1024)S(1)} %broadcast_clamp_fusion.2), kind=kCustom, calls=%fused_computation.2 | custom fusion | bytes 221184 | tf_op jit(solution)/shard_map/jit(_take)/gather | solution.py:234
  689.5 4.7 bitcast_select_fusion
  (118 shorter events, 89.0 us)
Async XLA Ops:
  0.9 77.9 %copy-start.3 = (s32[1,1,6144]{2,1,0:T(1,128)}, s32[1,1,6144]{2,1,0:T(1,128)S(1)}, u32[]{:S(2)}) copy-start(s32[1,1,6144]{2,1,0:T(1,128)S(1)} %get-tuple-element.38) | copy-start | bytes 73732
  53.6 2.7 copy-start.1
  56.2 22.9 %copy-start.9 = (s32[1,2,6400]{2,1,0:T(2,128)S(1)}, s32[1,2,6400]{2,1,0:T(2,128)}, u32[]{:S(2)}) copy-start(s32[1,2,6400]{2,1,0:T(2,128)} %param.7) | copy-start | bytes 153604
  59.7 20.8 %copy-start.7 = (s32[1,2,6144]{2,1,0:T(2,128)S(1)}, s32[1,2,6144]{2,1,0:T(2,128)}, u32[]{:S(2)}) copy-start(s32[1,2,6144]{2,1,0:T(2,128)} %param.6) | copy-start | bytes 147460
  65.8 30.7 %all-to-all-start = ((f32[8,64,192]{2,0,1:T(8,128)}), f32[8,64,192]{2,0,1:T(8,128)S(1)}, u32[]{:S(2)}, u32[]{:S(2)}) async-start(f32[8,64,192]{2,0,1:T(8,128)} %pad_maximum_fusion.3), calls=%async_computation | async-start | bytes 1048576 | tf_op jit(solution)/shard_map/all_to_all | solution.py:184
  79.1 60.0 %copy-start.5 = (s32[6144]{0:T(1024)}, s32[6144]{0:T(1024)S(1)}, u32[]{:S(2)}) copy-start(s32[6144]{0:T(1024)S(1)} %select_reduce_fusion) | copy-start | bytes 73732
  79.9 59.2 %copy-start.2 = (s32[6400]{0:T(1024)}, s32[6400]{0:T(1024)S(1)}, u32[]{:S(2)}) copy-start(s32[6400]{0:T(1024)S(1)} %get-tuple-element.17.second_ref) | copy-start | bytes 76804
  139.1 12.7 %copy-start = (f32[7,32768]{0,1:T(8,128)S(1)}, f32[7,32768]{0,1:T(8,128)}, u32[]{:S(2)}) copy-start(f32[7,32768]{0,1:T(8,128)} %scatter_custom_fusion) | copy-start | bytes 2752516
  184.0 34.3 %collective-permute-start = (f32[4,2,16,128]{3,2,1,0:T(8,128)S(1)}, f32[4,2,16,128]{3,2,1,0:T(8,128)S(1)}, u32[]{:S(2)}, u32[]{:S(2)}) collective-permute-start(f32[4,2,16,128]{3,2,1,0:T(8,128)S(1)} %get-tuple-element.34), channel_id=1, source_target_pairs={{0,4},{4,8},{8,12},{12,16},{16,20},{20,24},{24,28},{28,32},{32,36}... | collective-permute-start | bytes 196616 | tf_op jit(solution)/shard_map/ppermute | solution.py:30
  187.4 30.9 %collective-permute-start.1 = (f32[4,2,16,128]{3,2,1,0:T(8,128)S(1)}, f32[4,2,16,128]{3,2,1,0:T(8,128)S(1)}, u32[]{:S(2)}, u32[]{:S(2)}) collective-permute-start(f32[4,2,16,128]{3,2,1,0:T(8,128)S(1)} %get-tuple-element.35), channel_id=1, source_target_pairs={{4,0},{8,4},{12,8},{16,12},{20,16},{24,20},{28,24},{32,28},{36,32}... | collective-permute-start | bytes 196616 | tf_op jit(solution)/shard_map/ppermute | solution.py:33
  218.4 6.4 collective-permute-start.3
  219.7 5.5 collective-permute-start.2
  336.0 34.8 %collective-permute-start.4 = (f32[4,2,16,128]{3,2,1,0:T(8,128)S(1)}, f32[4,2,16,128]{3,2,1,0:T(8,128)S(1)}, u32[]{:S(2)}, u32[]{:S(2)}) collective-permute-start(f32[4,2,16,128]{3,2,1,0:T(8,128)S(1)} %get-tuple-element.32), channel_id=1, source_target_pairs={{0,4},{4,8},{8,12},{12,16},{16,20},{20,24},{24,28},{28,32},{32,36}... | collective-permute-start | bytes 196616 | tf_op jit(solution)/shard_map/ppermute | solution.py:30
  339.6 31.1 %collective-permute-start.5 = (f32[4,2,16,128]{3,2,1,0:T(8,128)S(1)}, f32[4,2,16,128]{3,2,1,0:T(8,128)S(1)}, u32[]{:S(2)}, u32[]{:S(2)}) collective-permute-start(f32[4,2,16,128]{3,2,1,0:T(8,128)S(1)} %get-tuple-element.33), channel_id=1, source_target_pairs={{4,0},{8,4},{12,8},{16,12},{20,16},{24,20},{28,24},{32,28},{36,32}... | collective-permute-start | bytes 196616 | tf_op jit(solution)/shard_map/ppermute | solution.py:33
  370.8 7.9 %collective-permute-start.7 = (f32[4,20,2,128]{3,0,2,1:T(4,128)S(1)}, f32[4,20,2,128]{3,0,2,1:T(4,128)S(1)}, u32[]{:S(2)}, u32[]{:S(2)}) collective-permute-start(f32[4,20,2,128]{3,0,2,1:T(4,128)S(1)} %copy.259), channel_id=1, source_target_pairs={{1,0},{2,1},{3,2},{5,4},{6,5},{7,6},{9,8},{10,9},{11,10},{13,12},{... | collective-permute-start | bytes 245768 | tf_op jit(solution)/shard_map/ppermute | solution.py:33
  372.1 7.8 %collective-permute-start.6 = (f32[4,20,2,128]{3,0,2,1:T(4,128)S(1)}, f32[4,20,2,128]{3,0,2,1:T(4,128)S(1)}, u32[]{:S(2)}, u32[]{:S(2)}) collective-permute-start(f32[4,20,2,128]{3,0,2,1:T(4,128)S(1)} %copy.258), channel_id=1, source_target_pairs={{0,1},{1,2},{2,3},{4,5},{5,6},{6,7},{8,9},{9,10},{10,11},{12,13},{... | collective-permute-start | bytes 245768 | tf_op jit(solution)/shard_map/ppermute | solution.py:30
  553.4 95.2 %copy-start.8 = (s32[6144,1]{0,1:T(1,128)S(1)}, s32[6144,1]{0,1:T(1,128)}, u32[]{:S(2)}) copy-start(s32[6144,1]{0,1:T(1,128)} %compare_select_fusion.4) | copy-start | bytes 73732
  553.4 95.2 %copy-start.4 = (s32[1,1,6144]{2,1,0:T(1,128)S(1)}, s32[1,1,6144]{2,1,0:T(1,128)}, u32[]{:S(2)}) copy-start(s32[1,1,6144]{2,1,0:T(1,128)} %copy-done.3) | copy-start | bytes 73732
  553.4 95.2 %copy-start.6 = (s32[6144]{0:T(1024)S(1)}, s32[6144]{0:T(1024)}, u32[]{:S(2)}) copy-start(s32[6144]{0:T(1024)} %copy-done.5) | copy-start | bytes 73732
  606.0 55.8 %all-to-all-start.1 = ((f32[4,64,192]{2,0,1:T(4,128)}), f32[4,64,192]{2,0,1:T(4,128)S(1)}, u32[]{:S(2)}, u32[]{:S(2)}) async-start(f32[4,64,192]{2,0,1:T(4,128)} %broadcast_select_fusion.1), calls=%async_computation.1 | async-start | bytes 524288 | tf_op jit(solution)/shard_map/all_to_all | solution.py:231

commit v2 on v1

--- a/solution.py
+++ b/solution.py
@@ -20,6 +20,7 @@
 visc_alpha = 0.5
 eta_square = 0.01
 pair_block = 64
+UNROLL = 4
 
 
 def extended(block, sides, width):
@@ -52,9 +53,7 @@
     depth = fields.shape[0]
     cells = fields.reshape(depth, pencil_count, NZ, CAP).transpose(1, 0, 3, 2)
     wide = jnp.broadcast_to(cells[..., None], cells.shape + (CAP,))
-    wide = wide.reshape(pencil_count, depth, CAP, NZ * CAP)
-    dummy = jnp.zeros((1, depth, CAP, NZ * CAP), jnp.float32)
-    return jnp.concatenate([wide, dummy], axis=0)
+    return wide.reshape(pencil_count, depth, CAP, NZ * CAP)
 
 
 def shifted(rows, step):
@@ -64,12 +63,29 @@
     return pltpu.roll(rows, shift, 1)
 
 
+def pair_loop(first_ref, second_ref, count_ref, last_pencil, contribution, out_ref):
+    count = count_ref[0]
+
+    def body(group, carry):
+        sums = []
+        for lane in range(UNROLL):
+            p = group * UNROLL + lane
+            a = first_ref[p]
+            b = jnp.minimum(second_ref[p], last_pencil)
+            live = p < count
+            sums.append((a, [jnp.where(live, t, 0.0) for t in contribution(a, b)]))
+        for a, parts in sums:
+            for k, t in enumerate(parts):
+                out_ref[a, k] = out_ref[a, k] + t
+        return carry
+
+    lax.fori_loop(0, (count + UNROLL - 1) // UNROLL, body, 0)
+
+
 def density_kernel(first_ref, second_ref, count_ref, own_ref, near_ref, out_ref):
     out_ref[...] = jnp.zeros(out_ref.shape, jnp.float32)
 
-    def body(p, carry):
-        a = first_ref[p]
-        b = second_ref[p]
+    def contribution(a, b):
         xi = own_ref[a, 0:1, :]
         yi = own_ref[a, 1:2, :]
         zi = own_ref[a, 2:3, :]
@@ -88,18 +104,15 @@
             sq = falloff * falloff
             weight = kernel_norm * (sq * sq) * (1.0 + 2.0 * radius)
             total = total + weight * shifted(mj, step)
-        out_ref[a] = out_ref[a] + total
-        return carry
-
-    lax.fori_loop(0, count_ref[0], body, 0)
+        return [total]
+
+    pair_loop(first_ref, second_ref, count_ref, near_ref.shape[0] - 1, contribution, out_ref)
 
 
 def force_kernel(first_ref, second_ref, count_ref, own_ref, near_ref, out_ref):
     out_ref[...] = jnp.zeros(out_ref.shape, jnp.float32)
 
-    def body(p, carry):
-        a = first_ref[p]
-        b = second_ref[p]
+    def contribution(a, b):
         left = [own_ref[a, k : k + 1, :] for k in range(8)]
         right = [near_ref[b, k] for k in range(9)]
         acc_x = jnp.zeros((CAP, NZ * CAP), jnp.float32)
@@ -122,20 +135,14 @@
             acc_x = acc_x + pair_coef * dx
             acc_y = acc_y + pair_coef * dy
             acc_z = acc_z + pair_coef * dz
-        out_ref[a, 0] = out_ref[a, 0] + acc_x
-        out_ref[a, 1] = out_ref[a, 1] + acc_y
-        out_ref[a, 2] = out_ref[a, 2] + acc_z
-        return carry
-
-    lax.fori_loop(0, count_ref[0], body, 0)
+        return [acc_x, acc_y, acc_z]
+
+    pair_loop(first_ref, second_ref, count_ref, near_ref.shape[0] - 1, contribution, out_ref)
 
 
 def pair_pass(kernel, first_ids, second_ids, pair_count, own_rows, near_rows, out_depth):
     pencils = own_rows.shape[0]
-    if out_depth == 1:
-        out_shape = (pencils, CAP, NZ * CAP)
-    else:
-        out_shape = (pencils, out_depth, CAP, NZ * CAP)
+    out_shape = (pencils, out_depth, CAP, NZ * CAP)
     vmem = pl.BlockSpec(memory_space=pltpu.VMEM)
     return pl.pallas_call(
         kernel,
@@ -204,7 +211,7 @@
     density_sums = pair_pass(
         density_kernel, first_list, second_list, pair_count, own_pos, near_rows, 1
     )
-    density_own = guarded(jnp.sum(density_sums, axis=1), mass_own)
+    density_own = guarded(jnp.sum(density_sums[:, 0], axis=1), mass_own)
     second_fields = jnp.concatenate(
         [own_grid[3:6], density_own.reshape(1, CX, CY, pencil_slots)], axis=0
     )

time: 706 us -> 587 us (0.83)
  the two profiles are of different devices: /device:TPU:1 before, /device:TPU:25 now
where the time goes in v2:
time: 587 us; the launch traced here: 575 us
  local copies, waits for them, and re-layouts  340 us (58%)
  Pallas kernels  79.6 us (14%)
  other arithmetic  64.1 us (11%)
  starting transfers between devices  55.9 us (10%)
  waiting for transfers between devices  34.8 us (6%)
    pallas_call x2, Pallas kernels, pair_pass(): pl.pallas_call(kernel, out_shape=jax.ShapeDtypeStruct(out_shape, jnp.floa...  79.6 us
    gather x2, local copies, waits for them, and re-layouts, local(): jnp.take(results, jnp.minimum(arrived_slot, slots_all - 1), axis=1)  51.7 us
    reshape x4, local copies, waits for them, and re-layouts, expand_cells(): return wide.reshape(pencil_count, depth, CAP, NZ * CAP)  41.1 us
    gather x1, local copies, waits for them, and re-layouts, local(): jnp.take(packed, picked, axis=1).reshape(8, lanes_total, capacity)  41 us
    scatter x1, local copies, waits for them, and re-layouts, local(): own_grid = jnp.zeros((7, slots_all), jnp.float32).at[:, arrived_slot].set...  37.9 us
    all_to_all x1, starting transfers between devices, local(): lax.all_to_all(reply, 'gx', split_axis=1, concat_axis=1, tiled=True)  24.4 us
    gather x1, local copies, waits for them, and re-layouts, local(): answer = jnp.take(home_rows.reshape(4, -1), row_index, axis=1)  23.7 us
    slice x2, local copies, waits for them, and re-layouts, local(): own_grid[3:6]  22.4 us
  transfers between devices with their start and end apart: 10, of which 4 were waited for; matrix products, arithmetic and copies ran while one was open for 11% of the time, Pallas kernels for 0%

profile of v2, /device:TPU:25, one launch (start us, length us, event | category | flops | bytes accessed | tf_op | source)
XLA Modules:
  0.0 575.1 jit_solution(15734189986278959431)
XLA Ops:
  4.0 41.0 %gather_fusion = f32[12288,8]{1,0:T(8,128)} fusion(f32[8,6144]{0,1:T(8,128)S(1)} %copy.213, s32[12288]{0:T(1024)S(1)} %broadcast_clamp_fusion.1), kind=kCustom, calls=%fused_computation | custom fusion | bytes 835584 | tf_op jit(solution)/shard_map/jit(_take)/gather | solution.py:188
  45.0 8.6 %select_bitcast_fusion = f32[8,12288]{0,1:T(8,128)S(1)} fusion(f32[12288,8]{1,0:T(8,128)} %gather_fusion, pred[12288]{0:T(1024)(128)(4,1)S(1)} %compare_and_fusion.1), kind=kLoop, calls=%fused_computation.12 | loop fusion | flops 98304 | bytes 798720 | tf_op jit(solution)/shard_map/jit(_take)/select_n | solution.py:188
  59.9 5.0 copy.214
  65.8 12.2 %all-to-all-start = ((f32[8,64,192]{2,0,1:T(8,128)}), f32[8,64,192]{2,0,1:T(8,128)S(1)}, u32[]{:S(2)}, u32[]{:S(2)}) async-start(f32[8,64,192]{2,0,1:T(8,128)} %pad_maximum_fusion.3), calls=%async_computation | async-start | bytes 1048576 | tf_op jit(solution)/shard_map/all_to_all | solution.py:191
  79.7 15.9 %all-to-all-done = f32[8,64,192]{2,0,1:T(8,128)S(1)} async-done(((f32[8,64,192]{2,0,1:T(8,128)}), f32[8,64,192]{2,0,1:T(8,128)S(1)}, u32[]{:S(2)}, u32[]{:S(2)}) %all-to-all-start) | async-done | bytes 393248 | tf_op jit(solution)/shard_map/all_to_all | solution.py:191
  100.3 37.9 %scatter_custom_fusion = f32[7,32768]{0,1:T(8,128)} fusion(s32[12288]{0:T(1024)S(1)} %bitcast.103, f32[12288,7]{1,0:T(8,128)} %copy.218, f32[]{:T(128)} %constant.97.clone.1), kind=kCustom, calls=%fused_computation.9 | custom fusion | bytes 918016 | tf_op jit(solution)/shard_map/scatter | solution.py:196
  138.3 12.7 %slice_reduce_fusion = f32[32768]{0:T(1024)S(1)} fusion(f32[7,32768]{0,1:T(8,128)} %scatter_custom_fusion), kind=kLoop, calls=%fused_computation.5 | loop fusion | bytes 262144 | tf_op jit(solution)/shard_map/slice | solution.py:200
  151.0 9.9 %fusion.8 = (pred[32768]{0:T(1024)(128)(4,1)S(1)}, pred[1,32768]{0,1:T(8,128)(4,1)}) fusion(f32[7,32768]{0,1:T(8,128)S(1)} %copy-done), kind=kLoop, calls=%fused_computation.80 | loop fusion | flops 32768 | bytes 196608 | tf_op jit(solution)/shard_map/gt | solution.py:166
  160.9 12.4 %fusion.9 = (f32[3,32768]{0,1:T(8,128)}, f32[3,32768]{0,1:T(8,128)}) fusion(f32[7,32768]{0,1:T(8,128)S(1)} %copy-done), kind=kLoop, calls=%fused_computation.81 | loop fusion | bytes 1572864 | tf_op jit(solution)/shard_map/slice | solution.py:216
  173.3 10.0 %copy.222 = f32[3,16,16,128]{3,2,1,0:T(8,128)S(1)} copy(f32[3,16,16,128]{0,3,2,1:T(8,128)} %bitcast.76) | data formatting | bytes 786432 | tf_op jit(solution)/shard_map/slice | solution.py:205
  188.7 9.4 %copy.231 = f32[6,256,128]{2,0,1:T(8,128)S(1)} copy(f32[6,256,128]{0,2,1:T(8,128)} %bitcast.75) | data formatting | bytes 1572864 | tf_op jit(solution)/shard_map/slice | solution.py:229
  198.2 10.0 %copy.233 = f32[3,16,16,128]{3,2,1,0:T(8,128)S(1)} copy(f32[3,16,16,128]{0,3,2,1:T(8,128)} %bitcast.79) | data formatting | bytes 786432 | tf_op jit(solution)/shard_map/slice | solution.py:216
  208.2 9.4 %copy.221 = f32[3,256,128]{2,0,1:T(4,128)S(1)} copy(f32[3,256,128]{0,2,1:T(8,128)} %bitcast.77) | data formatting | bytes 786432 | tf_op jit(solution)/shard_map/slice | solution.py:201
  225.5 4.3 copy.227
  229.8 5.1 reshape_reshape.2
  236.8 4.4 broadcast_bitcast_fusion.1
  241.2 9.9 %copy.229.near_ref = f32[400,4,8,128]{3,2,1,0:T(8,128)} copy(f32[400,4,8,128]{0,3,2,1:T(8,128)} %broadcast_bitcast_fusion.1) | data formatting | bytes 13107200 | tf_op jit(solution)/shard_map/reshape | solution.py:56
  251.1 30.8 %shard_map.37 = f32[256,1,8,128]{3,2,1,0:T(8,128)} custom-call(s32[6400]{0:T(1024)} %get-tuple-element.18.first_ref, s32[6400]{0:T(1024)} %copy-done.2, s32[1]{0:T(128)} %bitcast.7.count_ref, f32[256,8,128]{2,1,0:T(8,128)} %pad_bitcast_fusion.own_ref, f32[400,4,8,128]{3,2,1,0:T(8,128)} %copy.229.near_ref), custom_call_target="tpu_custom_call" | custom-call | tf_op jit(solution)/shard_map/pallas_call | solution.py:147
  283.5 5.8 %collective-permute-start.4 = (f32[4,2,16,128]{3,2,1,0:T(8,128)S(1)}, f32[4,2,16,128]{3,2,1,0:T(8,128)S(1)}, u32[]{:S(2)}, u32[]{:S(2)}) collective-permute-start(f32[4,2,16,128]{3,2,1,0:T(8,128)S(1)} %get-tuple-element.32), channel_id=1, source_target_pairs={{0,4},{4,8},{8,12},{12,16},{16,20},{20,24},{24,28},{28,32},{32,36}... | collective-permute-start | bytes 196616 | tf_op jit(solution)/shard_map/ppermute | solution.py:31
  291.3 8.3 %copy.246 = f32[1,32768]{0,1:T(8,128)} copy(f32[1,32768]{1,0:T(1,128)S(1)} %bitcast.92) | data formatting | bytes 262144 | tf_op jit(solution)/shard_map/reduce_sum | solution.py:214
  300.0 12.4 %broadcast_select_fusion = f32[1,32768]{0,1:T(8,128)} fusion(pred[1,32768]{0,1:T(8,128)(4,1)} %get-tuple-element.24, f32[1,32768]{0,1:T(8,128)} %copy.246), kind=kLoop, calls=%fused_computation.8 | loop fusion | flops 32768 | bytes 294912 | tf_op jit(solution)/shard_map/jit(_where)/select_n | solution.py:166
  343.8 8.8 %broadcast_bitcast_fusion = f32[400,9,8,128]{0,3,2,1:T(8,128)} fusion(f32[400,9,8,16]{0,3,2,1:T(8,128)S(1)} %copy.242), kind=kLoop, calls=%fused_computation.7 | loop fusion | bytes 16588800 | tf_op jit(solution)/shard_map/reshape | solution.py:56
  352.6 17.9 %copy.243.near_ref = f32[400,9,8,128]{3,2,1,0:T(8,128)} copy(f32[400,9,8,128]{0,3,2,1:T(8,128)} %broadcast_bitcast_fusion) | data formatting | bytes 29491200 | tf_op jit(solution)/shard_map/reshape | solution.py:56
  370.5 48.8 %shard_map.38 = f32[256,3,8,128]{3,2,1,0:T(8,128)} custom-call(s32[6400]{0:T(1024)} %get-tuple-element.18.first_ref, s32[6400]{0:T(1024)} %copy-done.2, s32[1]{0:T(128)} %bitcast.7.count_ref, f32[256,8,128]{2,1,0:T(8,128)} %maximum_bitcast_fusion.own_ref, f32[400,9,8,128]{3,2,1,0:T(8,128)} %copy.243.near_ref), custom_call_target="tpu_custom_call" | custom-call | tf_op jit(solution)/shard_map/pallas_call | solution.py:147
  425.2 8.2 %copy.245 = f32[3,256,128]{0,2,1:T(8,128)} copy(f32[3,256,128]{2,0,1:T(4,128)S(1)} %scatter-add.4) | data formatting | bytes 786432 | tf_op jit(solution)/shard_map/scatter-add | solution.py:233
  433.4 17.3 %pad_maximum_fusion = f32[4,32768]{0,1:T(8,128)} fusion(f32[1,32768]{0,1:T(8,128)} %broadcast_select_fusion, f32[3,32768]{0,1:T(8,128)} %bitcast.78), kind=kLoop, calls=%fused_computation.4 | loop fusion | flops 131072 | bytes 1048576 | tf_op jit(solution)/shard_map/concatenate | solution.py:234
  450.7 46.8 %gather_fusion.1 = f32[12288,4]{1,0:T(8,128)} fusion(f32[4,32768]{0,1:T(8,128)} %pad_maximum_fusion, s32[12288]{0:T(1024)S(1)} %broadcast_clamp_fusion), kind=kCustom, calls=%fused_computation.1 | custom fusion | bytes 442368 | tf_op jit(solution)/shard_map/jit(_take)/gather | solution.py:235
  497.4 4.9 copy.247
  503.2 24.4 %all-to-all-start.1 = ((f32[4,64,192]{2,0,1:T(4,128)}), f32[4,64,192]{2,0,1:T(4,128)S(1)}, u32[]{:S(2)}, u32[]{:S(2)}) async-start(f32[4,64,192]{2,0,1:T(4,128)} %broadcast_select_fusion.1), calls=%async_computation.1 | async-start | bytes 524288 | tf_op jit(solution)/shard_map/all_to_all | solution.py:238
  527.6 13.0 %all-to-all-done.1 = f32[4,64,192]{2,0,1:T(4,128)S(1)} async-done(((f32[4,64,192]{2,0,1:T(4,128)}), f32[4,64,192]{2,0,1:T(4,128)S(1)}, u32[]{:S(2)}, u32[]{:S(2)}) %all-to-all-start.1) | async-done | bytes 196640 | tf_op jit(solution)/shard_map/all_to_all | solution.py:238
  544.7 23.7 %gather_fusion.2 = f32[6144,4]{1,0:T(8,128)} fusion(f32[4,12288]{0,1:T(8,128)} %bitcast.81, s32[6144]{0:T(1024)S(1)} %broadcast_clamp_fusion.2), kind=kCustom, calls=%fused_computation.2 | custom fusion | bytes 221184 | tf_op jit(solution)/shard_map/jit(_take)/gather | solution.py:241
  568.4 4.7 bitcast_select_fusion
  (106 shorter events, 80.4 us)
Async XLA Ops:
  53.6 2.7 copy-start.1
  56.2 22.1 %copy-start.4 = (s32[1,2,6400]{2,1,0:T(2,128)S(1)}, s32[1,2,6400]{2,1,0:T(2,128)}, u32[]{:S(2)}) copy-start(s32[1,2,6400]{2,1,0:T(2,128)} %param.7) | copy-start | bytes 153604
  59.7 20.0 %copy-start.3 = (s32[1,2,6144]{2,1,0:T(2,128)S(1)}, s32[1,2,6144]{2,1,0:T(2,128)}, u32[]{:S(2)}) copy-start(s32[1,2,6144]{2,1,0:T(2,128)} %param.6) | copy-start | bytes 147460
  65.8 29.9 %all-to-all-start = ((f32[8,64,192]{2,0,1:T(8,128)}), f32[8,64,192]{2,0,1:T(8,128)S(1)}, u32[]{:S(2)}, u32[]{:S(2)}) async-start(f32[8,64,192]{2,0,1:T(8,128)} %pad_maximum_fusion.3), calls=%async_computation | async-start | bytes 1048576 | tf_op jit(solution)/shard_map/all_to_all | solution.py:191
  79.0 59.2 %copy-start.2 = (s32[6400]{0:T(1024)}, s32[6400]{0:T(1024)S(1)}, u32[]{:S(2)}) copy-start(s32[6400]{0:T(1024)S(1)} %get-tuple-element.17.second_ref) | copy-start | bytes 76804
  138.3 12.7 %copy-start = (f32[7,32768]{0,1:T(8,128)S(1)}, f32[7,32768]{0,1:T(8,128)}, u32[]{:S(2)}) copy-start(f32[7,32768]{0,1:T(8,128)} %scatter_custom_fusion) | copy-start | bytes 2752516
  183.3 34.3 %collective-permute-start = (f32[4,2,16,128]{3,2,1,0:T(8,128)S(1)}, f32[4,2,16,128]{3,2,1,0:T(8,128)S(1)}, u32[]{:S(2)}, u32[]{:S(2)}) collective-permute-start(f32[4,2,16,128]{3,2,1,0:T(8,128)S(1)} %get-tuple-element.34), channel_id=1, source_target_pairs={{0,4},{4,8},{8,12},{12,16},{16,20},{20,24},{24,28},{28,32},{32,36}... | collective-permute-start | bytes 196616 | tf_op jit(solution)/shard_map/ppermute | solution.py:31
  186.7 30.9 %collective-permute-start.1 = (f32[4,2,16,128]{3,2,1,0:T(8,128)S(1)}, f32[4,2,16,128]{3,2,1,0:T(8,128)S(1)}, u32[]{:S(2)}, u32[]{:S(2)}) collective-permute-start(f32[4,2,16,128]{3,2,1,0:T(8,128)S(1)} %get-tuple-element.35), channel_id=1, source_target_pairs={{4,0},{8,4},{12,8},{16,12},{20,16},{24,20},{28,24},{32,28},{36,32}... | collective-permute-start | bytes 196616 | tf_op jit(solution)/shard_map/ppermute | solution.py:34
  217.7 4.7 collective-permute-start.3
  220.1 5.2 collective-permute-start.2
  283.5 37.2 %collective-permute-start.4 = (f32[4,2,16,128]{3,2,1,0:T(8,128)S(1)}, f32[4,2,16,128]{3,2,1,0:T(8,128)S(1)}, u32[]{:S(2)}, u32[]{:S(2)}) collective-permute-start(f32[4,2,16,128]{3,2,1,0:T(8,128)S(1)} %get-tuple-element.32), channel_id=1, source_target_pairs={{0,4},{4,8},{8,12},{12,16},{16,20},{20,24},{24,28},{28,32},{32,36}... | collective-permute-start | bytes 196616 | tf_op jit(solution)/shard_map/ppermute | solution.py:31
  289.2 31.4 %collective-permute-start.5 = (f32[4,2,16,128]{3,2,1,0:T(8,128)S(1)}, f32[4,2,16,128]{3,2,1,0:T(8,128)S(1)}, u32[]{:S(2)}, u32[]{:S(2)}) collective-permute-start(f32[4,2,16,128]{3,2,1,0:T(8,128)S(1)} %get-tuple-element.33), channel_id=1, source_target_pairs={{4,0},{8,4},{12,8},{16,12},{20,16},{24,20},{28,24},{32,28},{36,32}... | collective-permute-start | bytes 196616 | tf_op jit(solution)/shard_map/ppermute | solution.py:34
  320.8 3.6 collective-permute-start.7
  322.1 5.3 collective-permute-start.6
  503.2 37.5 %all-to-all-start.1 = ((f32[4,64,192]{2,0,1:T(4,128)}), f32[4,64,192]{2,0,1:T(4,128)S(1)}, u32[]{:S(2)}, u32[]{:S(2)}) async-start(f32[4,64,192]{2,0,1:T(4,128)} %broadcast_select_fusion.1), calls=%async_computation.1 | async-start | bytes 524288 | tf_op jit(solution)/shard_map/all_to_all | solution.py:238

commit v3 on v2

--- a/solution.py
+++ b/solution.py
@@ -166,6 +166,28 @@
     return jnp.where(masses > 0.0, density, rest_density)
 
 
+HIGHEST = lax.Precision.HIGHEST
+
+
+def window_maps(counts, starts, capacity, row_count):
+    lanes_total = counts.shape[0]
+    span = (127 + capacity + 127) // 128
+    chunk_total = (row_count + 127) // 128 + span
+    first_chunk = starts // 128
+    offset = starts % 128
+    k = jnp.arange(span * 128, dtype=jnp.int32)
+    w = jnp.arange(capacity, dtype=jnp.int32)
+    shift_map = (
+        (k[None, :, None] == offset[:, None, None] + w[None, None, :])
+        & (w[None, None, :] < counts[:, None, None])
+    ).astype(jnp.float32)
+    t = jnp.arange(chunk_total, dtype=jnp.int32)
+    chunk_map = (
+        t[None, None, :] == first_chunk[:, None, None] + jnp.arange(span, dtype=jnp.int32)[None, :, None]
+    ).astype(jnp.float32).reshape(lanes_total * span, chunk_total)
+    return shift_map, chunk_map, chunk_total
+
+
 def local(particles, routing, tile_list):
     lanes_total = lax.axis_size("gx")
     row_count = particles.shape[2]
@@ -183,9 +205,13 @@
     starts = jnp.cumsum(counts) - counts
     within = jnp.arange(capacity, dtype=jnp.int32)
     is_valid = within[None, :] < counts[:, None]
-    picked = jnp.where(is_valid, starts[:, None] + within[None, :], 0).reshape(-1)
     packed = jnp.concatenate([fields, slot_ids.astype(jnp.float32)[None, :]], axis=0)
-    outgoing = jnp.take(packed, picked, axis=1).reshape(8, lanes_total, capacity)
+    shift_map, chunk_map, chunk_total = window_maps(counts, starts, capacity, row_count)
+    chunked = jnp.pad(packed, ((0, 0), (0, chunk_total * 128 - row_count)))
+    windows = jnp.einsum(
+        "jt,ftl->fjl", chunk_map, chunked.reshape(8, chunk_total, 128), precision=HIGHEST
+    ).reshape(8, lanes_total, -1)
+    outgoing = jnp.einsum("fok,okw->fow", windows, shift_map, precision=HIGHEST)
     marker = jnp.where(is_valid, outgoing[7], float(slots_all))
     outgoing = jnp.concatenate([outgoing[:7], marker[None]], axis=0)
     arrived = lax.all_to_all(outgoing, "gx", split_axis=1, concat_axis=1, tiled=True)
@@ -236,9 +262,10 @@
         4, lanes_total, capacity
     )
     home_rows = lax.all_to_all(reply, "gx", split_axis=1, concat_axis=1, tiled=True)
-    start_of = jnp.sum(jnp.where(match_owner, starts[:, None], 0), axis=0)
-    row_index = owner_of * capacity + jnp.arange(row_count, dtype=jnp.int32) - start_of
-    answer = jnp.take(home_rows.reshape(4, -1), row_index, axis=1)
+    spread = jnp.einsum("fow,okw->fok", jnp.where(is_valid[None], home_rows.reshape(4, lanes_total, capacity), 0.0), shift_map, precision=HIGHEST)
+    answer = jnp.einsum(
+        "jt,fjl->ftl", chunk_map, spread.reshape(4, chunk_map.shape[0], 128), precision=HIGHEST
+    ).reshape(4, chunk_total * 128)[:, :row_count]
     return answer[None]
 
 

time: 587 us -> 524 us (0.89)
  the two profiles are of different devices: /device:TPU:25 before, /device:TPU:9 now
where the time goes in v3:
time: 524 us; the launch traced here: 517 us
  local copies, waits for them, and re-layouts  258 us (49%)
  Pallas kernels  83.7 us (16%)
  other arithmetic  50.2 us (10%)
  blocking collectives  42.4 us (8%)
  starting transfers between devices  34.2 us (7%)
  matrix products  29.1 us (6%)
  waiting for transfers between devices  18.5 us (4%)
    pallas_call x2, Pallas kernels, pair_pass(): pl.pallas_call(kernel, out_shape=jax.ShapeDtypeStruct(out_shape, jnp.floa...  83.7 us
    gather x2, local copies, waits for them, and re-layouts, local(): jnp.take(results, jnp.minimum(arrived_slot, slots_all - 1), axis=1)  52 us
    all_to_all x1, blocking collectives, local(): lax.all_to_all(reply, 'gx', split_axis=1, concat_axis=1, tiled=True)  42.4 us
    reshape x4, local copies, waits for them, and re-layouts, expand_cells(): return wide.reshape(pencil_count, depth, CAP, NZ * CAP)  41 us
    scatter x1, local copies, waits for them, and re-layouts, local(): own_grid = jnp.zeros((7, slots_all), jnp.float32).at[:, arrived_slot].set...  37.9 us
    slice x2, local copies, waits for them, and re-layouts, local(): own_grid[3:6]  22.4 us
    dot_general x1, matrix products, local(): outgoing = jnp.einsum('fok,okw->fow', windows, shift_map, precision=HIGHEST)  18.2 us
    concatenate x1, other arithmetic, local(): jnp.concatenate([accel, density_own[None]], axis=0).reshape(4, slots_all)  17.3 us
  transfers between devices with their start and end apart: 9, of which 3 were waited for; matrix products, arithmetic and copies ran while one was open for 12% of the time, Pallas kernels for 0%

profile of v3, /device:TPU:9, one launch (start us, length us, event | category | flops | bytes accessed | tf_op | source)
XLA Modules:
  0.0 516.7 jit_solution(8560530544128046754)
XLA Ops:
  3.7 18.2 %fusion.11 = f32[8,64,192]{2,0,1:T(8,128)S(1)} fusion(s32[64,192]{1,0:T(8,128)S(1)} %iota_add_fusion, pred[64,192]{1,0:T(8,128)(4,1)S(1)} %iota_compare_fusion.3, f32[8,64,384]{2,1,0:T(8,128)S(1)} %reshape.381), kind=kOutput, calls=%fused_computation.21 | convolution fusion | flops 462422016 | bytes 1241088 | tf_op jit(solution)/shard_map/fok,okw->fow/dot_general | solution.py:214
  22.9 12.2 %all-to-all-start = ((f32[8,64,192]{2,0,1:T(8,128)}), f32[8,64,192]{2,0,1:T(8,128)S(1)}, u32[]{:S(2)}, u32[]{:S(2)}) async-start(f32[8,64,192]{2,0,1:T(8,128)} %pad_maximum_fusion.3), calls=%async_computation | async-start | bytes 1048576 | tf_op jit(solution)/shard_map/all_to_all | solution.py:217
  36.5 16.2 %all-to-all-done = f32[8,64,192]{2,0,1:T(8,128)S(1)} async-done(((f32[8,64,192]{2,0,1:T(8,128)}), f32[8,64,192]{2,0,1:T(8,128)S(1)}, u32[]{:S(2)}, u32[]{:S(2)}) %all-to-all-start) | async-done | bytes 393248 | tf_op jit(solution)/shard_map/all_to_all | solution.py:217
  53.7 4.0 copy.173
  57.6 37.9 %scatter_custom_fusion = f32[7,32768]{0,1:T(8,128)} fusion(s32[12288]{0:T(1024)S(1)} %bitcast.102, f32[12288,7]{1,0:T(8,128)} %copy.173, f32[]{:T(128)} %constant.87.clone.1), kind=kCustom, calls=%fused_computation.15 | custom fusion | bytes 918016 | tf_op jit(solution)/shard_map/scatter | solution.py:222
  95.6 12.7 %slice_reduce_fusion = f32[32768]{0:T(1024)S(1)} fusion(f32[7,32768]{0,1:T(8,128)} %scatter_custom_fusion), kind=kLoop, calls=%fused_computation.7 | loop fusion | bytes 262144 | tf_op jit(solution)/shard_map/slice | solution.py:226
  108.3 9.9 %fusion.35 = (pred[32768]{0:T(1024)(128)(4,1)S(1)}, pred[1,32768]{0,1:T(8,128)(4,1)}) fusion(f32[7,32768]{0,1:T(8,128)S(1)} %copy-done), kind=kLoop, calls=%fused_computation.97 | loop fusion | flops 32768 | bytes 196608 | tf_op jit(solution)/shard_map/gt | solution.py:166
  118.3 12.4 %fusion.36 = (f32[3,32768]{0,1:T(8,128)}, f32[3,32768]{0,1:T(8,128)}) fusion(f32[7,32768]{0,1:T(8,128)S(1)} %copy-done), kind=kLoop, calls=%fused_computation.98 | loop fusion | bytes 1572864 | tf_op jit(solution)/shard_map/slice | solution.py:242
  130.7 10.0 %copy.177 = f32[3,16,16,128]{3,2,1,0:T(8,128)S(1)} copy(f32[3,16,16,128]{0,3,2,1:T(8,128)} %bitcast.80) | data formatting | bytes 786432 | tf_op jit(solution)/shard_map/slice | solution.py:231
  146.0 9.4 %copy.186 = f32[6,256,128]{2,0,1:T(8,128)S(1)} copy(f32[6,256,128]{0,2,1:T(8,128)} %bitcast.79) | data formatting | bytes 1572864 | tf_op jit(solution)/shard_map/slice | solution.py:255
  155.5 10.0 %copy.188 = f32[3,16,16,128]{3,2,1,0:T(8,128)S(1)} copy(f32[3,16,16,128]{0,3,2,1:T(8,128)} %bitcast.83) | data formatting | bytes 786432 | tf_op jit(solution)/shard_map/slice | solution.py:242
  165.5 9.4 %copy.176 = f32[3,256,128]{2,0,1:T(4,128)S(1)} copy(f32[3,256,128]{0,2,1:T(8,128)} %bitcast.81) | data formatting | bytes 786432 | tf_op jit(solution)/shard_map/slice | solution.py:227
  182.6 4.3 copy.182
  186.8 5.1 reshape_reshape.2
  193.8 4.4 broadcast_bitcast_fusion.1
  198.2 9.9 %copy.184.near_ref = f32[400,4,8,128]{3,2,1,0:T(8,128)} copy(f32[400,4,8,128]{0,3,2,1:T(8,128)} %broadcast_bitcast_fusion.1) | data formatting | bytes 13107200 | tf_op jit(solution)/shard_map/reshape | solution.py:56
  208.1 32.4 %shard_map.37 = f32[256,1,8,128]{3,2,1,0:T(8,128)} custom-call(s32[6400]{0:T(1024)} %get-tuple-element.18.first_ref, s32[6400]{0:T(1024)} %copy-done.1, s32[1]{0:T(128)} %bitcast.7.count_ref, f32[256,8,128]{2,1,0:T(8,128)} %pad_bitcast_fusion.own_ref, f32[400,4,8,128]{3,2,1,0:T(8,128)} %copy.184.near_ref), custom_call_target="tpu_custom_call" | custom-call | tf_op jit(solution)/shard_map/pallas_call | solution.py:147
  246.6 8.3 %copy.201 = f32[1,32768]{0,1:T(8,128)} copy(f32[1,32768]{1,0:T(1,128)S(1)} %bitcast.94) | data formatting | bytes 262144 | tf_op jit(solution)/shard_map/reduce_sum | solution.py:240
  255.2 12.4 %broadcast_select_fusion = f32[1,32768]{0,1:T(8,128)} fusion(pred[1,32768]{0,1:T(8,128)(4,1)} %get-tuple-element.24, f32[1,32768]{0,1:T(8,128)} %copy.201), kind=kLoop, calls=%fused_computation.14 | loop fusion | flops 32768 | bytes 294912 | tf_op jit(solution)/shard_map/jit(_where)/select_n | solution.py:166
  268.9 3.4 copy.187
  272.4 3.5 concatenate.59
  276.0 4.1 collective-permute-start.7
  291.9 3.5 concatenate.63
  301.6 8.8 %broadcast_bitcast_fusion = f32[400,9,8,128]{0,3,2,1:T(8,128)} fusion(f32[400,9,8,16]{0,3,2,1:T(8,128)S(1)} %copy.197), kind=kLoop, calls=%fused_computation.9 | loop fusion | bytes 16588800 | tf_op jit(solution)/shard_map/reshape | solution.py:56
  310.4 17.8 %copy.198.near_ref = f32[400,9,8,128]{3,2,1,0:T(8,128)} copy(f32[400,9,8,128]{0,3,2,1:T(8,128)} %broadcast_bitcast_fusion) | data formatting | bytes 29491200 | tf_op jit(solution)/shard_map/reshape | solution.py:56
  328.2 51.3 %shard_map.38 = f32[256,3,8,128]{3,2,1,0:T(8,128)} custom-call(s32[6400]{0:T(1024)} %get-tuple-element.18.first_ref, s32[6400]{0:T(1024)} %copy-done.1, s32[1]{0:T(128)} %bitcast.7.count_ref, f32[256,8,128]{2,1,0:T(8,128)} %maximum_bitcast_fusion.own_ref, f32[400,9,8,128]{3,2,1,0:T(8,128)} %copy.198.near_ref), custom_call_target="tpu_custom_call" | custom-call | tf_op jit(solution)/shard_map/pallas_call | solution.py:147
  385.4 8.2 %copy.200 = f32[3,256,128]{0,2,1:T(8,128)} copy(f32[3,256,128]{2,0,1:T(4,128)S(1)} %scatter-add.4) | data formatting | bytes 786432 | tf_op jit(solution)/shard_map/scatter-add | solution.py:259
  393.6 17.3 %pad_maximum_fusion = f32[4,32768]{0,1:T(8,128)} fusion(f32[1,32768]{0,1:T(8,128)} %broadcast_select_fusion, f32[3,32768]{0,1:T(8,128)} %bitcast.82), kind=kLoop, calls=%fused_computation.6 | loop fusion | flops 131072 | bytes 1048576 | tf_op jit(solution)/shard_map/concatenate | solution.py:260
  410.9 47.1 %gather_fusion = f32[12288,4]{1,0:T(8,128)} fusion(f32[4,32768]{0,1:T(8,128)} %pad_maximum_fusion, s32[12288]{0:T(1024)S(1)} %broadcast_clamp_fusion), kind=kCustom, calls=%fused_computation | custom fusion | bytes 442368 | tf_op jit(solution)/shard_map/jit(_take)/gather | solution.py:261
  458.0 4.9 copy.202
  463.0 42.4 %all_to_all.10 = f32[4,64,192]{2,0,1:T(4,128)S(1)} all-to-all(f32[4,64,192]{2,0,1:T(4,128)S(1)} %broadcast_select_fusion.1), channel_id=1, replica_groups=mesh['gx'=64,'gy'=4] {'gx'}, dimensions={1} | all-to-all | bytes 393216 | tf_op jit(solution)/shard_map/all_to_all | solution.py:264
  505.4 10.1 %fusion.14 = f32[4,64,384]{2,0,1:T(4,128)S(1)} fusion(s32[64,192]{1,0:T(8,128)S(1)} %iota_add_fusion, pred[64,192]{1,0:T(8,128)(4,1)S(1)} %iota_compare_fusion.3, f32[4,64,192]{2,0,1:T(4,128)S(1)} %all_to_all.10), kind=kOutput, calls=%fused_computation.22 | convolution fusion | flops 235978752 | bytes 651264 | tf_op jit(solution)/shard_map/fow,okw->fok/dot_general | solution.py:265
  (97 shorter events, 54.5 us)
Async XLA Ops:
  1.8 20.0 %copy-start.3 = (s32[192]{0:T(256)}, s32[192]{0:T(256)S(1)}, u32[]{:S(2)}) copy-start(s32[192]{0:T(256)S(1)} %add.127) | copy-start | bytes 2308
  3.7 31.4 %copy-start.2 = (s32[1,2,6400]{2,1,0:T(2,128)S(1)}, s32[1,2,6400]{2,1,0:T(2,128)}, u32[]{:S(2)}) copy-start(s32[1,2,6400]{2,1,0:T(2,128)} %param.7) | copy-start | bytes 153604
  22.9 29.9 %all-to-all-start = ((f32[8,64,192]{2,0,1:T(8,128)}), f32[8,64,192]{2,0,1:T(8,128)S(1)}, u32[]{:S(2)}, u32[]{:S(2)}) async-start(f32[8,64,192]{2,0,1:T(8,128)} %pad_maximum_fusion.3), calls=%async_computation | async-start | bytes 1048576 | tf_op jit(solution)/shard_map/all_to_all | solution.py:217
  35.8 59.7 %copy-start.1 = (s32[6400]{0:T(1024)}, s32[6400]{0:T(1024)S(1)}, u32[]{:S(2)}) copy-start(s32[6400]{0:T(1024)S(1)} %get-tuple-element.17.second_ref) | copy-start | bytes 76804
  95.6 12.8 %copy-start = (f32[7,32768]{0,1:T(8,128)S(1)}, f32[7,32768]{0,1:T(8,128)}, u32[]{:S(2)}) copy-start(f32[7,32768]{0,1:T(8,128)} %scatter_custom_fusion) | copy-start | bytes 2752516
  140.7 34.3 %collective-permute-start = (f32[4,2,16,128]{3,2,1,0:T(8,128)S(1)}, f32[4,2,16,128]{3,2,1,0:T(8,128)S(1)}, u32[]{:S(2)}, u32[]{:S(2)}) collective-permute-start(f32[4,2,16,128]{3,2,1,0:T(8,128)S(1)} %get-tuple-element.38), channel_id=1, source_target_pairs={{0,4},{4,8},{8,12},{12,16},{16,20},{20,24},{24,28},{28,32},{32,36}... | collective-permute-start | bytes 196616 | tf_op jit(solution)/shard_map/ppermute | solution.py:31
  144.1 30.9 %collective-permute-start.1 = (f32[4,2,16,128]{3,2,1,0:T(8,128)S(1)}, f32[4,2,16,128]{3,2,1,0:T(8,128)S(1)}, u32[]{:S(2)}, u32[]{:S(2)}) collective-permute-start(f32[4,2,16,128]{3,2,1,0:T(8,128)S(1)} %get-tuple-element.39), channel_id=1, source_target_pairs={{4,0},{8,4},{12,8},{16,12},{20,16},{24,20},{28,24},{32,28},{36,32}... | collective-permute-start | bytes 196616 | tf_op jit(solution)/shard_map/ppermute | solution.py:34
  175.1 6.3 %collective-permute-start.3 = (f32[4,20,2,128]{3,0,2,1:T(4,128)S(1)}, f32[4,20,2,128]{3,0,2,1:T(4,128)S(1)}, u32[]{:S(2)}, u32[]{:S(2)}) collective-permute-start(f32[4,20,2,128]{3,0,2,1:T(4,128)S(1)} %copy.211), channel_id=1, source_target_pairs={{1,0},{2,1},{3,2},{5,4},{6,5},{7,6},{9,8},{10,9},{11,10},{13,12},{... | collective-permute-start | bytes 245768 | tf_op jit(solution)/shard_map/ppermute | solution.py:34
  177.2 5.2 %collective-permute-start.2 = (f32[4,20,2,128]{3,0,2,1:T(4,128)S(1)}, f32[4,20,2,128]{3,0,2,1:T(4,128)S(1)}, u32[]{:S(2)}, u32[]{:S(2)}) collective-permute-start(f32[4,20,2,128]{3,0,2,1:T(4,128)S(1)} %copy.210), channel_id=1, source_target_pairs={{0,1},{1,2},{2,3},{4,5},{5,6},{6,7},{8,9},{9,10},{10,11},{12,13},{... | collective-permute-start | bytes 245768 | tf_op jit(solution)/shard_map/ppermute | solution.py:31
  242.0 33.8 %collective-permute-start.4 = (f32[4,2,16,128]{3,2,1,0:T(8,128)S(1)}, f32[4,2,16,128]{3,2,1,0:T(8,128)S(1)}, u32[]{:S(2)}, u32[]{:S(2)}) collective-permute-start(f32[4,2,16,128]{3,2,1,0:T(8,128)S(1)} %get-tuple-element.36), channel_id=1, source_target_pairs={{0,4},{4,8},{8,12},{12,16},{16,20},{20,24},{24,28},{28,32},{32,36}... | collective-permute-start | bytes 196616 | tf_op jit(solution)/shard_map/ppermute | solution.py:31
  244.0 31.9 %collective-permute-start.5 = (f32[4,2,16,128]{3,2,1,0:T(8,128)S(1)}, f32[4,2,16,128]{3,2,1,0:T(8,128)S(1)}, u32[]{:S(2)}, u32[]{:S(2)}) collective-permute-start(f32[4,2,16,128]{3,2,1,0:T(8,128)S(1)} %get-tuple-element.37), channel_id=1, source_target_pairs={{4,0},{8,4},{12,8},{16,12},{20,16},{24,20},{28,24},{32,28},{36,32}... | collective-permute-start | bytes 196616 | tf_op jit(solution)/shard_map/ppermute | solution.py:34
  276.0 7.9 %collective-permute-start.7 = (f32[4,20,2,128]{3,0,2,1:T(4,128)S(1)}, f32[4,20,2,128]{3,0,2,1:T(4,128)S(1)}, u32[]{:S(2)}, u32[]{:S(2)}) collective-permute-start(f32[4,20,2,128]{3,0,2,1:T(4,128)S(1)} %copy.213), channel_id=1, source_target_pairs={{1,0},{2,1},{3,2},{5,4},{6,5},{7,6},{9,8},{10,9},{11,10},{13,12},{... | collective-permute-start | bytes 245768 | tf_op jit(solution)/shard_map/ppermute | solution.py:34
  280.1 5.2 %collective-permute-start.6 = (f32[4,20,2,128]{3,0,2,1:T(4,128)S(1)}, f32[4,20,2,128]{3,0,2,1:T(4,128)S(1)}, u32[]{:S(2)}, u32[]{:S(2)}) collective-permute-start(f32[4,20,2,128]{3,0,2,1:T(4,128)S(1)} %copy.212), channel_id=1, source_target_pairs={{0,1},{1,2},{2,3},{4,5},{5,6},{6,7},{8,9},{9,10},{10,11},{12,13},{... | collective-permute-start | bytes 245768 | tf_op jit(solution)/shard_map/ppermute | solution.py:31
  505.4 10.2 %copy-start.4 = (s32[192]{0:T(256)S(1)}, s32[192]{0:T(256)}, u32[]{:S(2)}) copy-start(s32[192]{0:T(256)} %copy-done.3) | copy-start | bytes 2308

commit v4 on v3

--- a/solution.py
+++ b/solution.py
@@ -20,7 +20,6 @@
 visc_alpha = 0.5
 eta_square = 0.01
 pair_block = 64
-UNROLL = 4
 
 
 def extended(block, sides, width):
@@ -63,13 +62,13 @@
     return pltpu.roll(rows, shift, 1)
 
 
-def pair_loop(first_ref, second_ref, count_ref, last_pencil, contribution, out_ref):
+def pair_loop(first_ref, second_ref, count_ref, last_pencil, contribution, out_ref, unroll):
     count = count_ref[0]
 
     def body(group, carry):
         sums = []
-        for lane in range(UNROLL):
-            p = group * UNROLL + lane
+        for lane in range(unroll):
+            p = group * unroll + lane
             a = first_ref[p]
             b = jnp.minimum(second_ref[p], last_pencil)
             live = p < count
@@ -79,7 +78,7 @@
                 out_ref[a, k] = out_ref[a, k] + t
         return carry
 
-    lax.fori_loop(0, (count + UNROLL - 1) // UNROLL, body, 0)
+    lax.fori_loop(0, (count + unroll - 1) // unroll, body, 0)
 
 
 def density_kernel(first_ref, second_ref, count_ref, own_ref, near_ref, out_ref):
@@ -106,7 +105,7 @@
             total = total + weight * shifted(mj, step)
         return [total]
 
-    pair_loop(first_ref, second_ref, count_ref, near_ref.shape[0] - 1, contribution, out_ref)
+    pair_loop(first_ref, second_ref, count_ref, near_ref.shape[0] - 1, contribution, out_ref, 8)
 
 
 def force_kernel(first_ref, second_ref, count_ref, own_ref, near_ref, out_ref):
@@ -137,7 +136,7 @@
             acc_z = acc_z + pair_coef * dz
         return [acc_x, acc_y, acc_z]
 
-    pair_loop(first_ref, second_ref, count_ref, near_ref.shape[0] - 1, contribution, out_ref)
+    pair_loop(first_ref, second_ref, count_ref, near_ref.shape[0] - 1, contribution, out_ref, 4)
 
 
 def pair_pass(kernel, first_ids, second_ids, pair_count, own_rows, near_rows, out_depth):

time: 524 us -> 508 us (0.969)
  the two profiles are of different devices: /device:TPU:9 before, /device:TPU:25 now
where the time goes in v4:
time: 508 us; the launch traced here: 500 us
  local copies, waits for them, and re-layouts  258 us (51%)
  Pallas kernels  74.6 us (15%)
  other arithmetic  50.2 us (10%)
  starting transfers between devices  33.2 us (7%)
  blocking collectives  32.2 us (6%)
  matrix products  29.1 us (6%)
  waiting for transfers between devices  22.2 us (4%)
    pallas_call x2, Pallas kernels, pair_pass(): pl.pallas_call(kernel, out_shape=jax.ShapeDtypeStruct(out_shape, jnp.floa...  74.6 us
    gather x2, local copies, waits for them, and re-layouts, local(): jnp.take(results, jnp.minimum(arrived_slot, slots_all - 1), axis=1)  52 us
    reshape x4, local copies, waits for them, and re-layouts, expand_cells(): return wide.reshape(pencil_count, depth, CAP, NZ * CAP)  41 us
    scatter x1, local copies, waits for them, and re-layouts, local(): own_grid = jnp.zeros((7, slots_all), jnp.float32).at[:, arrived_slot].set...  37.9 us
    all_to_all x1, blocking collectives, local(): lax.all_to_all(reply, 'gx', split_axis=1, concat_axis=1, tiled=True)  32.2 us
    slice x2, local copies, waits for them, and re-layouts, local(): own_grid[3:6]  22.4 us
    dot_general x1, matrix products, local(): outgoing = jnp.einsum('fok,okw->fow', windows, shift_map, precision=HIGHEST)  18.2 us
    concatenate x1, other arithmetic, local(): jnp.concatenate([accel, density_own[None]], axis=0).reshape(4, slots_all)  17.3 us
  transfers between devices with their start and end apart: 9, of which 3 were waited for; matrix products, arithmetic and copies ran while one was open for 12% of the time, Pallas kernels for 0%

profile of v4, /device:TPU:25, one launch (start us, length us, event | category | flops | bytes accessed | tf_op | source)
XLA Modules:
  0.0 500.2 jit_solution(11612190482278215118)
XLA Ops:
  3.7 18.2 %fusion.11 = f32[8,64,192]{2,0,1:T(8,128)S(1)} fusion(s32[64,192]{1,0:T(8,128)S(1)} %iota_add_fusion, pred[64,192]{1,0:T(8,128)(4,1)S(1)} %iota_compare_fusion.3, f32[8,64,384]{2,1,0:T(8,128)S(1)} %reshape.381), kind=kOutput, calls=%fused_computation.21 | convolution fusion | flops 462422016 | bytes 1241088 | tf_op jit(solution)/shard_map/fok,okw->fow/dot_general | solution.py:213
  22.9 12.2 %all-to-all-start = ((f32[8,64,192]{2,0,1:T(8,128)}), f32[8,64,192]{2,0,1:T(8,128)S(1)}, u32[]{:S(2)}, u32[]{:S(2)}) async-start(f32[8,64,192]{2,0,1:T(8,128)} %pad_maximum_fusion.3), calls=%async_computation | async-start | bytes 1048576 | tf_op jit(solution)/shard_map/all_to_all | solution.py:216
  36.5 16.2 %all-to-all-done = f32[8,64,192]{2,0,1:T(8,128)S(1)} async-done(((f32[8,64,192]{2,0,1:T(8,128)}), f32[8,64,192]{2,0,1:T(8,128)S(1)}, u32[]{:S(2)}, u32[]{:S(2)}) %all-to-all-start) | async-done | bytes 393248 | tf_op jit(solution)/shard_map/all_to_all | solution.py:216
  53.7 4.0 copy.173
  57.6 37.9 %scatter_custom_fusion = f32[7,32768]{0,1:T(8,128)} fusion(s32[12288]{0:T(1024)S(1)} %bitcast.102, f32[12288,7]{1,0:T(8,128)} %copy.173, f32[]{:T(128)} %constant.87.clone.1), kind=kCustom, calls=%fused_computation.15 | custom fusion | bytes 918016 | tf_op jit(solution)/shard_map/scatter | solution.py:221
  95.6 12.7 %slice_reduce_fusion = f32[32768]{0:T(1024)S(1)} fusion(f32[7,32768]{0,1:T(8,128)} %scatter_custom_fusion), kind=kLoop, calls=%fused_computation.7 | loop fusion | bytes 262144 | tf_op jit(solution)/shard_map/slice | solution.py:225
  108.3 9.9 %fusion.35 = (pred[32768]{0:T(1024)(128)(4,1)S(1)}, pred[1,32768]{0,1:T(8,128)(4,1)}) fusion(f32[7,32768]{0,1:T(8,128)S(1)} %copy-done), kind=kLoop, calls=%fused_computation.97 | loop fusion | flops 32768 | bytes 196608 | tf_op jit(solution)/shard_map/gt | solution.py:165
  118.3 12.4 %fusion.36 = (f32[3,32768]{0,1:T(8,128)}, f32[3,32768]{0,1:T(8,128)}) fusion(f32[7,32768]{0,1:T(8,128)S(1)} %copy-done), kind=kLoop, calls=%fused_computation.98 | loop fusion | bytes 1572864 | tf_op jit(solution)/shard_map/slice | solution.py:241
  130.7 10.0 %copy.177 = f32[3,16,16,128]{3,2,1,0:T(8,128)S(1)} copy(f32[3,16,16,128]{0,3,2,1:T(8,128)} %bitcast.80) | data formatting | bytes 786432 | tf_op jit(solution)/shard_map/slice | solution.py:230
  146.0 9.4 %copy.186 = f32[6,256,128]{2,0,1:T(8,128)S(1)} copy(f32[6,256,128]{0,2,1:T(8,128)} %bitcast.79) | data formatting | bytes 1572864 | tf_op jit(solution)/shard_map/slice | solution.py:254
  155.5 10.0 %copy.188 = f32[3,16,16,128]{3,2,1,0:T(8,128)S(1)} copy(f32[3,16,16,128]{0,3,2,1:T(8,128)} %bitcast.83) | data formatting | bytes 786432 | tf_op jit(solution)/shard_map/slice | solution.py:241
  165.5 9.4 %copy.176 = f32[3,256,128]{2,0,1:T(4,128)S(1)} copy(f32[3,256,128]{0,2,1:T(8,128)} %bitcast.81) | data formatting | bytes 786432 | tf_op jit(solution)/shard_map/slice | solution.py:226
  182.9 4.3 copy.182
  187.1 5.1 %reshape_reshape.2 = f32[4,400,16,8]{1,3,2,0:T(8,128)} reshape(f32[4,20,20,128]{2,1,3,0:T(8,128)} %copy.182) | data formatting | bytes 1638400 | tf_op jit(solution)/shard_map/reshape;reshape | solution.py:53
  194.1 4.4 broadcast_bitcast_fusion.1
  198.4 9.9 %copy.184.near_ref = f32[400,4,8,128]{3,2,1,0:T(8,128)} copy(f32[400,4,8,128]{0,3,2,1:T(8,128)} %broadcast_bitcast_fusion.1) | data formatting | bytes 13107200 | tf_op jit(solution)/shard_map/reshape | solution.py:55
  208.4 25.2 %shard_map.37 = f32[256,1,8,128]{3,2,1,0:T(8,128)} custom-call(s32[6400]{0:T(1024)} %get-tuple-element.18.first_ref, s32[6400]{0:T(1024)} %copy-done.1, s32[1]{0:T(128)} %bitcast.7.count_ref, f32[256,8,128]{2,1,0:T(8,128)} %pad_bitcast_fusion.own_ref, f32[400,4,8,128]{3,2,1,0:T(8,128)} %copy.184.near_ref), custom_call_target="tpu_custom_call" | custom-call | tf_op jit(solution)/shard_map/pallas_call | solution.py:146
  235.1 6.1 %collective-permute-start.4 = (f32[4,2,16,128]{3,2,1,0:T(8,128)S(1)}, f32[4,2,16,128]{3,2,1,0:T(8,128)S(1)}, u32[]{:S(2)}, u32[]{:S(2)}) collective-permute-start(f32[4,2,16,128]{3,2,1,0:T(8,128)S(1)} %get-tuple-element.36), channel_id=1, source_target_pairs={{0,4},{4,8},{8,12},{12,16},{16,20},{20,24},{24,28},{28,32},{32,36}... | collective-permute-start | bytes 196616 | tf_op jit(solution)/shard_map/ppermute | solution.py:30
  243.4 8.3 %copy.201 = f32[1,32768]{0,1:T(8,128)} copy(f32[1,32768]{1,0:T(1,128)S(1)} %bitcast.94) | data formatting | bytes 262144 | tf_op jit(solution)/shard_map/reduce_sum | solution.py:239
  252.0 12.4 %broadcast_select_fusion = f32[1,32768]{0,1:T(8,128)} fusion(pred[1,32768]{0,1:T(8,128)(4,1)} %get-tuple-element.24, f32[1,32768]{0,1:T(8,128)} %copy.201), kind=kLoop, calls=%fused_computation.14 | loop fusion | flops 32768 | bytes 294912 | tf_op jit(solution)/shard_map/jit(_where)/select_n | solution.py:165
  265.7 3.4 copy.187
  269.2 3.5 concatenate.59
  287.4 3.5 concatenate.63
  297.0 8.8 %broadcast_bitcast_fusion = f32[400,9,8,128]{0,3,2,1:T(8,128)} fusion(f32[400,9,8,16]{0,3,2,1:T(8,128)S(1)} %copy.197), kind=kLoop, calls=%fused_computation.9 | loop fusion | bytes 16588800 | tf_op jit(solution)/shard_map/reshape | solution.py:55
  305.8 17.8 %copy.198.near_ref = f32[400,9,8,128]{3,2,1,0:T(8,128)} copy(f32[400,9,8,128]{0,3,2,1:T(8,128)} %broadcast_bitcast_fusion) | data formatting | bytes 29491200 | tf_op jit(solution)/shard_map/reshape | solution.py:55
  323.7 49.4 %shard_map.38 = f32[256,3,8,128]{3,2,1,0:T(8,128)} custom-call(s32[6400]{0:T(1024)} %get-tuple-element.18.first_ref, s32[6400]{0:T(1024)} %copy-done.1, s32[1]{0:T(128)} %bitcast.7.count_ref, f32[256,8,128]{2,1,0:T(8,128)} %maximum_bitcast_fusion.own_ref, f32[400,9,8,128]{3,2,1,0:T(8,128)} %copy.198.near_ref), custom_call_target="tpu_custom_call" | custom-call | tf_op jit(solution)/shard_map/pallas_call | solution.py:146
  379.0 8.2 %copy.200 = f32[3,256,128]{0,2,1:T(8,128)} copy(f32[3,256,128]{2,0,1:T(4,128)S(1)} %scatter-add.4) | data formatting | bytes 786432 | tf_op jit(solution)/shard_map/scatter-add | solution.py:258
  387.2 17.3 %pad_maximum_fusion = f32[4,32768]{0,1:T(8,128)} fusion(f32[1,32768]{0,1:T(8,128)} %broadcast_select_fusion, f32[3,32768]{0,1:T(8,128)} %bitcast.82), kind=kLoop, calls=%fused_computation.6 | loop fusion | flops 131072 | bytes 1048576 | tf_op jit(solution)/shard_map/concatenate | solution.py:259
  404.5 47.1 %gather_fusion = f32[12288,4]{1,0:T(8,128)} fusion(f32[4,32768]{0,1:T(8,128)} %pad_maximum_fusion, s32[12288]{0:T(1024)S(1)} %broadcast_clamp_fusion), kind=kCustom, calls=%fused_computation | custom fusion | bytes 442368 | tf_op jit(solution)/shard_map/jit(_take)/gather | solution.py:260
  451.6 4.9 copy.202
  456.6 32.2 %all_to_all.10 = f32[4,64,192]{2,0,1:T(4,128)S(1)} all-to-all(f32[4,64,192]{2,0,1:T(4,128)S(1)} %broadcast_select_fusion.1), channel_id=1, replica_groups=mesh['gx'=64,'gy'=4] {'gx'}, dimensions={1} | all-to-all | bytes 393216 | tf_op jit(solution)/shard_map/all_to_all | solution.py:263
  488.9 10.1 %fusion.14 = f32[4,64,384]{2,0,1:T(4,128)S(1)} fusion(s32[64,192]{1,0:T(8,128)S(1)} %iota_add_fusion, pred[64,192]{1,0:T(8,128)(4,1)S(1)} %iota_compare_fusion.3, f32[4,64,192]{2,0,1:T(4,128)S(1)} %all_to_all.10), kind=kOutput, calls=%fused_computation.22 | convolution fusion | flops 235978752 | bytes 651264 | tf_op jit(solution)/shard_map/fow,okw->fok/dot_general | solution.py:264
  (97 shorter events, 55.1 us)
Async XLA Ops:
  1.8 20.0 %copy-start.3 = (s32[192]{0:T(256)}, s32[192]{0:T(256)S(1)}, u32[]{:S(2)}) copy-start(s32[192]{0:T(256)S(1)} %add.127) | copy-start | bytes 2308
  3.7 31.4 %copy-start.2 = (s32[1,2,6400]{2,1,0:T(2,128)S(1)}, s32[1,2,6400]{2,1,0:T(2,128)}, u32[]{:S(2)}) copy-start(s32[1,2,6400]{2,1,0:T(2,128)} %param.7) | copy-start | bytes 153604
  22.9 29.9 %all-to-all-start = ((f32[8,64,192]{2,0,1:T(8,128)}), f32[8,64,192]{2,0,1:T(8,128)S(1)}, u32[]{:S(2)}, u32[]{:S(2)}) async-start(f32[8,64,192]{2,0,1:T(8,128)} %pad_maximum_fusion.3), calls=%async_computation | async-start | bytes 1048576 | tf_op jit(solution)/shard_map/all_to_all | solution.py:216
  35.8 59.7 %copy-start.1 = (s32[6400]{0:T(1024)}, s32[6400]{0:T(1024)S(1)}, u32[]{:S(2)}) copy-start(s32[6400]{0:T(1024)S(1)} %get-tuple-element.17.second_ref) | copy-start | bytes 76804
  95.6 12.8 %copy-start = (f32[7,32768]{0,1:T(8,128)S(1)}, f32[7,32768]{0,1:T(8,128)}, u32[]{:S(2)}) copy-start(f32[7,32768]{0,1:T(8,128)} %scatter_custom_fusion) | copy-start | bytes 2752516
  140.7 34.3 %collective-permute-start = (f32[4,2,16,128]{3,2,1,0:T(8,128)S(1)}, f32[4,2,16,128]{3,2,1,0:T(8,128)S(1)}, u32[]{:S(2)}, u32[]{:S(2)}) collective-permute-start(f32[4,2,16,128]{3,2,1,0:T(8,128)S(1)} %get-tuple-element.38), channel_id=1, source_target_pairs={{0,4},{4,8},{8,12},{12,16},{16,20},{20,24},{24,28},{28,32},{32,36}... | collective-permute-start | bytes 196616 | tf_op jit(solution)/shard_map/ppermute | solution.py:30
  144.1 30.9 %collective-permute-start.1 = (f32[4,2,16,128]{3,2,1,0:T(8,128)S(1)}, f32[4,2,16,128]{3,2,1,0:T(8,128)S(1)}, u32[]{:S(2)}, u32[]{:S(2)}) collective-permute-start(f32[4,2,16,128]{3,2,1,0:T(8,128)S(1)} %get-tuple-element.39), channel_id=1, source_target_pairs={{4,0},{8,4},{12,8},{16,12},{20,16},{24,20},{28,24},{32,28},{36,32}... | collective-permute-start | bytes 196616 | tf_op jit(solution)/shard_map/ppermute | solution.py:33
  175.1 4.7 collective-permute-start.3
  177.5 5.2 %collective-permute-start.2 = (f32[4,20,2,128]{3,0,2,1:T(4,128)S(1)}, f32[4,20,2,128]{3,0,2,1:T(4,128)S(1)}, u32[]{:S(2)}, u32[]{:S(2)}) collective-permute-start(f32[4,20,2,128]{3,0,2,1:T(4,128)S(1)} %copy.210), channel_id=1, source_target_pairs={{0,1},{1,2},{2,3},{4,5},{5,6},{6,7},{8,9},{9,10},{10,11},{12,13},{... | collective-permute-start | bytes 245768 | tf_op jit(solution)/shard_map/ppermute | solution.py:30
  235.1 37.5 %collective-permute-start.4 = (f32[4,2,16,128]{3,2,1,0:T(8,128)S(1)}, f32[4,2,16,128]{3,2,1,0:T(8,128)S(1)}, u32[]{:S(2)}, u32[]{:S(2)}) collective-permute-start(f32[4,2,16,128]{3,2,1,0:T(8,128)S(1)} %get-tuple-element.36), channel_id=1, source_target_pairs={{0,4},{4,8},{8,12},{12,16},{16,20},{20,24},{24,28},{28,32},{32,36}... | collective-permute-start | bytes 196616 | tf_op jit(solution)/shard_map/ppermute | solution.py:30
  241.3 31.4 %collective-permute-start.5 = (f32[4,2,16,128]{3,2,1,0:T(8,128)S(1)}, f32[4,2,16,128]{3,2,1,0:T(8,128)S(1)}, u32[]{:S(2)}, u32[]{:S(2)}) collective-permute-start(f32[4,2,16,128]{3,2,1,0:T(8,128)S(1)} %get-tuple-element.37), channel_id=1, source_target_pairs={{4,0},{8,4},{12,8},{16,12},{20,16},{24,20},{28,24},{32,28},{36,32}... | collective-permute-start | bytes 196616 | tf_op jit(solution)/shard_map/ppermute | solution.py:33
  272.8 4.8 collective-permute-start.7
  275.3 5.4 %collective-permute-start.6 = (f32[4,20,2,128]{3,0,2,1:T(4,128)S(1)}, f32[4,20,2,128]{3,0,2,1:T(4,128)S(1)}, u32[]{:S(2)}, u32[]{:S(2)}) collective-permute-start(f32[4,20,2,128]{3,0,2,1:T(4,128)S(1)} %copy.212), channel_id=1, source_target_pairs={{0,1},{1,2},{2,3},{4,5},{5,6},{6,7},{8,9},{9,10},{10,11},{12,13},{... | collective-permute-start | bytes 245768 | tf_op jit(solution)/shard_map/ppermute | solution.py:30
  488.9 10.2 %copy-start.4 = (s32[192]{0:T(256)S(1)}, s32[192]{0:T(256)}, u32[]{:S(2)}) copy-start(s32[192]{0:T(256)} %copy-done.3) | copy-start | bytes 2308

commit v5 on v4

--- a/solution.py
+++ b/solution.py
@@ -136,7 +136,7 @@
             acc_z = acc_z + pair_coef * dz
         return [acc_x, acc_y, acc_z]
 
-    pair_loop(first_ref, second_ref, count_ref, near_ref.shape[0] - 1, contribution, out_ref, 4)
+    pair_loop(first_ref, second_ref, count_ref, near_ref.shape[0] - 1, contribution, out_ref, 8)
 
 
 def pair_pass(kernel, first_ids, second_ids, pair_count, own_rows, near_rows, out_depth):

time: 508 us -> 503 us (level)
  Pallas kernels: 74.6 us -> 18.5 us
  blocking collectives: 32.2 us -> 67.6 us
  starting transfers between devices: 33.2 us -> 47.5 us
    pallas_call x2, Pallas kernels: 74.6 us -> 18.5 us  [pair_pass(): pl.pallas_call(kernel, out_shape=jax.ShapeDtypeStruct(out_shape, jnp.floa...]
    all_to_all x1, blocking collectives: 32.2 us -> 67.6 us  [local(): lax.all_to_all(reply, 'gx', split_axis=1, concat_axis=1, tiled=True)]
    ppermute x4, starting transfers between devices: 8.9 us -> 24.4 us  [extended(): lax.ppermute(lax.slice_in_dim(block, 0, width, axis=dim), axis, backward)]
where the time goes in v5:
time: 503 us; the launch traced here: 495 us
  local copies, waits for them, and re-layouts  258 us (51%)
  blocking collectives  67.6 us (13%)
  other arithmetic  50.2 us (10%)
  starting transfers between devices  47.5 us (9%)
  matrix products  29.1 us (6%)
  waiting for transfers between devices  23.1 us (5%)
  Pallas kernels  18.5 us (4%)
    all_to_all x1, blocking collectives, local(): lax.all_to_all(reply, 'gx', split_axis=1, concat_axis=1, tiled=True)  67.6 us
    gather x2, local copies, waits for them, and re-layouts, local(): jnp.take(results, jnp.minimum(arrived_slot, slots_all - 1), axis=1)  52 us
    reshape x4, local copies, waits for them, and re-layouts, expand_cells(): return wide.reshape(pencil_count, depth, CAP, NZ * CAP)  41 us
    scatter x1, local copies, waits for them, and re-layouts, local(): own_grid = jnp.zeros((7, slots_all), jnp.float32).at[:, arrived_slot].set...  37.9 us
    ppermute x4, starting transfers between devices, extended(): lax.ppermute(lax.slice_in_dim(block, 0, width, axis=dim), axis, backward)  24.4 us
    slice x2, local copies, waits for them, and re-layouts, local(): own_grid[3:6]  22.4 us
    pallas_call x2, Pallas kernels, pair_pass(): pl.pallas_call(kernel, out_shape=jax.ShapeDtypeStruct(out_shape, jnp.floa...  18.5 us
    dot_general x1, matrix products, local(): outgoing = jnp.einsum('fok,okw->fow', windows, shift_map, precision=HIGHEST)  18.2 us
  transfers between devices with their start and end apart: 9, of which 3 were waited for; matrix products, arithmetic and copies ran while one was open for 12% of the time, Pallas kernels for 0%

profile of v5, /device:TPU:25, one launch (start us, length us, event | category | flops | bytes accessed | tf_op | source)
XLA Modules:
  0.0 494.9 jit_solution(11173854684012254904)
XLA Ops:
  3.7 18.2 %fusion.11 = f32[8,64,192]{2,0,1:T(8,128)S(1)} fusion(s32[64,192]{1,0:T(8,128)S(1)} %iota_add_fusion, pred[64,192]{1,0:T(8,128)(4,1)S(1)} %iota_compare_fusion.3, f32[8,64,384]{2,1,0:T(8,128)S(1)} %reshape.381), kind=kOutput, calls=%fused_computation.21 | convolution fusion | flops 462422016 | bytes 1241088 | tf_op jit(solution)/shard_map/fok,okw->fow/dot_general | solution.py:213
  22.9 12.2 %all-to-all-start = ((f32[8,64,192]{2,0,1:T(8,128)}), f32[8,64,192]{2,0,1:T(8,128)S(1)}, u32[]{:S(2)}, u32[]{:S(2)}) async-start(f32[8,64,192]{2,0,1:T(8,128)} %pad_maximum_fusion.3), calls=%async_computation | async-start | bytes 1048576 | tf_op jit(solution)/shard_map/all_to_all | solution.py:216
  36.5 16.2 %all-to-all-done = f32[8,64,192]{2,0,1:T(8,128)S(1)} async-done(((f32[8,64,192]{2,0,1:T(8,128)}), f32[8,64,192]{2,0,1:T(8,128)S(1)}, u32[]{:S(2)}, u32[]{:S(2)}) %all-to-all-start) | async-done | bytes 393248 | tf_op jit(solution)/shard_map/all_to_all | solution.py:216
  53.7 4.0 copy.173
  57.6 37.9 %scatter_custom_fusion = f32[7,32768]{0,1:T(8,128)} fusion(s32[12288]{0:T(1024)S(1)} %bitcast.102, f32[12288,7]{1,0:T(8,128)} %copy.173, f32[]{:T(128)} %constant.87.clone.1), kind=kCustom, calls=%fused_computation.15 | custom fusion | bytes 918016 | tf_op jit(solution)/shard_map/scatter | solution.py:221
  95.6 12.7 %slice_reduce_fusion = f32[32768]{0:T(1024)S(1)} fusion(f32[7,32768]{0,1:T(8,128)} %scatter_custom_fusion), kind=kLoop, calls=%fused_computation.7 | loop fusion | bytes 262144 | tf_op jit(solution)/shard_map/slice | solution.py:225
  108.3 9.9 %fusion.35 = (pred[32768]{0:T(1024)(128)(4,1)S(1)}, pred[1,32768]{0,1:T(8,128)(4,1)}) fusion(f32[7,32768]{0,1:T(8,128)S(1)} %copy-done), kind=kLoop, calls=%fused_computation.97 | loop fusion | flops 32768 | bytes 196608 | tf_op jit(solution)/shard_map/gt | solution.py:165
  118.3 12.4 %fusion.36 = (f32[3,32768]{0,1:T(8,128)}, f32[3,32768]{0,1:T(8,128)}) fusion(f32[7,32768]{0,1:T(8,128)S(1)} %copy-done), kind=kLoop, calls=%fused_computation.98 | loop fusion | bytes 1572864 | tf_op jit(solution)/shard_map/slice | solution.py:241
  130.7 10.0 %copy.177 = f32[3,16,16,128]{3,2,1,0:T(8,128)S(1)} copy(f32[3,16,16,128]{0,3,2,1:T(8,128)} %bitcast.80) | data formatting | bytes 786432 | tf_op jit(solution)/shard_map/slice | solution.py:230
  146.0 9.4 %copy.186 = f32[6,256,128]{2,0,1:T(8,128)S(1)} copy(f32[6,256,128]{0,2,1:T(8,128)} %bitcast.79) | data formatting | bytes 1572864 | tf_op jit(solution)/shard_map/slice | solution.py:254
  155.5 10.0 %copy.188 = f32[3,16,16,128]{3,2,1,0:T(8,128)S(1)} copy(f32[3,16,16,128]{0,3,2,1:T(8,128)} %bitcast.83) | data formatting | bytes 786432 | tf_op jit(solution)/shard_map/slice | solution.py:241
  165.5 9.4 %copy.176 = f32[3,256,128]{2,0,1:T(4,128)S(1)} copy(f32[3,256,128]{0,2,1:T(8,128)} %bitcast.81) | data formatting | bytes 786432 | tf_op jit(solution)/shard_map/slice | solution.py:226
  182.9 4.3 copy.182
  187.1 5.1 %reshape_reshape.2 = f32[4,400,16,8]{1,3,2,0:T(8,128)} reshape(f32[4,20,20,128]{2,1,3,0:T(8,128)} %copy.182) | data formatting | bytes 1638400 | tf_op jit(solution)/shard_map/reshape;reshape | solution.py:53
  194.1 4.4 broadcast_bitcast_fusion.1
  198.4 9.9 %copy.184.near_ref = f32[400,4,8,128]{3,2,1,0:T(8,128)} copy(f32[400,4,8,128]{0,3,2,1:T(8,128)} %broadcast_bitcast_fusion.1) | data formatting | bytes 13107200 | tf_op jit(solution)/shard_map/reshape | solution.py:55
  208.4 7.3 %shard_map.37 = f32[256,1,8,128]{3,2,1,0:T(8,128)} custom-call(s32[6400]{0:T(1024)} %get-tuple-element.18.first_ref, s32[6400]{0:T(1024)} %copy-done.1, s32[1]{0:T(128)} %bitcast.7.count_ref, f32[256,8,128]{2,1,0:T(8,128)} %pad_bitcast_fusion.own_ref, f32[400,4,8,128]{3,2,1,0:T(8,128)} %copy.184.near_ref), custom_call_target="tpu_custom_call" | custom-call | tf_op jit(solution)/shard_map/pallas_call | solution.py:146
  217.2 5.0 %collective-permute-start.4 = (f32[4,2,16,128]{3,2,1,0:T(8,128)S(1)}, f32[4,2,16,128]{3,2,1,0:T(8,128)S(1)}, u32[]{:S(2)}, u32[]{:S(2)}) collective-permute-start(f32[4,2,16,128]{3,2,1,0:T(8,128)S(1)} %get-tuple-element.36), channel_id=1, source_target_pairs={{0,4},{4,8},{8,12},{12,16},{16,20},{20,24},{24,28},{28,32},{32,36}... | collective-permute-start | bytes 196616 | tf_op jit(solution)/shard_map/ppermute | solution.py:30
  224.4 8.3 %copy.201 = f32[1,32768]{0,1:T(8,128)} copy(f32[1,32768]{1,0:T(1,128)S(1)} %bitcast.94) | data formatting | bytes 262144 | tf_op jit(solution)/shard_map/reduce_sum | solution.py:239
  233.0 12.4 %broadcast_select_fusion = f32[1,32768]{0,1:T(8,128)} fusion(pred[1,32768]{0,1:T(8,128)(4,1)} %get-tuple-element.24, f32[1,32768]{0,1:T(8,128)} %copy.201), kind=kLoop, calls=%fused_computation.14 | loop fusion | flops 32768 | bytes 294912 | tf_op jit(solution)/shard_map/jit(_where)/select_n | solution.py:165
  250.2 3.5 concatenate.59
  253.8 18.0 %collective-permute-start.7 = (f32[4,20,2,128]{3,0,2,1:T(4,128)S(1)}, f32[4,20,2,128]{3,0,2,1:T(4,128)S(1)}, u32[]{:S(2)}, u32[]{:S(2)}) collective-permute-start(f32[4,20,2,128]{3,0,2,1:T(4,128)S(1)} %copy.213), channel_id=1, source_target_pairs={{1,0},{2,1},{3,2},{5,4},{6,5},{7,6},{9,8},{10,9},{11,10},{13,12},{... | collective-permute-start | bytes 245768 | tf_op jit(solution)/shard_map/ppermute | solution.py:33
  274.1 4.1 collective-permute-done.6
  294.5 8.8 %broadcast_bitcast_fusion = f32[400,9,8,128]{0,3,2,1:T(8,128)} fusion(f32[400,9,8,16]{0,3,2,1:T(8,128)S(1)} %copy.197), kind=kLoop, calls=%fused_computation.9 | loop fusion | bytes 16588800 | tf_op jit(solution)/shard_map/reshape | solution.py:55
  303.3 17.8 %copy.198.near_ref = f32[400,9,8,128]{3,2,1,0:T(8,128)} copy(f32[400,9,8,128]{0,3,2,1:T(8,128)} %broadcast_bitcast_fusion) | data formatting | bytes 29491200 | tf_op jit(solution)/shard_map/reshape | solution.py:55
  321.1 11.2 %shard_map.38 = f32[256,3,8,128]{3,2,1,0:T(8,128)} custom-call(s32[6400]{0:T(1024)} %get-tuple-element.18.first_ref, s32[6400]{0:T(1024)} %copy-done.1, s32[1]{0:T(128)} %bitcast.7.count_ref, f32[256,8,128]{2,1,0:T(8,128)} %maximum_bitcast_fusion.own_ref, f32[400,9,8,128]{3,2,1,0:T(8,128)} %copy.198.near_ref), custom_call_target="tpu_custom_call" | custom-call | tf_op jit(solution)/shard_map/pallas_call | solution.py:146
  338.3 8.2 %copy.200 = f32[3,256,128]{0,2,1:T(8,128)} copy(f32[3,256,128]{2,0,1:T(4,128)S(1)} %scatter-add.4) | data formatting | bytes 786432 | tf_op jit(solution)/shard_map/scatter-add | solution.py:258
  346.5 17.3 %pad_maximum_fusion = f32[4,32768]{0,1:T(8,128)} fusion(f32[1,32768]{0,1:T(8,128)} %broadcast_select_fusion, f32[3,32768]{0,1:T(8,128)} %bitcast.82), kind=kLoop, calls=%fused_computation.6 | loop fusion | flops 131072 | bytes 1048576 | tf_op jit(solution)/shard_map/concatenate | solution.py:259
  363.8 47.1 %gather_fusion = f32[12288,4]{1,0:T(8,128)} fusion(f32[4,32768]{0,1:T(8,128)} %pad_maximum_fusion, s32[12288]{0:T(1024)S(1)} %broadcast_clamp_fusion), kind=kCustom, calls=%fused_computation | custom fusion | bytes 442368 | tf_op jit(solution)/shard_map/jit(_take)/gather | solution.py:260
  410.9 4.9 copy.202
  415.9 67.6 %all_to_all.10 = f32[4,64,192]{2,0,1:T(4,128)S(1)} all-to-all(f32[4,64,192]{2,0,1:T(4,128)S(1)} %broadcast_select_fusion.1), channel_id=1, replica_groups=mesh['gx'=64,'gy'=4] {'gx'}, dimensions={1} | all-to-all | bytes 393216 | tf_op jit(solution)/shard_map/all_to_all | solution.py:263
  483.5 10.1 %fusion.14 = f32[4,64,384]{2,0,1:T(4,128)S(1)} fusion(s32[64,192]{1,0:T(8,128)S(1)} %iota_add_fusion, pred[64,192]{1,0:T(8,128)(4,1)S(1)} %iota_compare_fusion.3, f32[4,64,192]{2,0,1:T(4,128)S(1)} %all_to_all.10), kind=kOutput, calls=%fused_computation.22 | convolution fusion | flops 235978752 | bytes 651264 | tf_op jit(solution)/shard_map/fow,okw->fok/dot_general | solution.py:264
  (97 shorter events, 56.4 us)
Async XLA Ops:
  1.8 20.0 %copy-start.3 = (s32[192]{0:T(256)}, s32[192]{0:T(256)S(1)}, u32[]{:S(2)}) copy-start(s32[192]{0:T(256)S(1)} %add.127) | copy-start | bytes 2308
  3.7 31.4 %copy-start.2 = (s32[1,2,6400]{2,1,0:T(2,128)S(1)}, s32[1,2,6400]{2,1,0:T(2,128)}, u32[]{:S(2)}) copy-start(s32[1,2,6400]{2,1,0:T(2,128)} %param.7) | copy-start | bytes 153604
  22.9 29.9 %all-to-all-start = ((f32[8,64,192]{2,0,1:T(8,128)}), f32[8,64,192]{2,0,1:T(8,128)S(1)}, u32[]{:S(2)}, u32[]{:S(2)}) async-start(f32[8,64,192]{2,0,1:T(8,128)} %pad_maximum_fusion.3), calls=%async_computation | async-start | bytes 1048576 | tf_op jit(solution)/shard_map/all_to_all | solution.py:216
  35.8 59.7 %copy-start.1 = (s32[6400]{0:T(1024)}, s32[6400]{0:T(1024)S(1)}, u32[]{:S(2)}) copy-start(s32[6400]{0:T(1024)S(1)} %get-tuple-element.17.second_ref) | copy-start | bytes 76804
  95.6 12.8 %copy-start = (f32[7,32768]{0,1:T(8,128)S(1)}, f32[7,32768]{0,1:T(8,128)}, u32[]{:S(2)}) copy-start(f32[7,32768]{0,1:T(8,128)} %scatter_custom_fusion) | copy-start | bytes 2752516
  140.7 34.3 %collective-permute-start = (f32[4,2,16,128]{3,2,1,0:T(8,128)S(1)}, f32[4,2,16,128]{3,2,1,0:T(8,128)S(1)}, u32[]{:S(2)}, u32[]{:S(2)}) collective-permute-start(f32[4,2,16,128]{3,2,1,0:T(8,128)S(1)} %get-tuple-element.38), channel_id=1, source_target_pairs={{0,4},{4,8},{8,12},{12,16},{16,20},{20,24},{24,28},{28,32},{32,36}... | collective-permute-start | bytes 196616 | tf_op jit(solution)/shard_map/ppermute | solution.py:30
  144.1 30.9 %collective-permute-start.1 = (f32[4,2,16,128]{3,2,1,0:T(8,128)S(1)}, f32[4,2,16,128]{3,2,1,0:T(8,128)S(1)}, u32[]{:S(2)}, u32[]{:S(2)}) collective-permute-start(f32[4,2,16,128]{3,2,1,0:T(8,128)S(1)} %get-tuple-element.39), channel_id=1, source_target_pairs={{4,0},{8,4},{12,8},{16,12},{20,16},{24,20},{28,24},{32,28},{36,32}... | collective-permute-start | bytes 196616 | tf_op jit(solution)/shard_map/ppermute | solution.py:33
  175.1 4.7 collective-permute-start.3
  177.5 5.2 %collective-permute-start.2 = (f32[4,20,2,128]{3,0,2,1:T(4,128)S(1)}, f32[4,20,2,128]{3,0,2,1:T(4,128)S(1)}, u32[]{:S(2)}, u32[]{:S(2)}) collective-permute-start(f32[4,20,2,128]{3,0,2,1:T(4,128)S(1)} %copy.210), channel_id=1, source_target_pairs={{0,1},{1,2},{2,3},{4,5},{5,6},{6,7},{8,9},{9,10},{10,11},{12,13},{... | collective-permute-start | bytes 245768 | tf_op jit(solution)/shard_map/ppermute | solution.py:30
  217.2 36.5 %collective-permute-start.4 = (f32[4,2,16,128]{3,2,1,0:T(8,128)S(1)}, f32[4,2,16,128]{3,2,1,0:T(8,128)S(1)}, u32[]{:S(2)}, u32[]{:S(2)}) collective-permute-start(f32[4,2,16,128]{3,2,1,0:T(8,128)S(1)} %get-tuple-element.36), channel_id=1, source_target_pairs={{0,4},{4,8},{8,12},{12,16},{16,20},{20,24},{24,28},{28,32},{32,36}... | collective-permute-start | bytes 196616 | tf_op jit(solution)/shard_map/ppermute | solution.py:30
  222.3 31.4 %collective-permute-start.5 = (f32[4,2,16,128]{3,2,1,0:T(8,128)S(1)}, f32[4,2,16,128]{3,2,1,0:T(8,128)S(1)}, u32[]{:S(2)}, u32[]{:S(2)}) collective-permute-start(f32[4,2,16,128]{3,2,1,0:T(8,128)S(1)} %get-tuple-element.37), channel_id=1, source_target_pairs={{4,0},{8,4},{12,8},{16,12},{20,16},{24,20},{28,24},{32,28},{36,32}... | collective-permute-start | bytes 196616 | tf_op jit(solution)/shard_map/ppermute | solution.py:33
  253.8 20.3 %collective-permute-start.7 = (f32[4,20,2,128]{3,0,2,1:T(4,128)S(1)}, f32[4,20,2,128]{3,0,2,1:T(4,128)S(1)}, u32[]{:S(2)}, u32[]{:S(2)}) collective-permute-start(f32[4,20,2,128]{3,0,2,1:T(4,128)S(1)} %copy.213), channel_id=1, source_target_pairs={{1,0},{2,1},{3,2},{5,4},{6,5},{7,6},{9,8},{10,9},{11,10},{13,12},{... | collective-permute-start | bytes 245768 | tf_op jit(solution)/shard_map/ppermute | solution.py:33
  271.8 6.4 %collective-permute-start.6 = (f32[4,20,2,128]{3,0,2,1:T(4,128)S(1)}, f32[4,20,2,128]{3,0,2,1:T(4,128)S(1)}, u32[]{:S(2)}, u32[]{:S(2)}) collective-permute-start(f32[4,20,2,128]{3,0,2,1:T(4,128)S(1)} %copy.212), channel_id=1, source_target_pairs={{0,1},{1,2},{2,3},{4,5},{5,6},{6,7},{8,9},{9,10},{10,11},{12,13},{... | collective-permute-start | bytes 245768 | tf_op jit(solution)/shard_map/ppermute | solution.py:30
  483.5 10.2 %copy-start.4 = (s32[192]{0:T(256)S(1)}, s32[192]{0:T(256)}, u32[]{:S(2)}) copy-start(s32[192]{0:T(256)} %copy-done.3) | copy-start | bytes 2308

commit v6 on v5

--- a/solution.py
+++ b/solution.py
@@ -105,7 +105,7 @@
             total = total + weight * shifted(mj, step)
         return [total]
 
-    pair_loop(first_ref, second_ref, count_ref, near_ref.shape[0] - 1, contribution, out_ref, 8)
+    pair_loop(first_ref, second_ref, count_ref, near_ref.shape[0] - 1, contribution, out_ref, 16)
 
 
 def force_kernel(first_ref, second_ref, count_ref, own_ref, near_ref, out_ref):
@@ -136,7 +136,7 @@
             acc_z = acc_z + pair_coef * dz
         return [acc_x, acc_y, acc_z]
 
-    pair_loop(first_ref, second_ref, count_ref, near_ref.shape[0] - 1, contribution, out_ref, 8)
+    pair_loop(first_ref, second_ref, count_ref, near_ref.shape[0] - 1, contribution, out_ref, 16)
 
 
 def pair_pass(kernel, first_ids, second_ids, pair_count, own_rows, near_rows, out_depth):

time: 503 us -> 494 us (0.982)
  the two profiles are of different devices: /device:TPU:25 before, /device:TPU:17 now
where the time goes in v6:
time: 494 us; the launch traced here: 487 us
  local copies, waits for them, and re-layouts  258 us (52%)
  Pallas kernels  65.1 us (13%)
  other arithmetic  50.2 us (10%)
  starting transfers between devices  36.5 us (7%)
  blocking collectives  29.5 us (6%)
  matrix products  29.1 us (6%)
  waiting for transfers between devices  17.6 us (4%)
    pallas_call x2, Pallas kernels, pair_pass(): pl.pallas_call(kernel, out_shape=jax.ShapeDtypeStruct(out_shape, jnp.floa...  65.1 us
    gather x2, local copies, waits for them, and re-layouts, local(): jnp.take(results, jnp.minimum(arrived_slot, slots_all - 1), axis=1)  52 us
    reshape x4, local copies, waits for them, and re-layouts, expand_cells(): return wide.reshape(pencil_count, depth, CAP, NZ * CAP)  41 us
    scatter x1, local copies, waits for them, and re-layouts, local(): own_grid = jnp.zeros((7, slots_all), jnp.float32).at[:, arrived_slot].set...  37.9 us
    all_to_all x1, blocking collectives, local(): lax.all_to_all(reply, 'gx', split_axis=1, concat_axis=1, tiled=True)  29.5 us
    slice x2, local copies, waits for them, and re-layouts, local(): own_grid[3:6]  22.4 us
    dot_general x1, matrix products, local(): outgoing = jnp.einsum('fok,okw->fow', windows, shift_map, precision=HIGHEST)  18.2 us
    concatenate x1, other arithmetic, local(): jnp.concatenate([accel, density_own[None]], axis=0).reshape(4, slots_all)  17.3 us
  transfers between devices with their start and end apart: 9, of which 3 were waited for; matrix products, arithmetic and copies ran while one was open for 13% of the time, Pallas kernels for 0%

profile of v6, /device:TPU:17, one launch (start us, length us, event | category | flops | bytes accessed | tf_op | source)
XLA Modules:
  0.0 486.8 jit_solution(8554461693774105068)
XLA Ops:
  3.7 18.2 %fusion.11 = f32[8,64,192]{2,0,1:T(8,128)S(1)} fusion(s32[64,192]{1,0:T(8,128)S(1)} %iota_add_fusion, pred[64,192]{1,0:T(8,128)(4,1)S(1)} %iota_compare_fusion.3, f32[8,64,384]{2,1,0:T(8,128)S(1)} %reshape.381), kind=kOutput, calls=%fused_computation.21 | convolution fusion | flops 462422016 | bytes 1241088 | tf_op jit(solution)/shard_map/fok,okw->fow/dot_general | solution.py:213
  22.9 12.2 %all-to-all-start = ((f32[8,64,192]{2,0,1:T(8,128)}), f32[8,64,192]{2,0,1:T(8,128)S(1)}, u32[]{:S(2)}, u32[]{:S(2)}) async-start(f32[8,64,192]{2,0,1:T(8,128)} %pad_maximum_fusion.3), calls=%async_computation | async-start | bytes 1048576 | tf_op jit(solution)/shard_map/all_to_all | solution.py:216
  36.5 16.2 %all-to-all-done = f32[8,64,192]{2,0,1:T(8,128)S(1)} async-done(((f32[8,64,192]{2,0,1:T(8,128)}), f32[8,64,192]{2,0,1:T(8,128)S(1)}, u32[]{:S(2)}, u32[]{:S(2)}) %all-to-all-start) | async-done | bytes 393248 | tf_op jit(solution)/shard_map/all_to_all | solution.py:216
  53.7 4.0 copy.173
  57.6 37.9 %scatter_custom_fusion = f32[7,32768]{0,1:T(8,128)} fusion(s32[12288]{0:T(1024)S(1)} %bitcast.102, f32[12288,7]{1,0:T(8,128)} %copy.173, f32[]{:T(128)} %constant.87.clone.1), kind=kCustom, calls=%fused_computation.15 | custom fusion | bytes 918016 | tf_op jit(solution)/shard_map/scatter | solution.py:221
  95.6 12.7 %slice_reduce_fusion = f32[32768]{0:T(1024)S(1)} fusion(f32[7,32768]{0,1:T(8,128)} %scatter_custom_fusion), kind=kLoop, calls=%fused_computation.7 | loop fusion | bytes 262144 | tf_op jit(solution)/shard_map/slice | solution.py:225
  108.3 9.9 %fusion.35 = (pred[32768]{0:T(1024)(128)(4,1)S(1)}, pred[1,32768]{0,1:T(8,128)(4,1)}) fusion(f32[7,32768]{0,1:T(8,128)S(1)} %copy-done), kind=kLoop, calls=%fused_computation.97 | loop fusion | flops 32768 | bytes 196608 | tf_op jit(solution)/shard_map/gt | solution.py:165
  118.3 12.4 %fusion.36 = (f32[3,32768]{0,1:T(8,128)}, f32[3,32768]{0,1:T(8,128)}) fusion(f32[7,32768]{0,1:T(8,128)S(1)} %copy-done), kind=kLoop, calls=%fused_computation.98 | loop fusion | bytes 1572864 | tf_op jit(solution)/shard_map/slice | solution.py:241
  130.7 10.0 %copy.177 = f32[3,16,16,128]{3,2,1,0:T(8,128)S(1)} copy(f32[3,16,16,128]{0,3,2,1:T(8,128)} %bitcast.80) | data formatting | bytes 786432 | tf_op jit(solution)/shard_map/slice | solution.py:230
  146.0 9.4 %copy.186 = f32[6,256,128]{2,0,1:T(8,128)S(1)} copy(f32[6,256,128]{0,2,1:T(8,128)} %bitcast.79) | data formatting | bytes 1572864 | tf_op jit(solution)/shard_map/slice | solution.py:254
  155.5 10.0 %copy.188 = f32[3,16,16,128]{3,2,1,0:T(8,128)S(1)} copy(f32[3,16,16,128]{0,3,2,1:T(8,128)} %bitcast.83) | data formatting | bytes 786432 | tf_op jit(solution)/shard_map/slice | solution.py:241
  165.5 9.4 %copy.176 = f32[3,256,128]{2,0,1:T(4,128)S(1)} copy(f32[3,256,128]{0,2,1:T(8,128)} %bitcast.81) | data formatting | bytes 786432 | tf_op jit(solution)/shard_map/slice | solution.py:226
  182.6 4.3 copy.182
  186.8 5.1 %reshape_reshape.2 = f32[4,400,16,8]{1,3,2,0:T(8,128)} reshape(f32[4,20,20,128]{2,1,3,0:T(8,128)} %copy.182) | data formatting | bytes 1638400 | tf_op jit(solution)/shard_map/reshape;reshape | solution.py:53
  193.8 4.4 broadcast_bitcast_fusion.1
  198.2 9.9 %copy.184.near_ref = f32[400,4,8,128]{3,2,1,0:T(8,128)} copy(f32[400,4,8,128]{0,3,2,1:T(8,128)} %broadcast_bitcast_fusion.1) | data formatting | bytes 13107200 | tf_op jit(solution)/shard_map/reshape | solution.py:55
  208.1 23.0 %shard_map.37 = f32[256,1,8,128]{3,2,1,0:T(8,128)} custom-call(s32[6400]{0:T(1024)} %get-tuple-element.18.first_ref, s32[6400]{0:T(1024)} %copy-done.1, s32[1]{0:T(128)} %bitcast.7.count_ref, f32[256,8,128]{2,1,0:T(8,128)} %pad_bitcast_fusion.own_ref, f32[400,4,8,128]{3,2,1,0:T(8,128)} %copy.184.near_ref), custom_call_target="tpu_custom_call" | custom-call | tf_op jit(solution)/shard_map/pallas_call | solution.py:146
  232.6 5.4 %collective-permute-start.4 = (f32[4,2,16,128]{3,2,1,0:T(8,128)S(1)}, f32[4,2,16,128]{3,2,1,0:T(8,128)S(1)}, u32[]{:S(2)}, u32[]{:S(2)}) collective-permute-start(f32[4,2,16,128]{3,2,1,0:T(8,128)S(1)} %get-tuple-element.36), channel_id=1, source_target_pairs={{0,4},{4,8},{8,12},{12,16},{16,20},{20,24},{24,28},{28,32},{32,36}... | collective-permute-start | bytes 196616 | tf_op jit(solution)/shard_map/ppermute | solution.py:30
  240.1 8.3 %copy.201 = f32[1,32768]{0,1:T(8,128)} copy(f32[1,32768]{1,0:T(1,128)S(1)} %bitcast.94) | data formatting | bytes 262144 | tf_op jit(solution)/shard_map/reduce_sum | solution.py:239
  248.7 12.4 %broadcast_select_fusion = f32[1,32768]{0,1:T(8,128)} fusion(pred[1,32768]{0,1:T(8,128)(4,1)} %get-tuple-element.24, f32[1,32768]{0,1:T(8,128)} %copy.201), kind=kLoop, calls=%fused_computation.14 | loop fusion | flops 32768 | bytes 294912 | tf_op jit(solution)/shard_map/jit(_where)/select_n | solution.py:165
  265.9 3.5 concatenate.59
  271.5 4.3 collective-permute-start.6
  283.9 3.5 concatenate.63
  293.6 8.8 %broadcast_bitcast_fusion = f32[400,9,8,128]{0,3,2,1:T(8,128)} fusion(f32[400,9,8,16]{0,3,2,1:T(8,128)S(1)} %copy.197), kind=kLoop, calls=%fused_computation.9 | loop fusion | bytes 16588800 | tf_op jit(solution)/shard_map/reshape | solution.py:55
  302.4 17.8 %copy.198.near_ref = f32[400,9,8,128]{3,2,1,0:T(8,128)} copy(f32[400,9,8,128]{0,3,2,1:T(8,128)} %broadcast_bitcast_fusion) | data formatting | bytes 29491200 | tf_op jit(solution)/shard_map/reshape | solution.py:55
  320.2 42.1 %shard_map.38 = f32[256,3,8,128]{3,2,1,0:T(8,128)} custom-call(s32[6400]{0:T(1024)} %get-tuple-element.18.first_ref, s32[6400]{0:T(1024)} %copy-done.1, s32[1]{0:T(128)} %bitcast.7.count_ref, f32[256,8,128]{2,1,0:T(8,128)} %maximum_bitcast_fusion.own_ref, f32[400,9,8,128]{3,2,1,0:T(8,128)} %copy.198.near_ref), custom_call_target="tpu_custom_call" | custom-call | tf_op jit(solution)/shard_map/pallas_call | solution.py:146
  368.3 8.2 %copy.200 = f32[3,256,128]{0,2,1:T(8,128)} copy(f32[3,256,128]{2,0,1:T(4,128)S(1)} %scatter-add.4) | data formatting | bytes 786432 | tf_op jit(solution)/shard_map/scatter-add | solution.py:258
  376.5 17.3 %pad_maximum_fusion = f32[4,32768]{0,1:T(8,128)} fusion(f32[1,32768]{0,1:T(8,128)} %broadcast_select_fusion, f32[3,32768]{0,1:T(8,128)} %bitcast.82), kind=kLoop, calls=%fused_computation.6 | loop fusion | flops 131072 | bytes 1048576 | tf_op jit(solution)/shard_map/concatenate | solution.py:259
  393.8 47.1 %gather_fusion = f32[12288,4]{1,0:T(8,128)} fusion(f32[4,32768]{0,1:T(8,128)} %pad_maximum_fusion, s32[12288]{0:T(1024)S(1)} %broadcast_clamp_fusion), kind=kCustom, calls=%fused_computation | custom fusion | bytes 442368 | tf_op jit(solution)/shard_map/jit(_take)/gather | solution.py:260
  440.9 4.9 %copy.202 = f32[4,64,192]{2,0,1:T(4,128)S(1)} copy(f32[4,64,192]{0,2,1:T(8,128)} %bitcast.84) | data formatting | bytes 393216 | tf_op jit(solution)/shard_map/jit(_take)/gather | solution.py:260
  445.9 29.5 %all_to_all.10 = f32[4,64,192]{2,0,1:T(4,128)S(1)} all-to-all(f32[4,64,192]{2,0,1:T(4,128)S(1)} %broadcast_select_fusion.1), channel_id=1, replica_groups=mesh['gx'=64,'gy'=4] {'gx'}, dimensions={1} | all-to-all | bytes 393216 | tf_op jit(solution)/shard_map/all_to_all | solution.py:263
  475.4 10.1 %fusion.14 = f32[4,64,384]{2,0,1:T(4,128)S(1)} fusion(s32[64,192]{1,0:T(8,128)S(1)} %iota_add_fusion, pred[64,192]{1,0:T(8,128)(4,1)S(1)} %iota_compare_fusion.3, f32[4,64,192]{2,0,1:T(4,128)S(1)} %all_to_all.10), kind=kOutput, calls=%fused_computation.22 | convolution fusion | flops 235978752 | bytes 651264 | tf_op jit(solution)/shard_map/fow,okw->fok/dot_general | solution.py:264
  (97 shorter events, 53.7 us)
Async XLA Ops:
  1.8 20.0 %copy-start.3 = (s32[192]{0:T(256)}, s32[192]{0:T(256)S(1)}, u32[]{:S(2)}) copy-start(s32[192]{0:T(256)S(1)} %add.127) | copy-start | bytes 2308
  3.7 31.4 %copy-start.2 = (s32[1,2,6400]{2,1,0:T(2,128)S(1)}, s32[1,2,6400]{2,1,0:T(2,128)}, u32[]{:S(2)}) copy-start(s32[1,2,6400]{2,1,0:T(2,128)} %param.7) | copy-start | bytes 153604
  22.9 29.9 %all-to-all-start = ((f32[8,64,192]{2,0,1:T(8,128)}), f32[8,64,192]{2,0,1:T(8,128)S(1)}, u32[]{:S(2)}, u32[]{:S(2)}) async-start(f32[8,64,192]{2,0,1:T(8,128)} %pad_maximum_fusion.3), calls=%async_computation | async-start | bytes 1048576 | tf_op jit(solution)/shard_map/all_to_all | solution.py:216
  35.8 59.7 %copy-start.1 = (s32[6400]{0:T(1024)}, s32[6400]{0:T(1024)S(1)}, u32[]{:S(2)}) copy-start(s32[6400]{0:T(1024)S(1)} %get-tuple-element.17.second_ref) | copy-start | bytes 76804
  95.6 12.8 %copy-start = (f32[7,32768]{0,1:T(8,128)S(1)}, f32[7,32768]{0,1:T(8,128)}, u32[]{:S(2)}) copy-start(f32[7,32768]{0,1:T(8,128)} %scatter_custom_fusion) | copy-start | bytes 2752516
  140.7 34.3 %collective-permute-start = (f32[4,2,16,128]{3,2,1,0:T(8,128)S(1)}, f32[4,2,16,128]{3,2,1,0:T(8,128)S(1)}, u32[]{:S(2)}, u32[]{:S(2)}) collective-permute-start(f32[4,2,16,128]{3,2,1,0:T(8,128)S(1)} %get-tuple-element.38), channel_id=1, source_target_pairs={{0,4},{4,8},{8,12},{12,16},{16,20},{20,24},{24,28},{28,32},{32,36}... | collective-permute-start | bytes 196616 | tf_op jit(solution)/shard_map/ppermute | solution.py:30
  144.1 30.9 %collective-permute-start.1 = (f32[4,2,16,128]{3,2,1,0:T(8,128)S(1)}, f32[4,2,16,128]{3,2,1,0:T(8,128)S(1)}, u32[]{:S(2)}, u32[]{:S(2)}) collective-permute-start(f32[4,2,16,128]{3,2,1,0:T(8,128)S(1)} %get-tuple-element.39), channel_id=1, source_target_pairs={{4,0},{8,4},{12,8},{16,12},{20,16},{24,20},{28,24},{32,28},{36,32}... | collective-permute-start | bytes 196616 | tf_op jit(solution)/shard_map/ppermute | solution.py:33
  175.1 6.3 %collective-permute-start.3 = (f32[4,20,2,128]{3,0,2,1:T(4,128)S(1)}, f32[4,20,2,128]{3,0,2,1:T(4,128)S(1)}, u32[]{:S(2)}, u32[]{:S(2)}) collective-permute-start(f32[4,20,2,128]{3,0,2,1:T(4,128)S(1)} %copy.211), channel_id=1, source_target_pairs={{1,0},{2,1},{3,2},{5,4},{6,5},{7,6},{9,8},{10,9},{11,10},{13,12},{... | collective-permute-start | bytes 245768 | tf_op jit(solution)/shard_map/ppermute | solution.py:33
  177.2 5.2 %collective-permute-start.2 = (f32[4,20,2,128]{3,0,2,1:T(4,128)S(1)}, f32[4,20,2,128]{3,0,2,1:T(4,128)S(1)}, u32[]{:S(2)}, u32[]{:S(2)}) collective-permute-start(f32[4,20,2,128]{3,0,2,1:T(4,128)S(1)} %copy.210), channel_id=1, source_target_pairs={{0,1},{1,2},{2,3},{4,5},{5,6},{6,7},{8,9},{9,10},{10,11},{12,13},{... | collective-permute-start | bytes 245768 | tf_op jit(solution)/shard_map/ppermute | solution.py:30
  232.6 36.8 %collective-permute-start.4 = (f32[4,2,16,128]{3,2,1,0:T(8,128)S(1)}, f32[4,2,16,128]{3,2,1,0:T(8,128)S(1)}, u32[]{:S(2)}, u32[]{:S(2)}) collective-permute-start(f32[4,2,16,128]{3,2,1,0:T(8,128)S(1)} %get-tuple-element.36), channel_id=1, source_target_pairs={{0,4},{4,8},{8,12},{12,16},{16,20},{20,24},{24,28},{28,32},{32,36}... | collective-permute-start | bytes 196616 | tf_op jit(solution)/shard_map/ppermute | solution.py:30
  238.0 31.4 %collective-permute-start.5 = (f32[4,2,16,128]{3,2,1,0:T(8,128)S(1)}, f32[4,2,16,128]{3,2,1,0:T(8,128)S(1)}, u32[]{:S(2)}, u32[]{:S(2)}) collective-permute-start(f32[4,2,16,128]{3,2,1,0:T(8,128)S(1)} %get-tuple-element.37), channel_id=1, source_target_pairs={{4,0},{8,4},{12,8},{16,12},{20,16},{24,20},{28,24},{32,28},{36,32}... | collective-permute-start | bytes 196616 | tf_op jit(solution)/shard_map/ppermute | solution.py:33
  269.6 7.2 %collective-permute-start.7 = (f32[4,20,2,128]{3,0,2,1:T(4,128)S(1)}, f32[4,20,2,128]{3,0,2,1:T(4,128)S(1)}, u32[]{:S(2)}, u32[]{:S(2)}) collective-permute-start(f32[4,20,2,128]{3,0,2,1:T(4,128)S(1)} %copy.213), channel_id=1, source_target_pairs={{1,0},{2,1},{3,2},{5,4},{6,5},{7,6},{9,8},{10,9},{11,10},{13,12},{... | collective-permute-start | bytes 245768 | tf_op jit(solution)/shard_map/ppermute | solution.py:33
  271.5 5.8 %collective-permute-start.6 = (f32[4,20,2,128]{3,0,2,1:T(4,128)S(1)}, f32[4,20,2,128]{3,0,2,1:T(4,128)S(1)}, u32[]{:S(2)}, u32[]{:S(2)}) collective-permute-start(f32[4,20,2,128]{3,0,2,1:T(4,128)S(1)} %copy.212), channel_id=1, source_target_pairs={{0,1},{1,2},{2,3},{4,5},{5,6},{6,7},{8,9},{9,10},{10,11},{12,13},{... | collective-permute-start | bytes 245768 | tf_op jit(solution)/shard_map/ppermute | solution.py:30
  475.4 10.2 %copy-start.4 = (s32[192]{0:T(256)S(1)}, s32[192]{0:T(256)}, u32[]{:S(2)}) copy-start(s32[192]{0:T(256)} %copy-done.3) | copy-start | bytes 2308

commit v7 on v6

--- a/solution.py
+++ b/solution.py
@@ -105,7 +105,7 @@
             total = total + weight * shifted(mj, step)
         return [total]
 
-    pair_loop(first_ref, second_ref, count_ref, near_ref.shape[0] - 1, contribution, out_ref, 16)
+    pair_loop(first_ref, second_ref, count_ref, near_ref.shape[0] - 1, contribution, out_ref, 32)
 
 
 def force_kernel(first_ref, second_ref, count_ref, own_ref, near_ref, out_ref):
@@ -136,7 +136,7 @@
             acc_z = acc_z + pair_coef * dz
         return [acc_x, acc_y, acc_z]
 
-    pair_loop(first_ref, second_ref, count_ref, near_ref.shape[0] - 1, contribution, out_ref, 16)
+    pair_loop(first_ref, second_ref, count_ref, near_ref.shape[0] - 1, contribution, out_ref, 32)
 
 
 def pair_pass(kernel, first_ids, second_ids, pair_count, own_rows, near_rows, out_depth):

time: 494 us -> 487 us (0.986)
  the two profiles are of different devices: /device:TPU:17 before, /device:TPU:1 now
where the time goes in v7:
time: 487 us; the launch traced here: 480 us
  local copies, waits for them, and re-layouts  258 us (53%)
  blocking collectives  55 us (11%)
  other arithmetic  50.2 us (10%)
  starting transfers between devices  49.5 us (10%)
  matrix products  29.1 us (6%)
  Pallas kernels  20 us (4%)
  waiting for transfers between devices  17.1 us (4%)
    all_to_all x1, blocking collectives, local(): lax.all_to_all(reply, 'gx', split_axis=1, concat_axis=1, tiled=True)  55 us
    gather x2, local copies, waits for them, and re-layouts, local(): jnp.take(results, jnp.minimum(arrived_slot, slots_all - 1), axis=1)  52 us
    reshape x4, local copies, waits for them, and re-layouts, expand_cells(): return wide.reshape(pencil_count, depth, CAP, NZ * CAP)  41 us
    scatter x1, local copies, waits for them, and re-layouts, local(): own_grid = jnp.zeros((7, slots_all), jnp.float32).at[:, arrived_slot].set...  37.9 us
    ppermute x4, starting transfers between devices, extended(): lax.ppermute(lax.slice_in_dim(block, block.shape[dim] - width, None, axis...  30.1 us
    slice x2, local copies, waits for them, and re-layouts, local(): own_grid[3:6]  22.4 us
    pallas_call x2, Pallas kernels, pair_pass(): pl.pallas_call(kernel, out_shape=jax.ShapeDtypeStruct(out_shape, jnp.floa...  20 us
    dot_general x1, matrix products, local(): outgoing = jnp.einsum('fok,okw->fow', windows, shift_map, precision=HIGHEST)  18.2 us
  transfers between devices with their start and end apart: 9, of which 3 were waited for; matrix products, arithmetic and copies ran while one was open for 13% of the time, Pallas kernels for 0%

profile of v7, /device:TPU:1, one launch (start us, length us, event | category | flops | bytes accessed | tf_op | source)
XLA Modules:
  0.0 479.7 jit_solution(4585565406222649208)
XLA Ops:
  3.7 18.2 %fusion.11 = f32[8,64,192]{2,0,1:T(8,128)S(1)} fusion(s32[64,192]{1,0:T(8,128)S(1)} %iota_add_fusion, pred[64,192]{1,0:T(8,128)(4,1)S(1)} %iota_compare_fusion.3, f32[8,64,384]{2,1,0:T(8,128)S(1)} %reshape.381), kind=kOutput, calls=%fused_computation.21 | convolution fusion | flops 462422016 | bytes 1241088 | tf_op jit(solution)/shard_map/fok,okw->fow/dot_general | solution.py:213
  22.9 13.0 %all-to-all-start = ((f32[8,64,192]{2,0,1:T(8,128)}), f32[8,64,192]{2,0,1:T(8,128)S(1)}, u32[]{:S(2)}, u32[]{:S(2)}) async-start(f32[8,64,192]{2,0,1:T(8,128)} %pad_maximum_fusion.3), calls=%async_computation | async-start | bytes 1048576 | tf_op jit(solution)/shard_map/all_to_all | solution.py:216
  37.4 16.2 %all-to-all-done = f32[8,64,192]{2,0,1:T(8,128)S(1)} async-done(((f32[8,64,192]{2,0,1:T(8,128)}), f32[8,64,192]{2,0,1:T(8,128)S(1)}, u32[]{:S(2)}, u32[]{:S(2)}) %all-to-all-start) | async-done | bytes 393248 | tf_op jit(solution)/shard_map/all_to_all | solution.py:216
  54.5 4.0 copy.173
  58.4 37.9 %scatter_custom_fusion = f32[7,32768]{0,1:T(8,128)} fusion(s32[12288]{0:T(1024)S(1)} %bitcast.102, f32[12288,7]{1,0:T(8,128)} %copy.173, f32[]{:T(128)} %constant.87.clone.1), kind=kCustom, calls=%fused_computation.15 | custom fusion | bytes 918016 | tf_op jit(solution)/shard_map/scatter | solution.py:221
  96.4 12.7 %slice_reduce_fusion = f32[32768]{0:T(1024)S(1)} fusion(f32[7,32768]{0,1:T(8,128)} %scatter_custom_fusion), kind=kLoop, calls=%fused_computation.7 | loop fusion | bytes 262144 | tf_op jit(solution)/shard_map/slice | solution.py:225
  109.2 9.9 %fusion.35 = (pred[32768]{0:T(1024)(128)(4,1)S(1)}, pred[1,32768]{0,1:T(8,128)(4,1)}) fusion(f32[7,32768]{0,1:T(8,128)S(1)} %copy-done), kind=kLoop, calls=%fused_computation.97 | loop fusion | flops 32768 | bytes 196608 | tf_op jit(solution)/shard_map/gt | solution.py:165
  119.1 12.4 %fusion.36 = (f32[3,32768]{0,1:T(8,128)}, f32[3,32768]{0,1:T(8,128)}) fusion(f32[7,32768]{0,1:T(8,128)S(1)} %copy-done), kind=kLoop, calls=%fused_computation.98 | loop fusion | bytes 1572864 | tf_op jit(solution)/shard_map/slice | solution.py:241
  131.5 10.0 %copy.177 = f32[3,16,16,128]{3,2,1,0:T(8,128)S(1)} copy(f32[3,16,16,128]{0,3,2,1:T(8,128)} %bitcast.80) | data formatting | bytes 786432 | tf_op jit(solution)/shard_map/slice | solution.py:230
  146.8 9.4 %copy.186 = f32[6,256,128]{2,0,1:T(8,128)S(1)} copy(f32[6,256,128]{0,2,1:T(8,128)} %bitcast.79) | data formatting | bytes 1572864 | tf_op jit(solution)/shard_map/slice | solution.py:254
  156.3 10.0 %copy.188 = f32[3,16,16,128]{3,2,1,0:T(8,128)S(1)} copy(f32[3,16,16,128]{0,3,2,1:T(8,128)} %bitcast.83) | data formatting | bytes 786432 | tf_op jit(solution)/shard_map/slice | solution.py:241
  166.3 9.4 %copy.176 = f32[3,256,128]{2,0,1:T(4,128)S(1)} copy(f32[3,256,128]{0,2,1:T(8,128)} %bitcast.81) | data formatting | bytes 786432 | tf_op jit(solution)/shard_map/slice | solution.py:226
  177.2 4.0 collective-permute-start.2
  182.9 4.3 copy.182
  187.1 5.1 %reshape_reshape.2 = f32[4,400,16,8]{1,3,2,0:T(8,128)} reshape(f32[4,20,20,128]{2,1,3,0:T(8,128)} %copy.182) | data formatting | bytes 1638400 | tf_op jit(solution)/shard_map/reshape;reshape | solution.py:53
  194.1 4.4 broadcast_bitcast_fusion.1
  198.4 9.9 %copy.184.near_ref = f32[400,4,8,128]{3,2,1,0:T(8,128)} copy(f32[400,4,8,128]{0,3,2,1:T(8,128)} %broadcast_bitcast_fusion.1) | data formatting | bytes 13107200 | tf_op jit(solution)/shard_map/reshape | solution.py:55
  208.4 7.7 %shard_map.37 = f32[256,1,8,128]{3,2,1,0:T(8,128)} custom-call(s32[6400]{0:T(1024)} %get-tuple-element.18.first_ref, s32[6400]{0:T(1024)} %copy-done.1, s32[1]{0:T(128)} %bitcast.7.count_ref, f32[256,8,128]{2,1,0:T(8,128)} %pad_bitcast_fusion.own_ref, f32[400,4,8,128]{3,2,1,0:T(8,128)} %copy.184.near_ref), custom_call_target="tpu_custom_call" | custom-call | tf_op jit(solution)/shard_map/pallas_call | solution.py:146
  217.6 18.1 %collective-permute-start.4 = (f32[4,2,16,128]{3,2,1,0:T(8,128)S(1)}, f32[4,2,16,128]{3,2,1,0:T(8,128)S(1)}, u32[]{:S(2)}, u32[]{:S(2)}) collective-permute-start(f32[4,2,16,128]{3,2,1,0:T(8,128)S(1)} %get-tuple-element.36), channel_id=1, source_target_pairs={{0,4},{4,8},{8,12},{12,16},{16,20},{20,24},{24,28},{28,32},{32,36}... | collective-permute-start | bytes 196616 | tf_op jit(solution)/shard_map/ppermute | solution.py:30
  237.7 8.3 %copy.201 = f32[1,32768]{0,1:T(8,128)} copy(f32[1,32768]{1,0:T(1,128)S(1)} %bitcast.94) | data formatting | bytes 262144 | tf_op jit(solution)/shard_map/reduce_sum | solution.py:239
  246.3 12.4 %broadcast_select_fusion = f32[1,32768]{0,1:T(8,128)} fusion(pred[1,32768]{0,1:T(8,128)(4,1)} %get-tuple-element.24, f32[1,32768]{0,1:T(8,128)} %copy.201), kind=kLoop, calls=%fused_computation.14 | loop fusion | flops 32768 | bytes 294912 | tf_op jit(solution)/shard_map/jit(_where)/select_n | solution.py:165
  263.5 3.5 concatenate.59
  268.4 4.6 collective-permute-start.6
  290.8 8.8 %broadcast_bitcast_fusion = f32[400,9,8,128]{0,3,2,1:T(8,128)} fusion(f32[400,9,8,16]{0,3,2,1:T(8,128)S(1)} %copy.197), kind=kLoop, calls=%fused_computation.9 | loop fusion | bytes 16588800 | tf_op jit(solution)/shard_map/reshape | solution.py:55
  299.6 17.8 %copy.198.near_ref = f32[400,9,8,128]{3,2,1,0:T(8,128)} copy(f32[400,9,8,128]{0,3,2,1:T(8,128)} %broadcast_bitcast_fusion) | data formatting | bytes 29491200 | tf_op jit(solution)/shard_map/reshape | solution.py:55
  317.5 12.3 %shard_map.38 = f32[256,3,8,128]{3,2,1,0:T(8,128)} custom-call(s32[6400]{0:T(1024)} %get-tuple-element.18.first_ref, s32[6400]{0:T(1024)} %copy-done.1, s32[1]{0:T(128)} %bitcast.7.count_ref, f32[256,8,128]{2,1,0:T(8,128)} %maximum_bitcast_fusion.own_ref, f32[400,9,8,128]{3,2,1,0:T(8,128)} %copy.198.near_ref), custom_call_target="tpu_custom_call" | custom-call | tf_op jit(solution)/shard_map/pallas_call | solution.py:146
  335.7 8.2 %copy.200 = f32[3,256,128]{0,2,1:T(8,128)} copy(f32[3,256,128]{2,0,1:T(4,128)S(1)} %scatter-add.4) | data formatting | bytes 786432 | tf_op jit(solution)/shard_map/scatter-add | solution.py:258
  343.9 17.3 %pad_maximum_fusion = f32[4,32768]{0,1:T(8,128)} fusion(f32[1,32768]{0,1:T(8,128)} %broadcast_select_fusion, f32[3,32768]{0,1:T(8,128)} %bitcast.82), kind=kLoop, calls=%fused_computation.6 | loop fusion | flops 131072 | bytes 1048576 | tf_op jit(solution)/shard_map/concatenate | solution.py:259
  361.2 47.1 %gather_fusion = f32[12288,4]{1,0:T(8,128)} fusion(f32[4,32768]{0,1:T(8,128)} %pad_maximum_fusion, s32[12288]{0:T(1024)S(1)} %broadcast_clamp_fusion), kind=kCustom, calls=%fused_computation | custom fusion | bytes 442368 | tf_op jit(solution)/shard_map/jit(_take)/gather | solution.py:260
  408.3 4.9 %copy.202 = f32[4,64,192]{2,0,1:T(4,128)S(1)} copy(f32[4,64,192]{0,2,1:T(8,128)} %bitcast.84) | data formatting | bytes 393216 | tf_op jit(solution)/shard_map/jit(_take)/gather | solution.py:260
  413.3 55.0 %all_to_all.10 = f32[4,64,192]{2,0,1:T(4,128)S(1)} all-to-all(f32[4,64,192]{2,0,1:T(4,128)S(1)} %broadcast_select_fusion.1), channel_id=1, replica_groups=mesh['gx'=64,'gy'=4] {'gx'}, dimensions={1} | all-to-all | bytes 393216 | tf_op jit(solution)/shard_map/all_to_all | solution.py:263
  468.3 10.1 %fusion.14 = f32[4,64,384]{2,0,1:T(4,128)S(1)} fusion(s32[64,192]{1,0:T(8,128)S(1)} %iota_add_fusion, pred[64,192]{1,0:T(8,128)(4,1)S(1)} %iota_compare_fusion.3, f32[4,64,192]{2,0,1:T(4,128)S(1)} %all_to_all.10), kind=kOutput, calls=%fused_computation.22 | convolution fusion | flops 235978752 | bytes 651264 | tf_op jit(solution)/shard_map/fow,okw->fok/dot_general | solution.py:264
  (97 shorter events, 51.9 us)
Async XLA Ops:
  1.8 20.0 %copy-start.3 = (s32[192]{0:T(256)}, s32[192]{0:T(256)S(1)}, u32[]{:S(2)}) copy-start(s32[192]{0:T(256)S(1)} %add.127) | copy-start | bytes 2308
  3.7 32.3 %copy-start.2 = (s32[1,2,6400]{2,1,0:T(2,128)S(1)}, s32[1,2,6400]{2,1,0:T(2,128)}, u32[]{:S(2)}) copy-start(s32[1,2,6400]{2,1,0:T(2,128)} %param.7) | copy-start | bytes 153604
  22.9 30.7 %all-to-all-start = ((f32[8,64,192]{2,0,1:T(8,128)}), f32[8,64,192]{2,0,1:T(8,128)S(1)}, u32[]{:S(2)}, u32[]{:S(2)}) async-start(f32[8,64,192]{2,0,1:T(8,128)} %pad_maximum_fusion.3), calls=%async_computation | async-start | bytes 1048576 | tf_op jit(solution)/shard_map/all_to_all | solution.py:216
  36.7 59.7 %copy-start.1 = (s32[6400]{0:T(1024)}, s32[6400]{0:T(1024)S(1)}, u32[]{:S(2)}) copy-start(s32[6400]{0:T(1024)S(1)} %get-tuple-element.17.second_ref) | copy-start | bytes 76804
  96.4 12.8 %copy-start = (f32[7,32768]{0,1:T(8,128)S(1)}, f32[7,32768]{0,1:T(8,128)}, u32[]{:S(2)}) copy-start(f32[7,32768]{0,1:T(8,128)} %scatter_custom_fusion) | copy-start | bytes 2752516
  141.5 34.3 %collective-permute-start = (f32[4,2,16,128]{3,2,1,0:T(8,128)S(1)}, f32[4,2,16,128]{3,2,1,0:T(8,128)S(1)}, u32[]{:S(2)}, u32[]{:S(2)}) collective-permute-start(f32[4,2,16,128]{3,2,1,0:T(8,128)S(1)} %get-tuple-element.38), channel_id=1, source_target_pairs={{0,4},{4,8},{8,12},{12,16},{16,20},{20,24},{24,28},{28,32},{32,36}... | collective-permute-start | bytes 196616 | tf_op jit(solution)/shard_map/ppermute | solution.py:30
  144.9 30.9 %collective-permute-start.1 = (f32[4,2,16,128]{3,2,1,0:T(8,128)S(1)}, f32[4,2,16,128]{3,2,1,0:T(8,128)S(1)}, u32[]{:S(2)}, u32[]{:S(2)}) collective-permute-start(f32[4,2,16,128]{3,2,1,0:T(8,128)S(1)} %get-tuple-element.39), channel_id=1, source_target_pairs={{4,0},{8,4},{12,8},{16,12},{20,16},{24,20},{28,24},{32,28},{36,32}... | collective-permute-start | bytes 196616 | tf_op jit(solution)/shard_map/ppermute | solution.py:33
  175.9 6.3 %collective-permute-start.3 = (f32[4,20,2,128]{3,0,2,1:T(4,128)S(1)}, f32[4,20,2,128]{3,0,2,1:T(4,128)S(1)}, u32[]{:S(2)}, u32[]{:S(2)}) collective-permute-start(f32[4,20,2,128]{3,0,2,1:T(4,128)S(1)} %copy.211), channel_id=1, source_target_pairs={{1,0},{2,1},{3,2},{5,4},{6,5},{7,6},{9,8},{10,9},{11,10},{13,12},{... | collective-permute-start | bytes 245768 | tf_op jit(solution)/shard_map/ppermute | solution.py:33
  177.2 5.5 %collective-permute-start.2 = (f32[4,20,2,128]{3,0,2,1:T(4,128)S(1)}, f32[4,20,2,128]{3,0,2,1:T(4,128)S(1)}, u32[]{:S(2)}, u32[]{:S(2)}) collective-permute-start(f32[4,20,2,128]{3,0,2,1:T(4,128)S(1)} %copy.210), channel_id=1, source_target_pairs={{0,1},{1,2},{2,3},{4,5},{5,6},{6,7},{8,9},{9,10},{10,11},{12,13},{... | collective-permute-start | bytes 245768 | tf_op jit(solution)/shard_map/ppermute | solution.py:30
  217.6 49.3 %collective-permute-start.4 = (f32[4,2,16,128]{3,2,1,0:T(8,128)S(1)}, f32[4,2,16,128]{3,2,1,0:T(8,128)S(1)}, u32[]{:S(2)}, u32[]{:S(2)}) collective-permute-start(f32[4,2,16,128]{3,2,1,0:T(8,128)S(1)} %get-tuple-element.36), channel_id=1, source_target_pairs={{0,4},{4,8},{8,12},{12,16},{16,20},{20,24},{24,28},{28,32},{32,36}... | collective-permute-start | bytes 196616 | tf_op jit(solution)/shard_map/ppermute | solution.py:30
  235.7 31.2 %collective-permute-start.5 = (f32[4,2,16,128]{3,2,1,0:T(8,128)S(1)}, f32[4,2,16,128]{3,2,1,0:T(8,128)S(1)}, u32[]{:S(2)}, u32[]{:S(2)}) collective-permute-start(f32[4,2,16,128]{3,2,1,0:T(8,128)S(1)} %get-tuple-element.37), channel_id=1, source_target_pairs={{4,0},{8,4},{12,8},{16,12},{20,16},{24,20},{28,24},{32,28},{36,32}... | collective-permute-start | bytes 196616 | tf_op jit(solution)/shard_map/ppermute | solution.py:33
  267.1 6.9 %collective-permute-start.7 = (f32[4,20,2,128]{3,0,2,1:T(4,128)S(1)}, f32[4,20,2,128]{3,0,2,1:T(4,128)S(1)}, u32[]{:S(2)}, u32[]{:S(2)}) collective-permute-start(f32[4,20,2,128]{3,0,2,1:T(4,128)S(1)} %copy.213), channel_id=1, source_target_pairs={{1,0},{2,1},{3,2},{5,4},{6,5},{7,6},{9,8},{10,9},{11,10},{13,12},{... | collective-permute-start | bytes 245768 | tf_op jit(solution)/shard_map/ppermute | solution.py:33
  268.4 6.1 %collective-permute-start.6 = (f32[4,20,2,128]{3,0,2,1:T(4,128)S(1)}, f32[4,20,2,128]{3,0,2,1:T(4,128)S(1)}, u32[]{:S(2)}, u32[]{:S(2)}) collective-permute-start(f32[4,20,2,128]{3,0,2,1:T(4,128)S(1)} %copy.212), channel_id=1, source_target_pairs={{0,1},{1,2},{2,3},{4,5},{5,6},{6,7},{8,9},{9,10},{10,11},{12,13},{... | collective-permute-start | bytes 245768 | tf_op jit(solution)/shard_map/ppermute | solution.py:30
  468.3 10.2 %copy-start.4 = (s32[192]{0:T(256)S(1)}, s32[192]{0:T(256)}, u32[]{:S(2)}) copy-start(s32[192]{0:T(256)} %copy-done.3) | copy-start | bytes 2308

commit v8 on v7

--- a/solution.py
+++ b/solution.py
@@ -105,7 +105,7 @@
             total = total + weight * shifted(mj, step)
         return [total]
 
-    pair_loop(first_ref, second_ref, count_ref, near_ref.shape[0] - 1, contribution, out_ref, 32)
+    pair_loop(first_ref, second_ref, count_ref, near_ref.shape[0] - 1, contribution, out_ref, 64)
 
 
 def force_kernel(first_ref, second_ref, count_ref, own_ref, near_ref, out_ref):
@@ -136,7 +136,7 @@
             acc_z = acc_z + pair_coef * dz
         return [acc_x, acc_y, acc_z]
 
-    pair_loop(first_ref, second_ref, count_ref, near_ref.shape[0] - 1, contribution, out_ref, 32)
+    pair_loop(first_ref, second_ref, count_ref, near_ref.shape[0] - 1, contribution, out_ref, 64)
 
 
 def pair_pass(kernel, first_ids, second_ids, pair_count, own_rows, near_rows, out_depth):

time: 487 us -> 500 us (1.027)
  the two profiles are of different devices: /device:TPU:1 before, /device:TPU:9 now
where the time goes in v8:
time: 500 us; the launch traced here: 492 us
  local copies, waits for them, and re-layouts  258 us (52%)
  blocking collectives  58.5 us (12%)
  other arithmetic  50.2 us (10%)
  starting transfers between devices  46.9 us (9%)
  Pallas kernels  30.6 us (6%)
  matrix products  29.1 us (6%)
  waiting for transfers between devices  18 us (4%)
    all_to_all x1, blocking collectives, local(): lax.all_to_all(reply, 'gx', split_axis=1, concat_axis=1, tiled=True)  58.5 us
    gather x2, local copies, waits for them, and re-layouts, local(): jnp.take(results, jnp.minimum(arrived_slot, slots_all - 1), axis=1)  52 us
    reshape x4, local copies, waits for them, and re-layouts, expand_cells(): return wide.reshape(pencil_count, depth, CAP, NZ * CAP)  41 us
    scatter x1, local copies, waits for them, and re-layouts, local(): own_grid = jnp.zeros((7, slots_all), jnp.float32).at[:, arrived_slot].set...  37.8 us
    pallas_call x2, Pallas kernels, pair_pass(): pl.pallas_call(kernel, out_shape=jax.ShapeDtypeStruct(out_shape, jnp.floa...  30.6 us
    ppermute x4, starting transfers between devices, extended(): lax.ppermute(lax.slice_in_dim(block, block.shape[dim] - width, None, axis...  26.9 us
    slice x2, local copies, waits for them, and re-layouts, local(): own_grid[3:6]  22.4 us
    dot_general x1, matrix products, local(): outgoing = jnp.einsum('fok,okw->fow', windows, shift_map, precision=HIGHEST)  18.2 us
  transfers between devices with their start and end apart: 9, of which 3 were waited for; matrix products, arithmetic and copies ran while one was open for 13% of the time, Pallas kernels for 0%

profile of v8, /device:TPU:9, one launch (start us, length us, event | category | flops | bytes accessed | tf_op | source)
XLA Modules:
  0.0 492.0 jit_solution(2356233740104270538)
XLA Ops:
  3.7 18.2 %fusion.11 = f32[8,64,192]{2,0,1:T(8,128)S(1)} fusion(s32[64,192]{1,0:T(8,128)S(1)} %iota_add_fusion, pred[64,192]{1,0:T(8,128)(4,1)S(1)} %iota_compare_fusion.3, f32[8,64,384]{2,1,0:T(8,128)S(1)} %reshape.381), kind=kOutput, calls=%fused_computation.21 | convolution fusion | flops 462422016 | bytes 1241088 | tf_op jit(solution)/shard_map/fok,okw->fow/dot_general | solution.py:213
  22.9 12.2 %all-to-all-start = ((f32[8,64,192]{2,0,1:T(8,128)}), f32[8,64,192]{2,0,1:T(8,128)S(1)}, u32[]{:S(2)}, u32[]{:S(2)}) async-start(f32[8,64,192]{2,0,1:T(8,128)} %pad_maximum_fusion.3), calls=%async_computation | async-start | bytes 1048576 | tf_op jit(solution)/shard_map/all_to_all | solution.py:216
  36.5 16.2 %all-to-all-done = f32[8,64,192]{2,0,1:T(8,128)S(1)} async-done(((f32[8,64,192]{2,0,1:T(8,128)}), f32[8,64,192]{2,0,1:T(8,128)S(1)}, u32[]{:S(2)}, u32[]{:S(2)}) %all-to-all-start) | async-done | bytes 393248 | tf_op jit(solution)/shard_map/all_to_all | solution.py:216
  53.7 4.0 copy.173
  57.6 37.8 %scatter_custom_fusion = f32[7,32768]{0,1:T(8,128)} fusion(s32[12288]{0:T(1024)S(1)} %bitcast.102, f32[12288,7]{1,0:T(8,128)} %copy.173, f32[]{:T(128)} %constant.87.clone.1), kind=kCustom, calls=%fused_computation.15 | custom fusion | bytes 918016 | tf_op jit(solution)/shard_map/scatter | solution.py:221
  95.5 12.7 %slice_reduce_fusion = f32[32768]{0:T(1024)S(1)} fusion(f32[7,32768]{0,1:T(8,128)} %scatter_custom_fusion), kind=kLoop, calls=%fused_computation.7 | loop fusion | bytes 262144 | tf_op jit(solution)/shard_map/slice | solution.py:225
  108.2 9.9 %fusion.35 = (pred[32768]{0:T(1024)(128)(4,1)S(1)}, pred[1,32768]{0,1:T(8,128)(4,1)}) fusion(f32[7,32768]{0,1:T(8,128)S(1)} %copy-done), kind=kLoop, calls=%fused_computation.97 | loop fusion | flops 32768 | bytes 196608 | tf_op jit(solution)/shard_map/gt | solution.py:165
  118.2 12.4 %fusion.36 = (f32[3,32768]{0,1:T(8,128)}, f32[3,32768]{0,1:T(8,128)}) fusion(f32[7,32768]{0,1:T(8,128)S(1)} %copy-done), kind=kLoop, calls=%fused_computation.98 | loop fusion | bytes 1572864 | tf_op jit(solution)/shard_map/slice | solution.py:241
  130.6 10.0 %copy.177 = f32[3,16,16,128]{3,2,1,0:T(8,128)S(1)} copy(f32[3,16,16,128]{0,3,2,1:T(8,128)} %bitcast.80) | data formatting | bytes 786432 | tf_op jit(solution)/shard_map/slice | solution.py:230
  145.9 9.4 %copy.186 = f32[6,256,128]{2,0,1:T(8,128)S(1)} copy(f32[6,256,128]{0,2,1:T(8,128)} %bitcast.79) | data formatting | bytes 1572864 | tf_op jit(solution)/shard_map/slice | solution.py:254
  155.4 10.0 %copy.188 = f32[3,16,16,128]{3,2,1,0:T(8,128)S(1)} copy(f32[3,16,16,128]{0,3,2,1:T(8,128)} %bitcast.83) | data formatting | bytes 786432 | tf_op jit(solution)/shard_map/slice | solution.py:241
  165.4 9.4 %copy.176 = f32[3,256,128]{2,0,1:T(4,128)S(1)} copy(f32[3,256,128]{0,2,1:T(8,128)} %bitcast.81) | data formatting | bytes 786432 | tf_op jit(solution)/shard_map/slice | solution.py:226
  182.5 4.3 copy.182
  186.8 5.1 %reshape_reshape.2 = f32[4,400,16,8]{1,3,2,0:T(8,128)} reshape(f32[4,20,20,128]{2,1,3,0:T(8,128)} %copy.182) | data formatting | bytes 1638400 | tf_op jit(solution)/shard_map/reshape;reshape | solution.py:53
  193.7 4.4 broadcast_bitcast_fusion.1
  198.1 9.9 %copy.184.near_ref = f32[400,4,8,128]{3,2,1,0:T(8,128)} copy(f32[400,4,8,128]{0,3,2,1:T(8,128)} %broadcast_bitcast_fusion.1) | data formatting | bytes 13107200 | tf_op jit(solution)/shard_map/reshape | solution.py:55
  208.0 18.4 %shard_map.37 = f32[256,1,8,128]{3,2,1,0:T(8,128)} custom-call(s32[6400]{0:T(1024)} %get-tuple-element.18.first_ref, s32[6400]{0:T(1024)} %copy-done.1, s32[1]{0:T(128)} %bitcast.7.count_ref, f32[256,8,128]{2,1,0:T(8,128)} %pad_bitcast_fusion.own_ref, f32[400,4,8,128]{3,2,1,0:T(8,128)} %copy.184.near_ref), custom_call_target="tpu_custom_call" | custom-call | tf_op jit(solution)/shard_map/pallas_call | solution.py:146
  227.9 17.0 %collective-permute-start.4 = (f32[4,2,16,128]{3,2,1,0:T(8,128)S(1)}, f32[4,2,16,128]{3,2,1,0:T(8,128)S(1)}, u32[]{:S(2)}, u32[]{:S(2)}) collective-permute-start(f32[4,2,16,128]{3,2,1,0:T(8,128)S(1)} %get-tuple-element.36), channel_id=1, source_target_pairs={{0,4},{4,8},{8,12},{12,16},{16,20},{20,24},{24,28},{28,32},{32,36}... | collective-permute-start | bytes 196616 | tf_op jit(solution)/shard_map/ppermute | solution.py:30
  246.8 8.3 %copy.201 = f32[1,32768]{0,1:T(8,128)} copy(f32[1,32768]{1,0:T(1,128)S(1)} %bitcast.94) | data formatting | bytes 262144 | tf_op jit(solution)/shard_map/reduce_sum | solution.py:239
  255.5 12.4 %broadcast_select_fusion = f32[1,32768]{0,1:T(8,128)} fusion(pred[1,32768]{0,1:T(8,128)(4,1)} %get-tuple-element.24, f32[1,32768]{0,1:T(8,128)} %copy.201), kind=kLoop, calls=%fused_computation.14 | loop fusion | flops 32768 | bytes 294912 | tf_op jit(solution)/shard_map/jit(_where)/select_n | solution.py:165
  269.2 3.4 copy.187
  272.6 3.5 concatenate.59
  290.0 3.5 concatenate.63
  299.7 8.8 %broadcast_bitcast_fusion = f32[400,9,8,128]{0,3,2,1:T(8,128)} fusion(f32[400,9,8,16]{0,3,2,1:T(8,128)S(1)} %copy.197), kind=kLoop, calls=%fused_computation.9 | loop fusion | bytes 16588800 | tf_op jit(solution)/shard_map/reshape | solution.py:55
  308.5 17.8 %copy.198.near_ref = f32[400,9,8,128]{3,2,1,0:T(8,128)} copy(f32[400,9,8,128]{0,3,2,1:T(8,128)} %broadcast_bitcast_fusion) | data formatting | bytes 29491200 | tf_op jit(solution)/shard_map/reshape | solution.py:55
  326.4 12.2 %shard_map.38 = f32[256,3,8,128]{3,2,1,0:T(8,128)} custom-call(s32[6400]{0:T(1024)} %get-tuple-element.18.first_ref, s32[6400]{0:T(1024)} %copy-done.1, s32[1]{0:T(128)} %bitcast.7.count_ref, f32[256,8,128]{2,1,0:T(8,128)} %maximum_bitcast_fusion.own_ref, f32[400,9,8,128]{3,2,1,0:T(8,128)} %copy.198.near_ref), custom_call_target="tpu_custom_call" | custom-call | tf_op jit(solution)/shard_map/pallas_call | solution.py:146
  344.5 8.2 %copy.200 = f32[3,256,128]{0,2,1:T(8,128)} copy(f32[3,256,128]{2,0,1:T(4,128)S(1)} %scatter-add.4) | data formatting | bytes 786432 | tf_op jit(solution)/shard_map/scatter-add | solution.py:258
  352.7 17.3 %pad_maximum_fusion = f32[4,32768]{0,1:T(8,128)} fusion(f32[1,32768]{0,1:T(8,128)} %broadcast_select_fusion, f32[3,32768]{0,1:T(8,128)} %bitcast.82), kind=kLoop, calls=%fused_computation.6 | loop fusion | flops 131072 | bytes 1048576 | tf_op jit(solution)/shard_map/concatenate | solution.py:259
  370.0 47.1 %gather_fusion = f32[12288,4]{1,0:T(8,128)} fusion(f32[4,32768]{0,1:T(8,128)} %pad_maximum_fusion, s32[12288]{0:T(1024)S(1)} %broadcast_clamp_fusion), kind=kCustom, calls=%fused_computation | custom fusion | bytes 442368 | tf_op jit(solution)/shard_map/jit(_take)/gather | solution.py:260
  417.1 4.9 %copy.202 = f32[4,64,192]{2,0,1:T(4,128)S(1)} copy(f32[4,64,192]{0,2,1:T(8,128)} %bitcast.84) | data formatting | bytes 393216 | tf_op jit(solution)/shard_map/jit(_take)/gather | solution.py:260
  422.1 58.5 %all_to_all.10 = f32[4,64,192]{2,0,1:T(4,128)S(1)} all-to-all(f32[4,64,192]{2,0,1:T(4,128)S(1)} %broadcast_select_fusion.1), channel_id=1, replica_groups=mesh['gx'=64,'gy'=4] {'gx'}, dimensions={1} | all-to-all | bytes 393216 | tf_op jit(solution)/shard_map/all_to_all | solution.py:263
  480.6 10.1 %fusion.14 = f32[4,64,384]{2,0,1:T(4,128)S(1)} fusion(s32[64,192]{1,0:T(8,128)S(1)} %iota_add_fusion, pred[64,192]{1,0:T(8,128)(4,1)S(1)} %iota_compare_fusion.3, f32[4,64,192]{2,0,1:T(4,128)S(1)} %all_to_all.10), kind=kOutput, calls=%fused_computation.22 | convolution fusion | flops 235978752 | bytes 651264 | tf_op jit(solution)/shard_map/fow,okw->fok/dot_general | solution.py:264
  (97 shorter events, 53.8 us)
Async XLA Ops:
  1.8 20.0 %copy-start.3 = (s32[192]{0:T(256)}, s32[192]{0:T(256)S(1)}, u32[]{:S(2)}) copy-start(s32[192]{0:T(256)S(1)} %add.127) | copy-start | bytes 2308
  3.7 31.4 %copy-start.2 = (s32[1,2,6400]{2,1,0:T(2,128)S(1)}, s32[1,2,6400]{2,1,0:T(2,128)}, u32[]{:S(2)}) copy-start(s32[1,2,6400]{2,1,0:T(2,128)} %param.7) | copy-start | bytes 153604
  22.9 29.9 %all-to-all-start = ((f32[8,64,192]{2,0,1:T(8,128)}), f32[8,64,192]{2,0,1:T(8,128)S(1)}, u32[]{:S(2)}, u32[]{:S(2)}) async-start(f32[8,64,192]{2,0,1:T(8,128)} %pad_maximum_fusion.3), calls=%async_computation | async-start | bytes 1048576 | tf_op jit(solution)/shard_map/all_to_all | solution.py:216
  35.8 59.6 %copy-start.1 = (s32[6400]{0:T(1024)}, s32[6400]{0:T(1024)S(1)}, u32[]{:S(2)}) copy-start(s32[6400]{0:T(1024)S(1)} %get-tuple-element.17.second_ref) | copy-start | bytes 76804
  95.5 12.8 %copy-start = (f32[7,32768]{0,1:T(8,128)S(1)}, f32[7,32768]{0,1:T(8,128)}, u32[]{:S(2)}) copy-start(f32[7,32768]{0,1:T(8,128)} %scatter_custom_fusion) | copy-start | bytes 2752516
  140.6 34.3 %collective-permute-start = (f32[4,2,16,128]{3,2,1,0:T(8,128)S(1)}, f32[4,2,16,128]{3,2,1,0:T(8,128)S(1)}, u32[]{:S(2)}, u32[]{:S(2)}) collective-permute-start(f32[4,2,16,128]{3,2,1,0:T(8,128)S(1)} %get-tuple-element.38), channel_id=1, source_target_pairs={{0,4},{4,8},{8,12},{12,16},{16,20},{20,24},{24,28},{28,32},{32,36}... | collective-permute-start | bytes 196616 | tf_op jit(solution)/shard_map/ppermute | solution.py:30
  144.0 30.9 %collective-permute-start.1 = (f32[4,2,16,128]{3,2,1,0:T(8,128)S(1)}, f32[4,2,16,128]{3,2,1,0:T(8,128)S(1)}, u32[]{:S(2)}, u32[]{:S(2)}) collective-permute-start(f32[4,2,16,128]{3,2,1,0:T(8,128)S(1)} %get-tuple-element.39), channel_id=1, source_target_pairs={{4,0},{8,4},{12,8},{16,12},{20,16},{24,20},{28,24},{32,28},{36,32}... | collective-permute-start | bytes 196616 | tf_op jit(solution)/shard_map/ppermute | solution.py:33
  175.0 6.3 %collective-permute-start.3 = (f32[4,20,2,128]{3,0,2,1:T(4,128)S(1)}, f32[4,20,2,128]{3,0,2,1:T(4,128)S(1)}, u32[]{:S(2)}, u32[]{:S(2)}) collective-permute-start(f32[4,20,2,128]{3,0,2,1:T(4,128)S(1)} %copy.211), channel_id=1, source_target_pairs={{1,0},{2,1},{3,2},{5,4},{6,5},{7,6},{9,8},{10,9},{11,10},{13,12},{... | collective-permute-start | bytes 245768 | tf_op jit(solution)/shard_map/ppermute | solution.py:33
  177.1 5.2 %collective-permute-start.2 = (f32[4,20,2,128]{3,0,2,1:T(4,128)S(1)}, f32[4,20,2,128]{3,0,2,1:T(4,128)S(1)}, u32[]{:S(2)}, u32[]{:S(2)}) collective-permute-start(f32[4,20,2,128]{3,0,2,1:T(4,128)S(1)} %copy.210), channel_id=1, source_target_pairs={{0,1},{1,2},{2,3},{4,5},{5,6},{6,7},{8,9},{9,10},{10,11},{12,13},{... | collective-permute-start | bytes 245768 | tf_op jit(solution)/shard_map/ppermute | solution.py:30
  227.9 48.2 %collective-permute-start.4 = (f32[4,2,16,128]{3,2,1,0:T(8,128)S(1)}, f32[4,2,16,128]{3,2,1,0:T(8,128)S(1)}, u32[]{:S(2)}, u32[]{:S(2)}) collective-permute-start(f32[4,2,16,128]{3,2,1,0:T(8,128)S(1)} %get-tuple-element.36), channel_id=1, source_target_pairs={{0,4},{4,8},{8,12},{12,16},{16,20},{20,24},{24,28},{28,32},{32,36}... | collective-permute-start | bytes 196616 | tf_op jit(solution)/shard_map/ppermute | solution.py:30
  244.9 31.2 %collective-permute-start.5 = (f32[4,2,16,128]{3,2,1,0:T(8,128)S(1)}, f32[4,2,16,128]{3,2,1,0:T(8,128)S(1)}, u32[]{:S(2)}, u32[]{:S(2)}) collective-permute-start(f32[4,2,16,128]{3,2,1,0:T(8,128)S(1)} %get-tuple-element.37), channel_id=1, source_target_pairs={{4,0},{8,4},{12,8},{16,12},{20,16},{24,20},{28,24},{32,28},{36,32}... | collective-permute-start | bytes 196616 | tf_op jit(solution)/shard_map/ppermute | solution.py:33
  276.3 6.3 %collective-permute-start.7 = (f32[4,20,2,128]{3,0,2,1:T(4,128)S(1)}, f32[4,20,2,128]{3,0,2,1:T(4,128)S(1)}, u32[]{:S(2)}, u32[]{:S(2)}) collective-permute-start(f32[4,20,2,128]{3,0,2,1:T(4,128)S(1)} %copy.213), channel_id=1, source_target_pairs={{1,0},{2,1},{3,2},{5,4},{6,5},{7,6},{9,8},{10,9},{11,10},{13,12},{... | collective-permute-start | bytes 245768 | tf_op jit(solution)/shard_map/ppermute | solution.py:33
  278.2 5.2 %collective-permute-start.6 = (f32[4,20,2,128]{3,0,2,1:T(4,128)S(1)}, f32[4,20,2,128]{3,0,2,1:T(4,128)S(1)}, u32[]{:S(2)}, u32[]{:S(2)}) collective-permute-start(f32[4,20,2,128]{3,0,2,1:T(4,128)S(1)} %copy.212), channel_id=1, source_target_pairs={{0,1},{1,2},{2,3},{4,5},{5,6},{6,7},{8,9},{9,10},{10,11},{12,13},{... | collective-permute-start | bytes 245768 | tf_op jit(solution)/shard_map/ppermute | solution.py:30
  480.6 10.2 %copy-start.4 = (s32[192]{0:T(256)S(1)}, s32[192]{0:T(256)}, u32[]{:S(2)}) copy-start(s32[192]{0:T(256)} %copy-done.3) | copy-start | bytes 2308
